TPU v7x, 32 devices: a whole 2x2x4 slice. The times are simulated.
32 devices in a mesh: expert: 4 (over y, core), dp: 8 (over z, x).
Axes of the slice: x: 2, y: 2, z: 4, core: 2. Of those that a mesh axis runs over, the one named last changes fastest.
Arguments:
- tokens: bfloat16 [4096, 4096], P(('expert', 'dp')), may hold values from -6 to 6
- gates: float32 [4096, 8], P(('expert', 'dp')), may hold values from 0.05 to 1
- routes: int32 [4096, 8], P(('expert', 'dp')), may hold values from 0 to 63, all different within a row; in each aligned block of 128 rows (0 to 127, 128 to 255, ...) at most 32 rows name the same one
- doc_ids: int32 [4096], P(('expert', 'dp')), may hold values from 0 to 1
- hidden_grad: bfloat16 [64, 1024, 1536], P('expert', 'dp'), may hold values from -6 to 6
- proj_in: bfloat16 [4096, 64], replicated, may hold values from -0.09375 to 0.09375
- proj_out: bfloat16 [64, 1536, 64], P('expert'), may hold values from -0.15625 to 0.15625
- val_features: bfloat16 [32, 64, 4096], P('dp', 'expert'), may hold values from -6 to 6
Outputs:
- scores: float32 [16, 32], P('dp')
Inputs may be any that keep to these rules, and one draw needn't show every extreme that they name: Each row names 8 different experts; among the rows of one device no expert is named by more than 32 routes, and in every draw some expert by exactly 32.
All inputs are finite; a program needn't handle non-finite values.
Results may differ from a plain program's by a relative error of at most 0.0049.
Values may be sent and summed in bfloat16 or wider, within the bound.
No kernel may reach another device: no remote copies, remote signals or barrier semaphores. Data moves between devices by JAX's collectives and lax.ppermute only.
A program may use at most 64 MiB of HBM per device.

v0:
```python
import jax
import jax.numpy as jnp
from jax import lax
from jax.sharding import PartitionSpec as P

DOC_GRP = 2


def body(tokens, gates, routes, doc_ids, hidden_grad, proj_in, proj_out, val_features):
    tok_count, top_count = routes.shape
    rank = proj_in.shape[1]
    exp_local = proj_out.shape[0]
    groups = lax.axis_size("expert")
    experts = exp_local * groups
    capacity = hidden_grad.shape[1] // groups
    act = jnp.dot(tokens, proj_in, preferred_element_type=jnp.float32)
    sent = (gates[:, :, None] * act[:, None, :]).astype(jnp.bfloat16).reshape(-1, rank)
    flat_routes = routes.reshape(-1)
    onehot = (flat_routes[:, None] == jnp.arange(experts, dtype=jnp.int32)[None, :]).astype(
        jnp.int32
    )
    prior = jnp.cumsum(onehot, axis=0) - onehot
    slot = jnp.sum(prior * onehot, axis=1)
    index = flat_routes * capacity + slot
    buffer = jnp.zeros((experts * capacity, rank), jnp.bfloat16).at[index].set(sent)
    buffer = buffer.reshape(experts, capacity * rank)
    owners = (
        jnp.full((experts * capacity,), DOC_GRP, jnp.int32)
        .at[index]
        .set(jnp.repeat(doc_ids, top_count))
    )
    owners = owners.reshape(experts, capacity)
    arrived, arrived_docs = (
        lax.all_to_all(buffer, "expert", split_axis=0, concat_axis=1, tiled=True),
        lax.all_to_all(owners, "expert", split_axis=0, concat_axis=1, tiled=True),
    )
    lowered = jnp.einsum(
        "erf,efk->erk", hidden_grad, proj_out, preferred_element_type=jnp.float32
    ).astype(jnp.bfloat16)
    slot_rows = lowered.shape[1]
    arrived = arrived.reshape(exp_local, slot_rows, rank)
    member = (
        arrived_docs[:, :, None] == jnp.arange(DOC_GRP, dtype=jnp.int32)[None, None, :]
    ).astype(jnp.bfloat16)
    spread = (member[:, :, :, None] * arrived[:, :, None, :]).reshape(
        exp_local, slot_rows, DOC_GRP * rank
    )
    features = jnp.einsum("erm,erb->emb", spread, lowered, preferred_element_type=jnp.float32)
    features = features.reshape(exp_local, DOC_GRP, rank * rank).astype(jnp.bfloat16)
    scale = 1.0 / jnp.sqrt(jnp.float32(experts * rank * rank))
    part = jnp.einsum(
        "edk,vek->dv",
        features,
        lax.all_gather(val_features, "dp", axis=0, tiled=True),
        preferred_element_type=jnp.float32,
    )
    summed = lax.psum(part, "expert")
    return summed * scale


def solution(mesh):
    in_specs = (
        P(("expert", "dp"), None),
        P(("expert", "dp"), None),
        P(("expert", "dp"), None),
        P(("expert", "dp")),
        P("expert", "dp", None),
        P(),
        P("expert", None, None),
        P("dp", "expert", None),
    )
    out_specs = P("dp", None)
    return jax.shard_map(body, mesh=mesh, in_specs=in_specs, out_specs=out_specs, check_vma=False)
```

profile of v0, /device:TPU:0, one launch (start us, length us, event | category | flops | bytes accessed | tf_op | source)
XLA Modules:
  0.0 105.2 jit_solution(4999100933322094039)
XLA Ops:
  6.5 0.0 copy-start
  6.5 0.0 copy-start.2
  6.5 0.0 all-gather.2.cloned.1.call-start
  6.5 0.7 all-gather.2.cloned.1.call-update
  7.3 0.9 copy.37
  8.2 0.1 eq.48
  8.3 0.1 eq.44
  8.4 0.7 fusion.14
  9.1 30.8 %reduce-window.6 = s32[64,8,128]{2,1,0:T(8,128)S(1)} reduce-window(s32[64,8,128]{2,1,0:T(8,128)} %fusion.14, s32[]{:T(128)} %constant.3.clone.1), window={size=1x1x128 pad=0_0x0_0x127_0}, to_apply=%region_0.0 | reduce-window | flops 8323072 | bytes 524292 | tf_op jit(solution)/shard_map/reduce-window
  39.9 0.8 slice.8
  40.7 1.1 %copy.39 = s32[64,8,1]{0,1,2:T(8,128)S(1)} copy(s32[64,8,1]{2,1,0:T(8,128)} %slice.8) | data formatting | bytes 4096 | tf_op jit(solution)/shard_map/slice
  41.8 0.1 copy.40
  41.9 0.7 broadcast_multiply_fusion.1
  42.6 0.1 copy.36
  42.7 0.1 mul.64
  42.8 0.7 broadcast_in_dim.7
  43.5 0.1 reshape.85
  43.6 0.1 broadcast_add_fusion
  43.8 0.1 fusion.10
  43.9 4.3 %scatter_custom_fusion = s32[2048]{0:T(1024)S(1)} fusion(s32[1024]{0:T(1024)S(1)} %bitcast.42, s32[1024]{0:T(1024)S(1)} %reshape.85, s32[]{:T(128)} %constant.6.clone.1), kind=kCustom, calls=%fused_computation.24 | custom fusion | bytes 8196 | tf_op jit(solution)/shard_map/scatter | solution.py:30
  48.2 0.1 all_to_all.24
  48.3 0.7 reshape.102
  48.9 4.3 %all-to-all-start = ((s32[4,1,512]{2,1,0:T(1,128)}), s32[4,1,512]{2,1,0:T(1,128)S(1)}, u32[]{:S(2)}, u32[]{:S(2)}) async-start(s32[4,1,512]{2,1,0:T(1,128)} %reshape.102), calls=%async_computation | async-start | bytes 16384 | tf_op jit(solution)/shard_map/all_to_all | solution.py:35
  53.2 1.8 %fusion.17 = f32[128,64]{1,0:T(8,128)S(1)} fusion(bf16[128,4096]{1,0:T(8,128)(2,1)} %param.8, bf16[4096,64]{0,1:T(8,128)(2,1)} %param.13), kind=kOutput, calls=%fused_computation.28 | convolution fusion | flops 67108864 | bytes 1605632 | tf_op jit(solution)/shard_map/dot_general | solution.py:16
  55.0 0.0 copy-done.2
  55.0 0.1 copy.42
  55.1 0.1 mul.67
  55.2 4.5 %scatter_custom_fusion.1 = bf16[2048,64]{1,0:T(8,128)(2,1)} fusion(s32[1024]{0:T(1024)S(1)} %bitcast.43, f32[128,64]{1,0:T(8,128)S(1)} %fusion.17, f32[1024]{0:T(1024)S(1)} %mul.67, bf16[]{:T(256)} %constant.5.clone.1), kind=kCustom, calls=%fused_computation.9 | custom fusion | flops 131072 | bytes 331778 | tf_op jit(solution)/shard_map/scatter | solution.py:25
  59.7 2.2 %all_to_all.27 = bf16[4,16,2048]{2,1,0:T(8,128)(2,1)} reshape(bf16[2048,64]{1,0:T(8,128)(2,1)} %scatter_custom_fusion.1) | data formatting | bytes 524288 | tf_op jit(solution)/shard_map/all_to_all | solution.py:34
  61.9 0.0 all-to-all-done
  61.9 3.6 %all-to-all-start.1 = ((bf16[4,16,2048]{2,1,0:T(8,128)(2,1)}), bf16[4,16,2048]{2,1,0:T(8,128)(2,1)S(1)}, u32[]{:S(2)}, u32[]{:S(2)}) async-start(bf16[4,16,2048]{2,1,0:T(8,128)(2,1)} %all_to_all.27), calls=%async_computation.1 | async-start | bytes 524288 | tf_op jit(solution)/shard_map/all_to_all | solution.py:34
  65.5 0.5 broadcast.61
  66.0 0.7 reduce
  66.7 0.1 reshape.103
  66.8 0.1 eq.52
  66.9 4.6 %all-to-all-done.1 = bf16[4,16,2048]{2,1,0:T(8,128)(2,1)S(1)} async-done(((bf16[4,16,2048]{2,1,0:T(8,128)(2,1)}), bf16[4,16,2048]{2,1,0:T(8,128)(2,1)S(1)}, u32[]{:S(2)}, u32[]{:S(2)}) %all-to-all-start.1) | async-done | bytes 262176 | tf_op jit(solution)/shard_map/all_to_all | solution.py:34
  71.5 0.0 copy-start.1
  71.5 0.7 copy-done.1
  72.2 1.2 %copy.44 = bf16[16,4,2048]{2,1,0:T(4,128)(2,1)S(1)} copy(bf16[16,4,2048]{2,0,1:T(8,128)(2,1)} %bitcast.37) | data formatting | bytes 524288 | tf_op jit(solution)/shard_map/all_to_all | solution.py:34
  73.3 1.2 %mul.72 = bf16[16,128,64]{2,1,0:T(8,128)(2,1)} reshape(bf16[16,4,2048]{2,1,0:T(4,128)(2,1)S(1)} %copy.44) | data formatting | bytes 524288 | tf_op jit(solution)/shard_map/mul | solution.py:45
  74.5 1.2 %copy.45 = bf16[16,128,64]{1,2,0:T(8,128)(2,1)S(1)} copy(bf16[16,128,64]{2,1,0:T(8,128)(2,1)} %mul.72) | data formatting | bytes 524288 | tf_op jit(solution)/shard_map/mul | solution.py:45
  75.8 0.8 broadcast_multiply_fusion
  76.6 0.0 copy-done
  76.6 5.5 %convolution_convert_fusion = bf16[16,128,64]{1,2,0:T(8,128)(2,1)S(1)} fusion(bf16[16,128,128]{1,2,0:T(8,128)(2,1)} %bitcast.36, bf16[16,128,1536]{2,1,0:T(8,128)(2,1)} %param.12, bf16[16,1536,64]{1,2,0:T(8,128)(2,1)S(1)} %copy-done), kind=kOutput, calls=%fused_computation.4 | convolution fusion | flops 436469760 | bytes 10223616 | tf_op jit(solution)/shard_map/erm,erb->emb/dot_general | solution.py:48
  82.2 1.0 copy.47
  83.2 1.4 %convert_element_type.33 = bf16[16,2,4096]{2,1,0:T(2,128)(2,1)S(1)} reshape(bf16[16,128,64]{2,1,0:T(8,128)(2,1)} %copy.47) | data formatting | bytes 524288 | tf_op jit(solution)/shard_map/convert_element_type | solution.py:49
  84.6 0.4 all-gather.2.cloned.1.call-done
  85.0 7.1 %fusion.2 = f32[2,32]{1,0:T(2,128)S(1)} fusion(bf16[16,2,4096]{2,1,0:T(2,128)(2,1)S(1)} %convert_element_type.33, bf16[32,16,4096]{2,1,0:T(8,128)(2,1)} %all-gather.2.cloned.1.call-done), kind=kOutput, calls=%fused_computation.6 | convolution fusion | flops 8388608 | bytes 4456704 | tf_op jit(solution)/shard_map/edk,vek->dv/dot_general | solution.py:51
  92.1 5.6 %psum.7 = f32[2,32]{1,0:T(2,128)S(1)} all-reduce(f32[2,32]{1,0:T(2,128)S(1)} %fusion.2), channel_id=1, replica_groups=mesh['expert'=4,'dp'=8] {'expert'}, use_global_device_ids=true, to_apply=%region_5.6 | all-reduce | flops 64 | bytes 512 | tf_op jit(solution)/shard_map/psum | solution.py:57
  97.8 0.6 broadcast_multiply_fusion.2
  (5 shorter events, 0.1 us)
Async XLA Ops:
  6.5 70.1 %copy-start = (bf16[16,1536,64]{1,2,0:T(8,128)(2,1)S(1)}, bf16[16,1536,64]{1,2,0:T(8,128)(2,1)}, u32[]{:S(2)}) copy-start(bf16[16,1536,64]{1,2,0:T(8,128)(2,1)} %param.14) | copy-start | bytes 9437188
  6.5 48.5 %copy-start.2 = (f32[128,8]{0,1:T(8,128)S(1)}, f32[128,8]{0,1:T(8,128)}, u32[]{:S(2)}) copy-start(f32[128,8]{0,1:T(8,128)} %param.9) | copy-start | bytes 12292
  6.5 78.5 %all-gather.2.cloned.1.call-start = ((), (), s32[]{:S(2)}) async-start(), calls=%async_computation.2 | async-start | bytes 4718592 | tf_op jit(solution)/shard_map/all_gather | solution.py:54
  48.9 12.9 %all-to-all-start = ((s32[4,1,512]{2,1,0:T(1,128)}), s32[4,1,512]{2,1,0:T(1,128)S(1)}, u32[]{:S(2)}, u32[]{:S(2)}) async-start(s32[4,1,512]{2,1,0:T(1,128)} %reshape.102), calls=%async_computation | async-start | bytes 16384 | tf_op jit(solution)/shard_map/all_to_all | solution.py:35
  61.9 9.6 %all-to-all-start.1 = ((bf16[4,16,2048]{2,1,0:T(8,128)(2,1)}), bf16[4,16,2048]{2,1,0:T(8,128)(2,1)S(1)}, u32[]{:S(2)}, u32[]{:S(2)}) async-start(bf16[4,16,2048]{2,1,0:T(8,128)(2,1)} %all_to_all.27), calls=%async_computation.1 | async-start | bytes 524288 | tf_op jit(solution)/shard_map/all_to_all | solution.py:34
  71.5 0.7 copy-start.1
Sparse Core Ops, SparseCore 0:
  9.5 75.5 all-gather.1
where the time goes:
time: 107 us; the launch traced here: 105 us
  other arithmetic  39 us (36%)
  local copies, waits for them, and re-layouts  19 us (18%)
  matrix products  14.4 us (13%)
  between operations  13.5 us (13%)
  starting transfers between devices  7.86 us (7%)
  waiting for transfers between devices  5.71 us (5%)
  blocking collectives  5.64 us (5%)
    another operation x3, other arithmetic  31 us
    dot_general x1, matrix products, body(): jnp.einsum('edk,vek->dv', features, lax.all_gather(val_features, 'dp', ax...  7.1 us
    psum x1, blocking collectives, body(): summed = lax.psum(part, 'expert')  5.64 us
    dot_general x1, matrix products, body(): jnp.einsum('erm,erb->emb', spread, lowered, preferred_element_type=jnp.fl...  5.54 us
    all_to_all x1, waiting for transfers between devices, body(): lax.all_to_all(buffer, 'expert', split_axis=0, concat_axis=1, tiled=True)  4.59 us
    scatter x1, other arithmetic, body(): jnp.zeros((experts * capacity, rank), jnp.bfloat16).at[index].set(sent)  4.48 us
    scatter x1, local copies, waits for them, and re-layouts, body(): owners = jnp.full((experts * capacity,), DOC_GRP, jnp.int32).at[index].se...  4.32 us
    all_to_all x1, starting transfers between devices, body(): lax.all_to_all(owners, 'expert', split_axis=0, concat_axis=1, tiled=True)  4.27 us
  transfers between devices with their start and end apart: 3, of which 2 were waited for; matrix products, arithmetic and copies ran while one was open for 59% of the time, Pallas kernels for 0%

commit v1 on v0

v1 whole, which is shorter than its diff:
```python
import functools

import jax
import jax.numpy as jnp
from jax import lax
from jax.experimental import pallas as pl
from jax.experimental.pallas import tpu as pltpu
from jax.sharding import PartitionSpec as P

DOC_GRP = 2
LANES = 128
F32 = jnp.float32
BF16 = jnp.bfloat16
NT = (((1,), (1,)), ((), ()))
TN = (((0,), (0,)), ((), ()))


def act_kernel(tok_ref, proj_ref, routes_ref, gates_ref, docs_ref, out_ref, acc_ref):
    rank = proj_ref.shape[0]
    top = routes_ref.shape[0]
    half = rank // 2
    step = pl.program_id(0)

    @pl.when(step == 0)
    def _():
        acc_ref[...] = jnp.zeros_like(acc_ref)

    acc_ref[...] += lax.dot_general(proj_ref[...], tok_ref[...], NT, preferred_element_type=F32)

    @pl.when(step == pl.num_programs(0) - 1)
    def _():
        out_ref[0:half, :] = acc_ref[pl.ds(0, half, stride=2), :]
        out_ref[half:rank, :] = acc_ref[pl.ds(1, half, stride=2), :]
        out_ref[rank : rank + top, :] = routes_ref[...].astype(F32)
        out_ref[rank + top : rank + 2 * top, :] = gates_ref[...]
        out_ref[rank + 2 * top :, :] = jnp.broadcast_to(
            docs_ref[...].astype(F32), (out_ref.shape[0] - rank - 2 * top, out_ref.shape[1])
        )


def lowered_kernel(grad_ref, proj_ref, out_ref):
    for e in range(grad_ref.shape[0]):
        low = lax.dot_general(grad_ref[e], proj_ref[e], NT, preferred_element_type=F32)
        out_ref[e] = jnp.concatenate([low, low], axis=1).astype(BF16)


def feature_kernel(groups, rank, top, me_ref, *refs):
    pays, low_ref, out_ref, a_ref, f_ref = refs[:groups], *refs[groups:]
    exp_local, rows, _ = low_ref.shape
    cap = rows // groups
    tok = pays[0].shape[1]
    half = rank // 2
    me = me_ref[0]
    base = (me * exp_local).astype(F32)
    experts = lax.broadcasted_iota(jnp.int32, (exp_local, tok), 0).astype(F32) + base
    before = (
        lax.broadcasted_iota(jnp.int32, (tok, tok), 0)
        < lax.broadcasted_iota(jnp.int32, (tok, tok), 1)
    ).astype(BF16)
    slots = lax.broadcasted_iota(jnp.int32, (cap, tok), 0).astype(F32)
    for k in range(groups):
        pay = pays[k]
        hit = jnp.zeros((exp_local, tok), F32)
        gate = jnp.zeros((exp_local, tok), F32)
        for t in range(top):
            same = pay[rank + t : rank + t + 1, :] == experts
            hit = jnp.where(same, 1.0, hit)
            gate = jnp.where(same, pay[rank + top + t : rank + top + t + 1, :], gate)
        slot = jnp.dot(hit.astype(BF16), before, preferred_element_type=F32)
        slot = jnp.where(hit > 0.0, slot, -1.0)
        doc = pay[rank + 2 * top : rank + 2 * top + 1, :]
        parts = []
        for par in range(2):
            act = pay[par * half : (par + 1) * half, :]
            for d in range(DOC_GRP):
                parts.append(jnp.where(doc == float(d), act, 0.0))
        act = jnp.concatenate(parts, axis=0)
        high = act.astype(BF16)
        low = (act - high.astype(F32)).astype(BF16)
        right = jnp.concatenate([high, low], axis=1)
        picks, scales = [], []
        for e in range(exp_local):
            pick = slot[e : e + 1, :] == slots
            picks.append(jnp.where(pick, 1.0, 0.0).astype(BF16))
            scales.append(
                jnp.sum(jnp.where(pick, gate[e : e + 1, :], 0.0), axis=1, keepdims=True)
            )
        left = jnp.concatenate(picks, axis=0)
        scale = jnp.concatenate(scales, axis=0)
        left = jnp.concatenate([left, left], axis=1)
        sent = lax.dot_general(left, right, NT, preferred_element_type=F32) * scale
        sent = sent.astype(BF16)
        source = pl.multiple_of(lax.bitwise_xor(me, k) * cap, cap)
        for e in range(exp_local):
            a_ref[e, pl.ds(source, cap), :] = sent[e * cap : (e + 1) * cap, :]
    wide = DOC_GRP * half
    lane = lax.broadcasted_iota(jnp.int32, (wide, 2 * rank), 1)
    for e in range(exp_local):
        feat = lax.dot_general(a_ref[e], low_ref[e], TN, preferred_element_type=F32)
        f_ref[pl.ds(e, wide, stride=exp_local), :] = jnp.where(
            lane < rank, feat[:wide], feat[wide:]
        )
    parts, _, chunks, _, _ = out_ref.shape
    size = chunks * exp_local
    for d in range(DOC_GRP):
        for p in range(parts):
            start = (d * half + p * chunks) * exp_local
            out_ref[p, d] = (
                f_ref[start : start + size, :].astype(BF16).reshape(chunks, exp_local, 2 * rank)
            )


def score_kernel(scale, feat_ref, val_ref, out_ref):
    dp, docs, chunks, exp_local, lanes = feat_ref.shape
    vals = val_ref.shape[1]
    left_rows, right_rows = dp * docs * exp_local, dp * vals * exp_local
    total = jnp.zeros((left_rows, right_rows), F32)
    for c in range(chunks):
        left = feat_ref[:, :, c].reshape(left_rows, lanes)
        right = val_ref[:, :, :, c * lanes : (c + 1) * lanes].reshape(right_rows, lanes)
        total += lax.dot_general(left, right, NT, preferred_element_type=F32)
    row = lax.broadcasted_iota(jnp.int32, total.shape, 0) % exp_local
    col = lax.broadcasted_iota(jnp.int32, total.shape, 1) % exp_local
    total = jnp.where(row == col, total, 0.0)
    total = jnp.sum(total.reshape(dp * docs, exp_local, right_rows), axis=1)
    pick = (
        lax.broadcasted_iota(jnp.int32, (right_rows, dp * vals), 0) // exp_local
        == lax.broadcasted_iota(jnp.int32, (right_rows, dp * vals), 1)
    ).astype(F32)
    scores = jnp.dot(
        total, pick, preferred_element_type=F32, precision=lax.Precision.HIGHEST
    ) * scale
    for i in range(out_ref.shape[0] // dp):
        for j in range(dp):
            out_ref[i * dp + j] = scores[j * docs : (j + 1) * docs, :]


def body(tokens, gates, routes, doc_ids, hidden_grad, proj_in, proj_out, val_features):
    tok, width = tokens.shape
    top = routes.shape[1]
    rank = proj_in.shape[1]
    groups = lax.axis_size("expert")
    dp = lax.axis_size("dp")
    exp_local, rows, hidden = hidden_grad.shape
    vals = val_features.shape[0]
    entries = rank * rank
    experts = exp_local * groups
    chunks = entries // LANES // dp

    val_split = val_features.reshape(vals, exp_local, dp, entries // dp).transpose(2, 0, 1, 3)
    val_all = lax.all_to_all(val_split, "dp", split_axis=0, concat_axis=0, tiled=True)

    pay_rows = rank + 2 * top + 8
    steps = 4
    pay = pl.pallas_call(
        act_kernel,
        out_shape=jax.ShapeDtypeStruct((pay_rows, tok), F32),
        grid=(steps,),
        in_specs=[
            pl.BlockSpec((tok, width // steps), lambda s: (0, s)),
            pl.BlockSpec((rank, width // steps), lambda s: (0, s)),
            pl.BlockSpec((top, tok), lambda s: (0, 0)),
            pl.BlockSpec((top, tok), lambda s: (0, 0)),
            pl.BlockSpec((1, tok), lambda s: (0, 0)),
        ],
        out_specs=pl.BlockSpec((pay_rows, tok), lambda s: (0, 0)),
        scratch_shapes=[pltpu.VMEM((rank, tok), F32)],
        cost_estimate=pl.CostEstimate(
            flops=2 * tok * width * rank, bytes_accessed=2 * width * (tok + rank), transcendentals=0
        ),
    )(tokens, proj_in.T, routes.T, gates.T, doc_ids.reshape(1, tok))

    pays = [pay]
    for k in range(1, groups):
        pays.append(lax.ppermute(pay, "expert", [(a, a ^ k) for a in range(groups)]))

    pair = 2
    low = pl.pallas_call(
        lowered_kernel,
        out_shape=jax.ShapeDtypeStruct((exp_local, rows, 2 * rank), BF16),
        grid=(exp_local // pair,),
        in_specs=[
            pl.BlockSpec((pair, rows, hidden), lambda s: (s, 0, 0)),
            pl.BlockSpec((pair, rank, hidden), lambda s: (s, 0, 0)),
        ],
        out_specs=pl.BlockSpec((pair, rows, 2 * rank), lambda s: (s, 0, 0)),
        cost_estimate=pl.CostEstimate(
            flops=2 * exp_local * rows * hidden * rank,
            bytes_accessed=2 * exp_local * hidden * (rows + rank),
            transcendentals=0,
        ),
    )(hidden_grad, proj_out.transpose(0, 2, 1))

    me = lax.axis_index("expert").astype(jnp.int32).reshape(1)
    vmem = pl.BlockSpec(memory_space=pltpu.VMEM)
    feats = pl.pallas_call(
        functools.partial(feature_kernel, groups, rank, top),
        out_shape=jax.ShapeDtypeStruct((dp, DOC_GRP, chunks, exp_local, LANES), BF16),
        in_specs=[pl.BlockSpec(memory_space=pltpu.SMEM)] + [vmem] * (groups + 1),
        out_specs=vmem,
        scratch_shapes=[
            pltpu.VMEM((exp_local, rows, 2 * rank), BF16),
            pltpu.VMEM((DOC_GRP * rank // 2 * exp_local, 2 * rank), F32),
        ],
    )(me, *pays, low)
    feats_all = lax.all_to_all(feats, "dp", split_axis=0, concat_axis=0, tiled=True)

    scale = 1.0 / float(experts * entries) ** 0.5
    part = pl.pallas_call(
        functools.partial(score_kernel, scale),
        out_shape=jax.ShapeDtypeStruct((groups * dp, DOC_GRP, dp * vals), F32),
        in_specs=[vmem, vmem],
        out_specs=vmem,
    )(feats_all, val_all)
    parts = lax.all_to_all(part, ("expert", "dp"), split_axis=0, concat_axis=0, tiled=True)
    return jnp.sum(parts, axis=0)


def solution(mesh):
    in_specs = (
        P(("expert", "dp"), None),
        P(("expert", "dp"), None),
        P(("expert", "dp"), None),
        P(("expert", "dp")),
        P("expert", "dp", None),
        P(),
        P("expert", None, None),
        P("dp", "expert", None),
    )
    out_specs = P("dp", None)
    return jax.shard_map(body, mesh=mesh, in_specs=in_specs, out_specs=out_specs, check_vma=False)
```

time: 107 us -> 65.8 us (0.61); the launches traced: 105 us -> 65.3 us
  other arithmetic: 39 us -> 0.6 us
  blocking collectives: 5.64 us -> 28.4 us
  local copies, waits for them, and re-layouts: 19 us -> 0.68 us
  Pallas kernels: 0 us -> 17.2 us
  matrix products: 14.4 us -> 0 us
  between operations: 13.5 us -> 0.05 us
  waiting for transfers between devices: 5.71 us -> 9.19 us
  starting transfers between devices: 7.86 us -> 9.15 us
    another operation x3 -> x0, other arithmetic: 31 us -> none
    all_to_all x0 -> x2, blocking collectives: none -> 28.4 us  [the longest x1 17.6 us: body(): lax.all_to_all(val_split, 'dp', split_axis=0, concat_axis=0, tiled=True)]
    pallas_call x0 -> x4, Pallas kernels: none -> 17.2 us  [the longest x1 8.17 us: body(): pl.pallas_call(lowered_kernel, out_shape=jax.ShapeDtypeStruct((exp_local,...]
    dot_general x3 -> x0, matrix products: 14.4 us -> none  [the longest x1 7.1 us: body(): jnp.einsum('edk,vek->dv', features, lax.all_gather(val_features, 'dp', ax...]
    psum x1 -> x0, blocking collectives: 5.64 us -> none  [body(): summed = lax.psum(part, 'expert')]
    all_to_all x2 -> x1, waiting for transfers between devices: 4.6 us -> 9.19 us  [body(): lax.all_to_all(feats, 'dp', split_axis=0, concat_axis=0, tiled=True)]
    scatter x1 -> x0, other arithmetic: 4.48 us -> none  [body(): jnp.zeros((experts * capacity, rank), jnp.bfloat16).at[index].set(sent)]
    scatter x1 -> x0, local copies, waits for them, and re-layouts: 4.32 us -> none  [body(): owners = jnp.full((experts * capacity,), DOC_GRP, jnp.int32).at[index].se...]
  transfers between devices with their start and end apart: 3 -> 4, of which waited for: 2 -> 1; matrix products, arithmetic and copies ran while one was open for 59% -> 0% of each run, Pallas kernels for 0% -> 13%
where the time goes in v1:
time: 65.8 us; the launch traced here: 65.3 us
  blocking collectives  28.4 us (43%)
  Pallas kernels  17.2 us (26%)
  waiting for transfers between devices  9.19 us (14%)
  starting transfers between devices  9.15 us (14%)
  local copies, waits for them, and re-layouts  0.68 us (1%)
    all_to_all x1, blocking collectives, body(): lax.all_to_all(val_split, 'dp', split_axis=0, concat_axis=0, tiled=True)  17.6 us
    all_to_all x1, blocking collectives, body(): lax.all_to_all(part, ('expert', 'dp'), split_axis=0, concat_axis=0, tiled...  10.8 us
    all_to_all x1, waiting for transfers between devices, body(): lax.all_to_all(feats, 'dp', split_axis=0, concat_axis=0, tiled=True)  9.19 us
    pallas_call x1, Pallas kernels, body(): pl.pallas_call(lowered_kernel, out_shape=jax.ShapeDtypeStruct((exp_local,...  8.17 us
    all_to_all x1, starting transfers between devices, body(): lax.all_to_all(feats, 'dp', split_axis=0, concat_axis=0, tiled=True)  6.03 us
    pallas_call x1, Pallas kernels, body(): pl.pallas_call(act_kernel, out_shape=jax.ShapeDtypeStruct((pay_rows, tok)...  3.37 us
    pallas_call x1, Pallas kernels, body(): pl.pallas_call(functools.partial(feature_kernel, groups, rank, top), out_...  3.2 us
    ppermute x3, starting transfers between devices, body(): lax.ppermute(pay, 'expert', [(a, a ^ k) for a in range(groups)])  3.12 us
  transfers between devices with their start and end apart: 4, of which 1 were waited for; matrix products, arithmetic and copies ran while one was open for 0% of the time, Pallas kernels for 13%

profile of v1, /device:TPU:0, one launch (start us, length us, event | category | flops | bytes accessed | tf_op | source)
XLA Modules:
  0.0 65.3 jit_solution(18391479728924877779)
XLA Ops:
  0.0 0.0 copy-start.1
  0.0 3.4 %shard_map.82.refs_0_ = f32[88,128]{1,0:T(8,128)} custom-call(bf16[128,4096]{1,0:T(8,128)(2,1)} %tok_ref.1, bf16[64,4096]{1,0:T(8,128)(2,1)} %bitcast.15, s32[8,128]{1,0:T(8,128)} %bitcast.17, f32[8,128]{1,0:T(8,128)} %bitcast.18, s32[1,128]{1,0:T(1,128)} %bitcast.19), custom_call_target="tpu_custom_call" | custom-call | flops 67108864 | bytes 1572864 | tf_op jit(solution)/shard_map/pallas_call | solution.py:155
  3.4 2.4 %collective-permute-start.2 = (f32[88,128]{1,0:T(8,128)}, f32[88,128]{1,0:T(8,128)S(1)}, u32[]{:S(2)}, u32[]{:S(2)}) collective-permute-start(f32[88,128]{1,0:T(8,128)} %shard_map.82.refs_0_), channel_id=1, source_target_pairs={{0,24},{8,16},{16,8},{24,0},{1,25},{9,17},{17,9},{25,1},{2,26},{10... | collective-permute-start | bytes 135176 | tf_op jit(solution)/shard_map/ppermute | solution.py:175
  5.8 0.6 collective-permute-start.1
  6.4 0.1 collective-permute-start
  6.5 8.2 %shard_map.83.refs_4_ = bf16[16,128,128]{2,1,0:T(8,128)(2,1)} custom-call(bf16[16,128,1536]{2,1,0:T(8,128)(2,1)} %grad_ref.1, bf16[16,64,1536]{2,1,0:T(8,128)(2,1)} %bitcast.13), custom_call_target="tpu_custom_call" | custom-call | flops 402653184 | bytes 9437184 | tf_op jit(solution)/shard_map/pallas_call | solution.py:178
  14.7 0.0 collective-permute-done.2.refs_3_
  14.7 0.0 copy-start.2
  14.7 0.0 collective-permute-done.1.refs_2_
  14.7 0.0 copy-start.3
  14.7 0.0 collective-permute-done.refs_1_
  14.7 0.0 copy-start.4
  14.7 0.6 copy-done.2
  15.3 0.0 copy-done.3
  15.3 0.0 copy-done.4
  15.3 3.2 %shard_map.84 = bf16[8,2,4,16,128]{4,3,2,1,0:T(8,128)(2,1)} custom-call(s32[1]{0:T(128)} %bitcast.me_ref, f32[88,128]{1,0:T(8,128)} %shard_map.82.refs_0_, f32[88,128]{1,0:T(8,128)} %copy-done.4, f32[88,128]{1,0:T(8,128)} %copy-done.3, f32[88,128]{1,0:T(8,128)} %copy-done.2, bf16[16,128,128]{2,1,0:T(8,128)(2,1)} %shard_map.83.refs_4_), custom_call_target="tpu_custom_call" | custom-call | tf_op jit(solution)/shard_map/pallas_call | solution.py:196
  18.5 6.0 %all-to-all-start = ((bf16[8,2,4,16,128]{4,3,2,1,0:T(8,128)(2,1)}), bf16[8,2,4,16,128]{4,3,2,1,0:T(8,128)(2,1)S(1)}, u32[]{:S(2)}, u32[]{:S(2)}) async-start(bf16[8,2,4,16,128]{4,3,2,1,0:T(8,128)(2,1)} %shard_map.84), calls=%async_computation | async-start | bytes 524288 | tf_op jit(solution)/shard_map/all_to_all | solution.py:206
  24.6 0.0 copy-done.1
  24.6 0.1 copy.12
  24.6 9.2 %all-to-all-done.feat_ref = bf16[8,2,4,16,128]{4,3,2,1,0:T(8,128)(2,1)S(1)} async-done(((bf16[8,2,4,16,128]{4,3,2,1,0:T(8,128)(2,1)}), bf16[8,2,4,16,128]{4,3,2,1,0:T(8,128)(2,1)S(1)}, u32[]{:S(2)}, u32[]{:S(2)}) %all-to-all-start) | async-done | bytes 262176 | tf_op jit(solution)/shard_map/all_to_all | solution.py:206
  33.8 0.0 copy-start
  33.8 17.6 %all_to_all.15.val_ref = bf16[8,4,16,512]{3,2,1,0:T(8,128)(2,1)} all-to-all(bf16[8,4,16,512]{3,2,1,0:T(8,128)(2,1)S(1)} %bitcast.14), channel_id=1, replica_groups=mesh['expert'=4,'dp'=8] {'dp'}, dimensions={0} | all-to-all | bytes 1048576 | tf_op jit(solution)/shard_map/all_to_all | solution.py:151
  51.4 0.0 copy-done
  51.4 2.4 %shard_map.85 = f32[32,2,32]{2,1,0:T(2,128)} custom-call(bf16[8,2,4,16,128]{4,3,2,1,0:T(8,128)(2,1)} %copy-done, bf16[8,4,16,512]{3,2,1,0:T(8,128)(2,1)} %all_to_all.15.val_ref), custom_call_target="tpu_custom_call" | custom-call | tf_op jit(solution)/shard_map/pallas_call | solution.py:209
  53.8 10.8 %all_to_all.16 = f32[32,2,32]{2,1,0:T(2,128)S(1)} all-to-all(f32[32,2,32]{2,1,0:T(2,128)} %shard_map.85), channel_id=1, replica_groups=mesh['expert'=4,'dp'=8] {'expert','dp'}, dimensions={0} | all-to-all | bytes 16384 | tf_op jit(solution)/shard_map/all_to_all | solution.py:215
  64.7 0.6 reduce_sum.9
Async XLA Ops:
  0.0 24.6 %copy-start.1 = (bf16[4,16,4096]{2,1,0:T(8,128)(2,1)S(1)}, bf16[4,16,4096]{2,1,0:T(8,128)(2,1)}, u32[]{:S(2)}) copy-start(bf16[4,16,4096]{2,1,0:T(8,128)(2,1)} %param.15) | copy-start | bytes 1572868
  3.4 11.3 %collective-permute-start.2 = (f32[88,128]{1,0:T(8,128)}, f32[88,128]{1,0:T(8,128)S(1)}, u32[]{:S(2)}, u32[]{:S(2)}) collective-permute-start(f32[88,128]{1,0:T(8,128)} %shard_map.82.refs_0_), channel_id=1, source_target_pairs={{0,24},{8,16},{16,8},{24,0},{1,25},{9,17},{17,9},{25,1},{2,26},{10... | collective-permute-start | bytes 135176 | tf_op jit(solution)/shard_map/ppermute | solution.py:175
  5.8 8.9 %collective-permute-start.1 = (f32[88,128]{1,0:T(8,128)}, f32[88,128]{1,0:T(8,128)S(1)}, u32[]{:S(2)}, u32[]{:S(2)}) collective-permute-start(f32[88,128]{1,0:T(8,128)} %shard_map.82.refs_0_), channel_id=1, source_target_pairs={{0,16},{8,24},{16,0},{24,8},{1,17},{9,25},{17,1},{25,9},{2,18},{10... | collective-permute-start | bytes 135176 | tf_op jit(solution)/shard_map/ppermute | solution.py:175
  6.4 8.3 %collective-permute-start = (f32[88,128]{1,0:T(8,128)}, f32[88,128]{1,0:T(8,128)S(1)}, u32[]{:S(2)}, u32[]{:S(2)}) collective-permute-start(f32[88,128]{1,0:T(8,128)} %shard_map.82.refs_0_), channel_id=1, source_target_pairs={{0,8},{8,0},{16,24},{24,16},{1,9},{9,1},{17,25},{25,17},{2,10},{10... | collective-permute-start | bytes 135176 | tf_op jit(solution)/shard_map/ppermute | solution.py:175
  14.7 0.6 copy-start.2
  14.7 0.6 copy-start.3
  14.7 0.6 copy-start.4
  18.5 15.3 %all-to-all-start = ((bf16[8,2,4,16,128]{4,3,2,1,0:T(8,128)(2,1)}), bf16[8,2,4,16,128]{4,3,2,1,0:T(8,128)(2,1)S(1)}, u32[]{:S(2)}, u32[]{:S(2)}) async-start(bf16[8,2,4,16,128]{4,3,2,1,0:T(8,128)(2,1)} %shard_map.84), calls=%async_computation | async-start | bytes 524288 | tf_op jit(solution)/shard_map/all_to_all | solution.py:206
  33.8 17.6 %copy-start = (bf16[8,2,4,16,128]{4,3,2,1,0:T(8,128)(2,1)}, bf16[8,2,4,16,128]{4,3,2,1,0:T(8,128)(2,1)S(1)}, u32[]{:S(2)}) copy-start(bf16[8,2,4,16,128]{4,3,2,1,0:T(8,128)(2,1)S(1)} %all-to-all-done.feat_ref) | copy-start | bytes 786436

commit v2 on v1

--- a/solution.py
+++ b/solution.py
@@ -7,6 +7,7 @@
 from jax.experimental.pallas import tpu as pltpu
 from jax.sharding import PartitionSpec as P
 
+
 DOC_GRP = 2
 LANES = 128
 F32 = jnp.float32
@@ -15,31 +16,57 @@
 TN = (((0,), (0,)), ((), ()))
 
 
-def act_kernel(tok_ref, proj_ref, routes_ref, gates_ref, docs_ref, out_ref, acc_ref):
+def act_kernel(tok_hbm, proj_hbm, routes_ref, gates_ref, docs_ref, out_ref, tok_ref, proj_ref, acc_ref, sems):
     rank = proj_ref.shape[0]
     top = routes_ref.shape[0]
     half = rank // 2
-    step = pl.program_id(0)
-
-    @pl.when(step == 0)
-    def _():
-        acc_ref[...] = jnp.zeros_like(acc_ref)
-
-    acc_ref[...] += lax.dot_general(proj_ref[...], tok_ref[...], NT, preferred_element_type=F32)
-
-    @pl.when(step == pl.num_programs(0) - 1)
-    def _():
-        out_ref[0:half, :] = acc_ref[pl.ds(0, half, stride=2), :]
-        out_ref[half:rank, :] = acc_ref[pl.ds(1, half, stride=2), :]
-        out_ref[rank : rank + top, :] = routes_ref[...].astype(F32)
-        out_ref[rank + top : rank + 2 * top, :] = gates_ref[...]
-        out_ref[rank + 2 * top :, :] = jnp.broadcast_to(
-            docs_ref[...].astype(F32), (out_ref.shape[0] - rank - 2 * top, out_ref.shape[1])
-        )
-
-
-def lowered_kernel(grad_ref, proj_ref, out_ref):
-    for e in range(grad_ref.shape[0]):
+    steps = sems.shape[0]
+    width = tok_ref.shape[1] // steps
+    copies = []
+    for s in range(steps):
+        cols = pl.ds(s * width, width)
+        copies.append(
+            (
+                pltpu.make_async_copy(proj_hbm.at[:, cols], proj_ref.at[:, cols], sems.at[s, 0]),
+                pltpu.make_async_copy(tok_hbm.at[:, cols], tok_ref.at[:, cols], sems.at[s, 1]),
+            )
+        )
+    for pair in copies:
+        for copy in pair:
+            copy.start()
+    out_ref[rank : rank + top, :] = routes_ref[...].astype(F32)
+    out_ref[rank + top : rank + 2 * top, :] = gates_ref[...]
+    out_ref[rank + 2 * top :, :] = jnp.broadcast_to(
+        docs_ref[...].astype(F32), (out_ref.shape[0] - rank - 2 * top, out_ref.shape[1])
+    )
+    total = jnp.zeros(acc_ref.shape, F32)
+    for s in range(steps):
+        for copy in copies[s]:
+            copy.wait()
+        cols = slice(s * width, (s + 1) * width)
+        total += lax.dot_general(
+            proj_ref[:, cols], tok_ref[:, cols], NT, preferred_element_type=F32
+        )
+    acc_ref[...] = total
+    out_ref[0:half, :] = acc_ref[pl.ds(0, half, stride=2), :]
+    out_ref[half:rank, :] = acc_ref[pl.ds(1, half, stride=2), :]
+
+
+def lowered_kernel(grad_hbm, proj_hbm, out_ref, grad_ref, proj_ref, sems):
+    copies = []
+    for e in range(sems.shape[0]):
+        copies.append(
+            (
+                pltpu.make_async_copy(proj_hbm.at[e], proj_ref.at[e], sems.at[e, 0]),
+                pltpu.make_async_copy(grad_hbm.at[e], grad_ref.at[e], sems.at[e, 1]),
+            )
+        )
+    for pair in copies:
+        for copy in pair:
+            copy.start()
+    for e in range(sems.shape[0]):
+        for copy in copies[e]:
+            copy.wait()
         low = lax.dot_general(grad_ref[e], proj_ref[e], NT, preferred_element_type=F32)
         out_ref[e] = jnp.concatenate([low, low], axis=1).astype(BF16)
 
@@ -135,7 +162,7 @@
             out_ref[i * dp + j] = scores[j * docs : (j + 1) * docs, :]
 
 
-def body(tokens, gates, routes, doc_ids, hidden_grad, proj_in, proj_out, val_features):
+def layer(tokens, gates, routes, doc_ids, hidden_grad, proj_in, proj_out, val_features):
     tok, width = tokens.shape
     top = routes.shape[1]
     rank = proj_in.shape[1]
@@ -150,23 +177,26 @@
     val_split = val_features.reshape(vals, exp_local, dp, entries // dp).transpose(2, 0, 1, 3)
     val_all = lax.all_to_all(val_split, "dp", split_axis=0, concat_axis=0, tiled=True)
 
+    vmem = pl.BlockSpec(memory_space=pltpu.VMEM)
+    hbm = pl.BlockSpec(memory_space=pltpu.HBM)
     pay_rows = rank + 2 * top + 8
     steps = 4
     pay = pl.pallas_call(
         act_kernel,
         out_shape=jax.ShapeDtypeStruct((pay_rows, tok), F32),
-        grid=(steps,),
-        in_specs=[
-            pl.BlockSpec((tok, width // steps), lambda s: (0, s)),
-            pl.BlockSpec((rank, width // steps), lambda s: (0, s)),
-            pl.BlockSpec((top, tok), lambda s: (0, 0)),
-            pl.BlockSpec((top, tok), lambda s: (0, 0)),
-            pl.BlockSpec((1, tok), lambda s: (0, 0)),
+        in_specs=[hbm, hbm, vmem, vmem, vmem],
+        out_specs=vmem,
+        scratch_shapes=[
+            pltpu.VMEM((tok, width), BF16),
+            pltpu.VMEM((rank, width), BF16),
+            pltpu.VMEM((rank, tok), F32),
+            pltpu.SemaphoreType.DMA((steps, 2)),
         ],
-        out_specs=pl.BlockSpec((pay_rows, tok), lambda s: (0, 0)),
-        scratch_shapes=[pltpu.VMEM((rank, tok), F32)],
+        compiler_params=pltpu.CompilerParams(vmem_limit_bytes=63 << 20),
         cost_estimate=pl.CostEstimate(
-            flops=2 * tok * width * rank, bytes_accessed=2 * width * (tok + rank), transcendentals=0
+            flops=2 * tok * width * rank,
+            bytes_accessed=2 * width * (tok + rank),
+            transcendentals=0,
         ),
     )(tokens, proj_in.T, routes.T, gates.T, doc_ids.reshape(1, tok))
 
@@ -174,16 +204,17 @@
     for k in range(1, groups):
         pays.append(lax.ppermute(pay, "expert", [(a, a ^ k) for a in range(groups)]))
 
-    pair = 2
     low = pl.pallas_call(
         lowered_kernel,
         out_shape=jax.ShapeDtypeStruct((exp_local, rows, 2 * rank), BF16),
-        grid=(exp_local // pair,),
-        in_specs=[
-            pl.BlockSpec((pair, rows, hidden), lambda s: (s, 0, 0)),
-            pl.BlockSpec((pair, rank, hidden), lambda s: (s, 0, 0)),
+        in_specs=[hbm, hbm],
+        out_specs=vmem,
+        scratch_shapes=[
+            pltpu.VMEM((exp_local, rows, hidden), BF16),
+            pltpu.VMEM((exp_local, rank, hidden), BF16),
+            pltpu.SemaphoreType.DMA((exp_local, 2)),
         ],
-        out_specs=pl.BlockSpec((pair, rows, 2 * rank), lambda s: (s, 0, 0)),
+        compiler_params=pltpu.CompilerParams(vmem_limit_bytes=62 << 20),
         cost_estimate=pl.CostEstimate(
             flops=2 * exp_local * rows * hidden * rank,
             bytes_accessed=2 * exp_local * hidden * (rows + rank),
@@ -192,7 +223,6 @@
     )(hidden_grad, proj_out.transpose(0, 2, 1))
 
     me = lax.axis_index("expert").astype(jnp.int32).reshape(1)
-    vmem = pl.BlockSpec(memory_space=pltpu.VMEM)
     feats = pl.pallas_call(
         functools.partial(feature_kernel, groups, rank, top),
         out_shape=jax.ShapeDtypeStruct((dp, DOC_GRP, chunks, exp_local, LANES), BF16),
@@ -202,6 +232,7 @@
             pltpu.VMEM((exp_local, rows, 2 * rank), BF16),
             pltpu.VMEM((DOC_GRP * rank // 2 * exp_local, 2 * rank), F32),
         ],
+        compiler_params=pltpu.CompilerParams(vmem_limit_bytes=16 << 20),
     )(me, *pays, low)
     feats_all = lax.all_to_all(feats, "dp", split_axis=0, concat_axis=0, tiled=True)
 
@@ -211,6 +242,7 @@
         out_shape=jax.ShapeDtypeStruct((groups * dp, DOC_GRP, dp * vals), F32),
         in_specs=[vmem, vmem],
         out_specs=vmem,
+        compiler_params=pltpu.CompilerParams(vmem_limit_bytes=40 << 20),
     )(feats_all, val_all)
     parts = lax.all_to_all(part, ("expert", "dp"), split_axis=0, concat_axis=0, tiled=True)
     return jnp.sum(parts, axis=0)
@@ -228,4 +260,4 @@
         P("dp", "expert", None),
     )
     out_specs = P("dp", None)
-    return jax.shard_map(body, mesh=mesh, in_specs=in_specs, out_specs=out_specs, check_vma=False)
+    return jax.shard_map(layer, mesh=mesh, in_specs=in_specs, out_specs=out_specs, check_vma=False)

time: 65.8 us -> 63.5 us (0.965)
  Pallas kernels: 17.2 us -> 14.8 us
    pallas_call x4, Pallas kernels: 17.2 us -> 14.8 us  [the longest x1 8.64 us: layer(): pl.pallas_call(lowered_kernel, out_shape=jax.ShapeDtypeStruct((exp_local,...]
  transfers between devices with their start and end apart: 4 -> 4, of which waited for: 1 -> 1; matrix products, arithmetic and copies ran while one was open for 0% -> 0% of each run, Pallas kernels for 13% -> 14%
where the time goes in v2:
time: 63.5 us; the launch traced here: 63.2 us
  blocking collectives  28 us (44%)
  Pallas kernels  14.8 us (23%)
  waiting for transfers between devices  9.27 us (15%)
  starting transfers between devices  9.21 us (15%)
  local copies, waits for them, and re-layouts  1.1 us (2%)
    all_to_all x1, blocking collectives, layer(): lax.all_to_all(val_split, 'dp', split_axis=0, concat_axis=0, tiled=True)  17.9 us
    all_to_all x1, blocking collectives, layer(): lax.all_to_all(part, ('expert', 'dp'), split_axis=0, concat_axis=0, tiled...  10.2 us
    all_to_all x1, waiting for transfers between devices, layer(): lax.all_to_all(feats, 'dp', split_axis=0, concat_axis=0, tiled=True)  9.26 us
    pallas_call x1, Pallas kernels, layer(): pl.pallas_call(lowered_kernel, out_shape=jax.ShapeDtypeStruct((exp_local,...  8.64 us
    all_to_all x1, starting transfers between devices, layer(): lax.all_to_all(feats, 'dp', split_axis=0, concat_axis=0, tiled=True)  6.03 us
    pallas_call x1, Pallas kernels, layer(): pl.pallas_call(act_kernel, out_shape=jax.ShapeDtypeStruct((pay_rows, tok)...  3.45 us
    ppermute x3, starting transfers between devices, layer(): lax.ppermute(pay, 'expert', [(a, a ^ k) for a in range(groups)])  3.18 us
    pallas_call x1, Pallas kernels, layer(): pl.pallas_call(functools.partial(feature_kernel, groups, rank, top), out_...  2.06 us
  transfers between devices with their start and end apart: 4, of which 1 were waited for; matrix products, arithmetic and copies ran while one was open for 0% of the time, Pallas kernels for 14%

profile of v2, /device:TPU:0, one launch (start us, length us, event | category | flops | bytes accessed | tf_op | source)
XLA Modules:
  0.0 63.2 jit_solution(4064603579399379213)
XLA Ops:
  0.0 0.0 copy-start.2
  0.0 3.5 %shard_map.82.refs_0_ = f32[88,128]{1,0:T(8,128)} custom-call(bf16[128,4096]{1,0:T(8,128)(2,1)} %tok_hbm.1, bf16[64,4096]{1,0:T(8,128)(2,1)} %bitcast.15, s32[8,128]{1,0:T(8,128)} %bitcast.17, f32[8,128]{1,0:T(8,128)} %bitcast.18, s32[1,128]{1,0:T(1,128)} %bitcast.19), custom_call_target="tpu_custom_call" | custom-call | flops 67108864 | bytes 1572864 | tf_op jit(solution)/shard_map/pallas_call | solution.py:184
  3.5 0.0 copy-start.1
  3.5 2.5 %collective-permute-start.2 = (f32[88,128]{1,0:T(8,128)}, f32[88,128]{1,0:T(8,128)S(1)}, u32[]{:S(2)}, u32[]{:S(2)}) collective-permute-start(f32[88,128]{1,0:T(8,128)} %shard_map.82.refs_0_), channel_id=1, source_target_pairs={{0,24},{8,16},{16,8},{24,0},{1,25},{9,17},{17,9},{25,1},{2,26},{10... | collective-permute-start | bytes 135176 | tf_op jit(solution)/shard_map/ppermute | solution.py:205
  6.0 0.6 %collective-permute-start.1 = (f32[88,128]{1,0:T(8,128)}, f32[88,128]{1,0:T(8,128)S(1)}, u32[]{:S(2)}, u32[]{:S(2)}) collective-permute-start(f32[88,128]{1,0:T(8,128)} %shard_map.82.refs_0_), channel_id=1, source_target_pairs={{0,16},{8,24},{16,0},{24,8},{1,17},{9,25},{17,1},{25,9},{2,18},{10... | collective-permute-start | bytes 135176 | tf_op jit(solution)/shard_map/ppermute | solution.py:205
  6.6 0.0 collective-permute-start
  6.7 8.6 %shard_map.83.refs_4_ = bf16[16,128,128]{2,1,0:T(8,128)(2,1)} custom-call(bf16[16,128,1536]{2,1,0:T(8,128)(2,1)} %grad_hbm.1, bf16[16,64,1536]{2,1,0:T(8,128)(2,1)} %bitcast.13), custom_call_target="tpu_custom_call" | custom-call | flops 402653184 | bytes 9437184 | tf_op jit(solution)/shard_map/pallas_call | solution.py:207
  15.3 0.0 collective-permute-done.2.refs_3_
  15.3 0.0 collective-permute-done.1.refs_2_
  15.3 0.0 collective-permute-done.refs_1_
  15.3 0.0 copy-done.1
  15.3 0.0 copy-start
  15.4 1.0 %copy-done = bf16[16,128,128]{2,1,0:T(8,128)(2,1)S(1)} copy-done((bf16[16,128,128]{2,1,0:T(8,128)(2,1)S(1)}, bf16[16,128,128]{2,1,0:T(8,128)(2,1)}, u32[]{:S(2)}) %copy-start) | copy-done | bytes 524312
  16.4 2.1 %shard_map.84 = bf16[8,2,4,16,128]{4,3,2,1,0:T(8,128)(2,1)} custom-call(s32[1]{0:T(128)} %bitcast.me_ref, f32[88,128]{1,0:T(8,128)S(1)} %copy-done.1, f32[88,128]{1,0:T(8,128)S(1)} %collective-permute-done.refs_1_, f32[88,128]{1,0:T(8,128)S(1)} %collective-permute-done.1.refs_2_, f32[88,128]{1,0:T(8,128)S(1)} %collective-permute-done.2.refs_3_, ...), custom_call_target="tpu_custom_call" | custom-call | tf_op jit(solution)/shard_map/pallas_call | solution.py:226
  18.4 6.0 %all-to-all-start = ((bf16[8,2,4,16,128]{4,3,2,1,0:T(8,128)(2,1)}), bf16[8,2,4,16,128]{4,3,2,1,0:T(8,128)(2,1)S(1)}, u32[]{:S(2)}, u32[]{:S(2)}) async-start(bf16[8,2,4,16,128]{4,3,2,1,0:T(8,128)(2,1)} %shard_map.84), calls=%async_computation | async-start | bytes 524288 | tf_op jit(solution)/shard_map/all_to_all | solution.py:237
  24.5 0.0 copy-done.2
  24.5 0.1 copy.12
  24.5 9.3 %all-to-all-done.feat_ref = bf16[8,2,4,16,128]{4,3,2,1,0:T(8,128)(2,1)S(1)} async-done(((bf16[8,2,4,16,128]{4,3,2,1,0:T(8,128)(2,1)}), bf16[8,2,4,16,128]{4,3,2,1,0:T(8,128)(2,1)S(1)}, u32[]{:S(2)}, u32[]{:S(2)}) %all-to-all-start) | async-done | bytes 262176 | tf_op jit(solution)/shard_map/all_to_all | solution.py:237
  33.8 17.9 %all_to_all.15.val_ref = bf16[8,4,16,512]{3,2,1,0:T(8,128)(2,1)S(1)} all-to-all(bf16[8,4,16,512]{3,2,1,0:T(8,128)(2,1)S(1)} %bitcast.14), channel_id=1, replica_groups=mesh['expert'=4,'dp'=8] {'dp'}, dimensions={0} | all-to-all | bytes 1048576 | tf_op jit(solution)/shard_map/all_to_all | solution.py:178
  51.7 0.7 %shard_map.85 = f32[32,2,32]{2,1,0:T(2,128)S(1)} custom-call(bf16[8,2,4,16,128]{4,3,2,1,0:T(8,128)(2,1)S(1)} %all-to-all-done.feat_ref, bf16[8,4,16,512]{3,2,1,0:T(8,128)(2,1)S(1)} %all_to_all.15.val_ref), custom_call_target="tpu_custom_call" | custom-call | tf_op jit(solution)/shard_map/pallas_call | solution.py:240
  52.4 10.2 %all_to_all.16 = f32[32,2,32]{2,1,0:T(2,128)S(1)} all-to-all(f32[32,2,32]{2,1,0:T(2,128)S(1)} %shard_map.85), channel_id=1, replica_groups=mesh['expert'=4,'dp'=8] {'expert','dp'}, dimensions={0} | all-to-all | bytes 16384 | tf_op jit(solution)/shard_map/all_to_all | solution.py:247
  62.5 0.6 reduce_sum.9
Async XLA Ops:
  0.0 24.5 %copy-start.2 = (bf16[4,16,4096]{2,1,0:T(8,128)(2,1)S(1)}, bf16[4,16,4096]{2,1,0:T(8,128)(2,1)}, u32[]{:S(2)}) copy-start(bf16[4,16,4096]{2,1,0:T(8,128)(2,1)} %param.15) | copy-start | bytes 1572868
  3.5 11.9 %copy-start.1 = (f32[88,128]{1,0:T(8,128)S(1)}, f32[88,128]{1,0:T(8,128)}, u32[]{:S(2)}) copy-start(f32[88,128]{1,0:T(8,128)} %shard_map.82.refs_0_) | copy-start | bytes 135172
  3.5 11.8 %collective-permute-start.2 = (f32[88,128]{1,0:T(8,128)}, f32[88,128]{1,0:T(8,128)S(1)}, u32[]{:S(2)}, u32[]{:S(2)}) collective-permute-start(f32[88,128]{1,0:T(8,128)} %shard_map.82.refs_0_), channel_id=1, source_target_pairs={{0,24},{8,16},{16,8},{24,0},{1,25},{9,17},{17,9},{25,1},{2,26},{10... | collective-permute-start | bytes 135176 | tf_op jit(solution)/shard_map/ppermute | solution.py:205
  6.0 9.3 %collective-permute-start.1 = (f32[88,128]{1,0:T(8,128)}, f32[88,128]{1,0:T(8,128)S(1)}, u32[]{:S(2)}, u32[]{:S(2)}) collective-permute-start(f32[88,128]{1,0:T(8,128)} %shard_map.82.refs_0_), channel_id=1, source_target_pairs={{0,16},{8,24},{16,0},{24,8},{1,17},{9,25},{17,1},{25,9},{2,18},{10... | collective-permute-start | bytes 135176 | tf_op jit(solution)/shard_map/ppermute | solution.py:205
  6.6 8.7 %collective-permute-start = (f32[88,128]{1,0:T(8,128)}, f32[88,128]{1,0:T(8,128)S(1)}, u32[]{:S(2)}, u32[]{:S(2)}) collective-permute-start(f32[88,128]{1,0:T(8,128)} %shard_map.82.refs_0_), channel_id=1, source_target_pairs={{0,8},{8,0},{16,24},{24,16},{1,9},{9,1},{17,25},{25,17},{2,10},{10... | collective-permute-start | bytes 135176 | tf_op jit(solution)/shard_map/ppermute | solution.py:205
  15.3 1.0 %copy-start = (bf16[16,128,128]{2,1,0:T(8,128)(2,1)S(1)}, bf16[16,128,128]{2,1,0:T(8,128)(2,1)}, u32[]{:S(2)}) copy-start(bf16[16,128,128]{2,1,0:T(8,128)(2,1)} %shard_map.83.refs_4_) | copy-start | bytes 1572868
  18.4 15.4 %all-to-all-start = ((bf16[8,2,4,16,128]{4,3,2,1,0:T(8,128)(2,1)}), bf16[8,2,4,16,128]{4,3,2,1,0:T(8,128)(2,1)S(1)}, u32[]{:S(2)}, u32[]{:S(2)}) async-start(bf16[8,2,4,16,128]{4,3,2,1,0:T(8,128)(2,1)} %shard_map.84), calls=%async_computation | async-start | bytes 524288 | tf_op jit(solution)/shard_map/all_to_all | solution.py:237

commit v3 on v2

--- a/solution.py
+++ b/solution.py
@@ -10,13 +10,17 @@
 
 DOC_GRP = 2
 LANES = 128
+VL_F = 53 << 20
 F32 = jnp.float32
 BF16 = jnp.bfloat16
 NT = (((1,), (1,)), ((), ()))
 TN = (((0,), (0,)), ((), ()))
 
 
-def act_kernel(tok_hbm, proj_hbm, routes_ref, gates_ref, docs_ref, out_ref, tok_ref, proj_ref, acc_ref, sems):
+def act_kernel(
+    tok_hbm, proj_hbm, val_hbm, routes_ref, gates_ref, docs_ref, out_ref, split_ref, *scratch
+):
+    tok_ref, proj_ref, acc_ref, sems, split_sems = scratch
     rank = proj_ref.shape[0]
     top = routes_ref.shape[0]
     half = rank // 2
@@ -34,6 +38,15 @@
     for pair in copies:
         for copy in pair:
             copy.start()
+    parts, _, _, piece = split_ref.shape
+    splits = [
+        pltpu.make_async_copy(
+            val_hbm.at[:, :, pl.ds(j * piece, piece)], split_ref.at[j], split_sems.at[j]
+        )
+        for j in range(parts)
+    ]
+    for copy in splits:
+        copy.start()
     out_ref[rank : rank + top, :] = routes_ref[...].astype(F32)
     out_ref[rank + top : rank + 2 * top, :] = gates_ref[...]
     out_ref[rank + 2 * top :, :] = jnp.broadcast_to(
@@ -50,30 +63,27 @@
     acc_ref[...] = total
     out_ref[0:half, :] = acc_ref[pl.ds(0, half, stride=2), :]
     out_ref[half:rank, :] = acc_ref[pl.ds(1, half, stride=2), :]
-
-
-def lowered_kernel(grad_hbm, proj_hbm, out_ref, grad_ref, proj_ref, sems):
+    for copy in splits:
+        copy.wait()
+
+
+def feature_kernel(groups, rank, top, me_ref, *refs):
+    pays = refs[:groups]
+    grad_hbm, proj_hbm, out_ref, a_ref, f_ref, grad_ref, proj_ref, sems = refs[groups:]
+    exp_local, rows, _ = grad_ref.shape
+    batch = exp_local // sems.shape[0]
     copies = []
-    for e in range(sems.shape[0]):
+    for n in range(sems.shape[0]):
+        part = pl.ds(n * batch, batch)
         copies.append(
             (
-                pltpu.make_async_copy(proj_hbm.at[e], proj_ref.at[e], sems.at[e, 0]),
-                pltpu.make_async_copy(grad_hbm.at[e], grad_ref.at[e], sems.at[e, 1]),
+                pltpu.make_async_copy(proj_hbm.at[part], proj_ref.at[part], sems.at[n, 0]),
+                pltpu.make_async_copy(grad_hbm.at[part], grad_ref.at[part], sems.at[n, 1]),
             )
         )
     for pair in copies:
         for copy in pair:
             copy.start()
-    for e in range(sems.shape[0]):
-        for copy in copies[e]:
-            copy.wait()
-        low = lax.dot_general(grad_ref[e], proj_ref[e], NT, preferred_element_type=F32)
-        out_ref[e] = jnp.concatenate([low, low], axis=1).astype(BF16)
-
-
-def feature_kernel(groups, rank, top, me_ref, *refs):
-    pays, low_ref, out_ref, a_ref, f_ref = refs[:groups], *refs[groups:]
-    exp_local, rows, _ = low_ref.shape
     cap = rows // groups
     tok = pays[0].shape[1]
     half = rank // 2
@@ -123,7 +133,12 @@
     wide = DOC_GRP * half
     lane = lax.broadcasted_iota(jnp.int32, (wide, 2 * rank), 1)
     for e in range(exp_local):
-        feat = lax.dot_general(a_ref[e], low_ref[e], TN, preferred_element_type=F32)
+        if e % batch == 0:
+            for copy in copies[e // batch]:
+                copy.wait()
+        low = lax.dot_general(grad_ref[e], proj_ref[e], NT, preferred_element_type=F32)
+        low = jnp.concatenate([low, low], axis=1).astype(BF16)
+        feat = lax.dot_general(a_ref[e], low, TN, preferred_element_type=F32)
         f_ref[pl.ds(e, wide, stride=exp_local), :] = jnp.where(
             lane < rank, feat[:wide], feat[wide:]
         )
@@ -174,23 +189,24 @@
     experts = exp_local * groups
     chunks = entries // LANES // dp
 
-    val_split = val_features.reshape(vals, exp_local, dp, entries // dp).transpose(2, 0, 1, 3)
-    val_all = lax.all_to_all(val_split, "dp", split_axis=0, concat_axis=0, tiled=True)
-
     vmem = pl.BlockSpec(memory_space=pltpu.VMEM)
     hbm = pl.BlockSpec(memory_space=pltpu.HBM)
     pay_rows = rank + 2 * top + 8
-    steps = 4
-    pay = pl.pallas_call(
+    steps = 2
+    pay, val_split = pl.pallas_call(
         act_kernel,
-        out_shape=jax.ShapeDtypeStruct((pay_rows, tok), F32),
-        in_specs=[hbm, hbm, vmem, vmem, vmem],
-        out_specs=vmem,
+        out_shape=(
+            jax.ShapeDtypeStruct((pay_rows, tok), F32),
+            jax.ShapeDtypeStruct((dp, vals, exp_local, entries // dp), BF16),
+        ),
+        in_specs=[hbm, hbm, hbm, vmem, vmem, vmem],
+        out_specs=(vmem, vmem),
         scratch_shapes=[
             pltpu.VMEM((tok, width), BF16),
             pltpu.VMEM((rank, width), BF16),
             pltpu.VMEM((rank, tok), F32),
             pltpu.SemaphoreType.DMA((steps, 2)),
+            pltpu.SemaphoreType.DMA((dp,)),
         ],
         compiler_params=pltpu.CompilerParams(vmem_limit_bytes=63 << 20),
         cost_estimate=pl.CostEstimate(
@@ -198,42 +214,34 @@
             bytes_accessed=2 * width * (tok + rank),
             transcendentals=0,
         ),
-    )(tokens, proj_in.T, routes.T, gates.T, doc_ids.reshape(1, tok))
+    )(tokens, proj_in.T, val_features, routes.T, gates.T, doc_ids.reshape(1, tok))
+
+    val_all = lax.all_to_all(val_split, "dp", split_axis=0, concat_axis=0, tiled=True)
 
     pays = [pay]
     for k in range(1, groups):
         pays.append(lax.ppermute(pay, "expert", [(a, a ^ k) for a in range(groups)]))
 
-    low = pl.pallas_call(
-        lowered_kernel,
-        out_shape=jax.ShapeDtypeStruct((exp_local, rows, 2 * rank), BF16),
-        in_specs=[hbm, hbm],
+    me = lax.axis_index("expert").astype(jnp.int32).reshape(1)
+    feats = pl.pallas_call(
+        functools.partial(feature_kernel, groups, rank, top),
+        out_shape=jax.ShapeDtypeStruct((dp, DOC_GRP, chunks, exp_local, LANES), BF16),
+        in_specs=[pl.BlockSpec(memory_space=pltpu.SMEM)] + [vmem] * groups + [hbm, hbm],
         out_specs=vmem,
         scratch_shapes=[
+            pltpu.VMEM((exp_local, rows, 2 * rank), BF16),
+            pltpu.VMEM((DOC_GRP * rank // 2 * exp_local, 2 * rank), F32),
             pltpu.VMEM((exp_local, rows, hidden), BF16),
             pltpu.VMEM((exp_local, rank, hidden), BF16),
-            pltpu.SemaphoreType.DMA((exp_local, 2)),
+            pltpu.SemaphoreType.DMA((4, 2)),
         ],
-        compiler_params=pltpu.CompilerParams(vmem_limit_bytes=62 << 20),
+        compiler_params=pltpu.CompilerParams(vmem_limit_bytes=VL_F),
         cost_estimate=pl.CostEstimate(
             flops=2 * exp_local * rows * hidden * rank,
             bytes_accessed=2 * exp_local * hidden * (rows + rank),
             transcendentals=0,
         ),
-    )(hidden_grad, proj_out.transpose(0, 2, 1))
-
-    me = lax.axis_index("expert").astype(jnp.int32).reshape(1)
-    feats = pl.pallas_call(
-        functools.partial(feature_kernel, groups, rank, top),
-        out_shape=jax.ShapeDtypeStruct((dp, DOC_GRP, chunks, exp_local, LANES), BF16),
-        in_specs=[pl.BlockSpec(memory_space=pltpu.SMEM)] + [vmem] * (groups + 1),
-        out_specs=vmem,
-        scratch_shapes=[
-            pltpu.VMEM((exp_local, rows, 2 * rank), BF16),
-            pltpu.VMEM((DOC_GRP * rank // 2 * exp_local, 2 * rank), F32),
-        ],
-        compiler_params=pltpu.CompilerParams(vmem_limit_bytes=16 << 20),
-    )(me, *pays, low)
+    )(me, *pays, hidden_grad, proj_out.transpose(0, 2, 1))
     feats_all = lax.all_to_all(feats, "dp", split_axis=0, concat_axis=0, tiled=True)
 
     scale = 1.0 / float(experts * entries) ** 0.5

time: 63.5 us -> 64.8 us (1.020)
  blocking collectives: 28 us -> 42.7 us
  starting transfers between devices: 9.21 us -> 3.18 us
  waiting for transfers between devices: 9.27 us -> 3.77 us
  Pallas kernels: 14.8 us -> 13.4 us
    all_to_all x0 -> x1, blocking collectives: none -> 14.5 us  [layer(): lax.all_to_all(feats, 'dp', split_axis=0, concat_axis=0, tiled=True)]
    all_to_all x1 -> x0, waiting for transfers between devices: 9.26 us -> none  [layer(): lax.all_to_all(feats, 'dp', split_axis=0, concat_axis=0, tiled=True)]
    pallas_call x2 -> x1, Pallas kernels: 12.1 us -> 3.68 us  [layer(): pl.pallas_call(act_kernel, out_shape=(jax.ShapeDtypeStruct((pay_rows, tok...]
    pallas_call x1, Pallas kernels: 2.06 us -> 9.06 us  [layer(): pl.pallas_call(functools.partial(feature_kernel, groups, rank, top), out_...]
    all_to_all x1 -> x0, starting transfers between devices: 6.03 us -> none  [layer(): lax.all_to_all(feats, 'dp', split_axis=0, concat_axis=0, tiled=True)]
    ppermute x3, waiting for transfers between devices: 0.01 us -> 3.77 us  [layer(): lax.ppermute(pay, 'expert', [(a, a ^ k) for a in range(groups)])]
  transfers between devices with their start and end apart: 4 -> 3, of which waited for: 1 -> 2; matrix products, arithmetic and copies ran while one was open for 0% -> 0% of each run, Pallas kernels for 14% -> 0%
where the time goes in v3:
time: 64.8 us; the launch traced here: 64.5 us
  blocking collectives  42.7 us (66%)
  Pallas kernels  13.4 us (21%)
  waiting for transfers between devices  3.77 us (6%)
  starting transfers between devices  3.18 us (5%)
  local copies, waits for them, and re-layouts  0.79 us (1%)
    all_to_all x1, blocking collectives, layer(): lax.all_to_all(val_split, 'dp', split_axis=0, concat_axis=0, tiled=True)  17.5 us
    all_to_all x1, blocking collectives, layer(): lax.all_to_all(feats, 'dp', split_axis=0, concat_axis=0, tiled=True)  14.5 us
    all_to_all x1, blocking collectives, layer(): lax.all_to_all(part, ('expert', 'dp'), split_axis=0, concat_axis=0, tiled...  10.7 us
    pallas_call x1, Pallas kernels, layer(): pl.pallas_call(functools.partial(feature_kernel, groups, rank, top), out_...  9.06 us
    ppermute x3, waiting for transfers between devices, layer(): lax.ppermute(pay, 'expert', [(a, a ^ k) for a in range(groups)])  3.77 us
    pallas_call x1, Pallas kernels, layer(): pl.pallas_call(act_kernel, out_shape=(jax.ShapeDtypeStruct((pay_rows, tok...  3.68 us
    ppermute x3, starting transfers between devices, layer(): lax.ppermute(pay, 'expert', [(a, a ^ k) for a in range(groups)])  3.18 us
  transfers between devices with their start and end apart: 3, of which 2 were waited for; matrix products, arithmetic and copies ran while one was open for 0% of the time, Pallas kernels for 0%

profile of v3, /device:TPU:0, one launch (start us, length us, event | category | flops | bytes accessed | tf_op | source)
XLA Modules:
  0.0 64.5 jit_solution(18201812541342086841)
XLA Ops:
  0.0 3.7 %shard_map.82 = (f32[88,128]{1,0:T(8,128)}, bf16[8,4,16,512]{3,2,1,0:T(8,128)(2,1)}) custom-call(bf16[128,4096]{1,0:T(8,128)(2,1)} %tok_hbm.1, bf16[64,4096]{1,0:T(8,128)(2,1)} %bitcast.7, bf16[4,16,4096]{2,1,0:T(8,128)(2,1)} %val_hbm.1, s32[8,128]{1,0:T(8,128)} %bitcast.8, f32[8,128]{1,0:T(8,128)} %bitcast.9, s32[1,128]{1,0:T(1,128)} %bitcast.10), custom_call_target="tpu_custom_call" | custom-call | flops 67108864 | bytes 1572864 | tf_op jit(solution)/shard_map/pallas_call | solution.py:196
  3.7 2.5 %collective-permute-start.2 = (f32[88,128]{1,0:T(8,128)}, f32[88,128]{1,0:T(8,128)S(1)}, u32[]{:S(2)}, u32[]{:S(2)}) collective-permute-start(f32[88,128]{1,0:T(8,128)} %get-tuple-element.7.refs_0_), channel_id=1, source_target_pairs={{0,24},{8,16},{16,8},{24,0},{1,25},{9,17},{17,9},{25,1},{2,26},{10... | collective-permute-start | bytes 135176 | tf_op jit(solution)/shard_map/ppermute | solution.py:223
  6.2 0.6 collective-permute-start.1
  6.8 0.0 collective-permute-start
  6.9 1.7 %collective-permute-done.2.refs_3_ = f32[88,128]{1,0:T(8,128)S(1)} collective-permute-done((f32[88,128]{1,0:T(8,128)}, f32[88,128]{1,0:T(8,128)S(1)}, u32[]{:S(2)}, u32[]{:S(2)}) %collective-permute-start.2) | collective-permute-done | bytes 45088 | tf_op jit(solution)/shard_map/ppermute | solution.py:223
  8.5 2.1 %collective-permute-done.1.refs_2_ = f32[88,128]{1,0:T(8,128)S(1)} collective-permute-done((f32[88,128]{1,0:T(8,128)}, f32[88,128]{1,0:T(8,128)S(1)}, u32[]{:S(2)}, u32[]{:S(2)}) %collective-permute-start.1) | collective-permute-done | bytes 45088 | tf_op jit(solution)/shard_map/ppermute | solution.py:223
  10.6 0.0 collective-permute-done.refs_1_
  10.6 0.0 copy-start
  10.6 0.8 %copy-done = f32[88,128]{1,0:T(8,128)S(1)} copy-done((f32[88,128]{1,0:T(8,128)S(1)}, f32[88,128]{1,0:T(8,128)}, u32[]{:S(2)}) %copy-start) | copy-done | bytes 45080
  11.4 0.0 copy-start.1
  11.4 9.1 %shard_map.83 = bf16[8,2,4,16,128]{4,3,2,1,0:T(8,128)(2,1)S(1)} custom-call(s32[1]{0:T(128)} %bitcast.me_ref, f32[88,128]{1,0:T(8,128)S(1)} %copy-done, f32[88,128]{1,0:T(8,128)S(1)} %collective-permute-done.refs_1_, f32[88,128]{1,0:T(8,128)S(1)} %collective-permute-done.1.refs_2_, f32[88,128]{1,0:T(8,128)S(1)} %collective-permute-done.2.refs_3_, ...), custom_call_target="tpu_custom_call" | custom-call | flops 402653184 | bytes 9437184 | tf_op jit(solution)/shard_map/pallas_call | solution.py:226
  20.5 14.5 %all_to_all.15.feat_ref = bf16[8,2,4,16,128]{4,3,2,1,0:T(8,128)(2,1)S(1)} all-to-all(bf16[8,2,4,16,128]{4,3,2,1,0:T(8,128)(2,1)S(1)} %shard_map.83), channel_id=1, replica_groups=mesh['expert'=4,'dp'=8] {'dp'}, dimensions={0} | all-to-all | bytes 524288 | tf_op jit(solution)/shard_map/all_to_all | solution.py:245
  35.0 0.0 copy-done.1
  35.0 17.5 %all_to_all.16.val_ref = bf16[8,4,16,512]{3,2,1,0:T(8,128)(2,1)S(1)} all-to-all(bf16[8,4,16,512]{3,2,1,0:T(8,128)(2,1)S(1)} %copy-done.1), channel_id=1, replica_groups=mesh['expert'=4,'dp'=8] {'dp'}, dimensions={0} | all-to-all | bytes 1048576 | tf_op jit(solution)/shard_map/all_to_all | solution.py:219
  52.5 0.7 %shard_map.84 = f32[32,2,32]{2,1,0:T(2,128)S(1)} custom-call(bf16[8,2,4,16,128]{4,3,2,1,0:T(8,128)(2,1)S(1)} %all_to_all.15.feat_ref, bf16[8,4,16,512]{3,2,1,0:T(8,128)(2,1)S(1)} %all_to_all.16.val_ref), custom_call_target="tpu_custom_call" | custom-call | tf_op jit(solution)/shard_map/pallas_call | solution.py:248
  53.2 10.7 %all_to_all.17 = f32[32,2,32]{2,1,0:T(2,128)S(1)} all-to-all(f32[32,2,32]{2,1,0:T(2,128)S(1)} %shard_map.84), channel_id=1, replica_groups=mesh['expert'=4,'dp'=8] {'expert','dp'}, dimensions={0} | all-to-all | bytes 16384 | tf_op jit(solution)/shard_map/all_to_all | solution.py:255
  63.9 0.6 reduce_sum.9
Async XLA Ops:
  3.7 4.9 %collective-permute-start.2 = (f32[88,128]{1,0:T(8,128)}, f32[88,128]{1,0:T(8,128)S(1)}, u32[]{:S(2)}, u32[]{:S(2)}) collective-permute-start(f32[88,128]{1,0:T(8,128)} %get-tuple-element.7.refs_0_), channel_id=1, source_target_pairs={{0,24},{8,16},{16,8},{24,0},{1,25},{9,17},{17,9},{25,1},{2,26},{10... | collective-permute-start | bytes 135176 | tf_op jit(solution)/shard_map/ppermute | solution.py:223
  6.2 4.4 %collective-permute-start.1 = (f32[88,128]{1,0:T(8,128)}, f32[88,128]{1,0:T(8,128)S(1)}, u32[]{:S(2)}, u32[]{:S(2)}) collective-permute-start(f32[88,128]{1,0:T(8,128)} %get-tuple-element.7.refs_0_), channel_id=1, source_target_pairs={{0,16},{8,24},{16,0},{24,8},{1,17},{9,25},{17,1},{25,9},{2,18},{10... | collective-permute-start | bytes 135176 | tf_op jit(solution)/shard_map/ppermute | solution.py:223
  6.8 3.8 %collective-permute-start = (f32[88,128]{1,0:T(8,128)}, f32[88,128]{1,0:T(8,128)S(1)}, u32[]{:S(2)}, u32[]{:S(2)}) collective-permute-start(f32[88,128]{1,0:T(8,128)} %get-tuple-element.7.refs_0_), channel_id=1, source_target_pairs={{0,8},{8,0},{16,24},{24,16},{1,9},{9,1},{17,25},{25,17},{2,10},{10... | collective-permute-start | bytes 135176 | tf_op jit(solution)/shard_map/ppermute | solution.py:223
  10.6 0.8 %copy-start = (f32[88,128]{1,0:T(8,128)S(1)}, f32[88,128]{1,0:T(8,128)}, u32[]{:S(2)}) copy-start(f32[88,128]{1,0:T(8,128)} %get-tuple-element.7.refs_0_) | copy-start | bytes 135172
  11.4 23.6 %copy-start.1 = (bf16[8,4,16,512]{3,2,1,0:T(8,128)(2,1)S(1)}, bf16[8,4,16,512]{3,2,1,0:T(8,128)(2,1)}, u32[]{:S(2)}) copy-start(bf16[8,4,16,512]{3,2,1,0:T(8,128)(2,1)} %get-tuple-element.8) | copy-start | bytes 1572868

commit v4 on v3

--- a/solution.py
+++ b/solution.py
@@ -20,7 +20,7 @@
 def act_kernel(
     tok_hbm, proj_hbm, val_hbm, routes_ref, gates_ref, docs_ref, out_ref, split_ref, *scratch
 ):
-    tok_ref, proj_ref, acc_ref, sems, split_sems = scratch
+    tok_ref, proj_ref, acc_ref, piece_ref, sems, split_sems = scratch
     rank = proj_ref.shape[0]
     top = routes_ref.shape[0]
     half = rank // 2
@@ -35,23 +35,27 @@
                 pltpu.make_async_copy(tok_hbm.at[:, cols], tok_ref.at[:, cols], sems.at[s, 1]),
             )
         )
+    parts, _, _, piece = piece_ref.shape
+    splits = [
+        pltpu.make_async_copy(
+            val_hbm.at[:, :, pl.ds(j * piece, piece)], piece_ref.at[j], split_sems.at[j]
+        )
+        for j in range(parts)
+    ]
+    whole = pltpu.make_async_copy(piece_ref, split_ref, split_sems.at[parts])
+    for copy in splits:
+        copy.start()
     for pair in copies:
         for copy in pair:
             copy.start()
-    parts, _, _, piece = split_ref.shape
-    splits = [
-        pltpu.make_async_copy(
-            val_hbm.at[:, :, pl.ds(j * piece, piece)], split_ref.at[j], split_sems.at[j]
-        )
-        for j in range(parts)
-    ]
-    for copy in splits:
-        copy.start()
     out_ref[rank : rank + top, :] = routes_ref[...].astype(F32)
     out_ref[rank + top : rank + 2 * top, :] = gates_ref[...]
     out_ref[rank + 2 * top :, :] = jnp.broadcast_to(
         docs_ref[...].astype(F32), (out_ref.shape[0] - rank - 2 * top, out_ref.shape[1])
     )
+    for copy in splits:
+        copy.wait()
+    whole.start()
     total = jnp.zeros(acc_ref.shape, F32)
     for s in range(steps):
         for copy in copies[s]:
@@ -63,13 +67,14 @@
     acc_ref[...] = total
     out_ref[0:half, :] = acc_ref[pl.ds(0, half, stride=2), :]
     out_ref[half:rank, :] = acc_ref[pl.ds(1, half, stride=2), :]
-    for copy in splits:
-        copy.wait()
-
-
-def feature_kernel(groups, rank, top, me_ref, *refs):
+    whole.wait()
+
+
+def feature_kernel(groups, parts, rank, top, me_ref, *refs):
     pays = refs[:groups]
-    grad_hbm, proj_hbm, out_ref, a_ref, f_ref, grad_ref, proj_ref, sems = refs[groups:]
+    grad_hbm, proj_hbm = refs[groups : groups + 2]
+    outs = refs[groups + 2 : groups + 2 + parts]
+    a_ref, low_ref, f_ref, grad_ref, proj_ref, sems = refs[groups + 2 + parts :]
     exp_local, rows, _ = grad_ref.shape
     batch = exp_local // sems.shape[0]
     copies = []
@@ -106,12 +111,12 @@
         slot = jnp.dot(hit.astype(BF16), before, preferred_element_type=F32)
         slot = jnp.where(hit > 0.0, slot, -1.0)
         doc = pay[rank + 2 * top : rank + 2 * top + 1, :]
-        parts = []
+        masked = []
         for par in range(2):
             act = pay[par * half : (par + 1) * half, :]
             for d in range(DOC_GRP):
-                parts.append(jnp.where(doc == float(d), act, 0.0))
-        act = jnp.concatenate(parts, axis=0)
+                masked.append(jnp.where(doc == float(d), act, 0.0))
+        act = jnp.concatenate(masked, axis=0)
         high = act.astype(BF16)
         low = (act - high.astype(F32)).astype(BF16)
         right = jnp.concatenate([high, low], axis=1)
@@ -132,49 +137,64 @@
             a_ref[e, pl.ds(source, cap), :] = sent[e * cap : (e + 1) * cap, :]
     wide = DOC_GRP * half
     lane = lax.broadcasted_iota(jnp.int32, (wide, 2 * rank), 1)
-    for e in range(exp_local):
-        if e % batch == 0:
-            for copy in copies[e // batch]:
-                copy.wait()
-        low = lax.dot_general(grad_ref[e], proj_ref[e], NT, preferred_element_type=F32)
-        low = jnp.concatenate([low, low], axis=1).astype(BF16)
-        feat = lax.dot_general(a_ref[e], low, TN, preferred_element_type=F32)
-        f_ref[pl.ds(e, wide, stride=exp_local), :] = jnp.where(
-            lane < rank, feat[:wide], feat[wide:]
-        )
-    parts, _, chunks, _, _ = out_ref.shape
+
+    def project(n):
+        for copy in copies[n]:
+            copy.wait()
+        for e in range(n * batch, (n + 1) * batch):
+            low = lax.dot_general(grad_ref[e], proj_ref[e], NT, preferred_element_type=F32)
+            low_ref[e] = jnp.concatenate([low, low], axis=1).astype(BF16)
+
+    def outer(n):
+        for e in range(n * batch, (n + 1) * batch):
+            feat = lax.dot_general(a_ref[e], low_ref[e], TN, preferred_element_type=F32)
+            f_ref[pl.ds(e, wide, stride=exp_local), :] = jnp.where(
+                lane < rank, feat[:wide], feat[wide:]
+            )
+
+    for n in range(sems.shape[0]):
+        project(n)
+        if n:
+            outer(n - 1)
+    outer(sems.shape[0] - 1)
+    _, chunks, _, _ = outs[0].shape
     size = chunks * exp_local
-    for d in range(DOC_GRP):
-        for p in range(parts):
-            start = (d * half + p * chunks) * exp_local
-            out_ref[p, d] = (
-                f_ref[start : start + size, :].astype(BF16).reshape(chunks, exp_local, 2 * rank)
-            )
-
-
-def score_kernel(scale, feat_ref, val_ref, out_ref):
-    dp, docs, chunks, exp_local, lanes = feat_ref.shape
+    for k in range(parts):
+        part = lax.bitwise_xor(me_ref[1], k)
+        for d in range(DOC_GRP):
+            start = pl.multiple_of((d * half + part * chunks) * exp_local, size)
+            outs[k][d] = (
+                f_ref[pl.ds(start, size), :].astype(BF16).reshape(chunks, exp_local, 2 * rank)
+            )
+
+
+def score_kernel(parts, scale, me_ref, *refs):
+    feats, val_ref, out_ref = refs[:parts], refs[parts], refs[parts + 1]
+    docs, chunks, exp_local, lanes = feats[0].shape
     vals = val_ref.shape[1]
-    left_rows, right_rows = dp * docs * exp_local, dp * vals * exp_local
+    left_rows, right_rows = parts * docs * exp_local, parts * vals * exp_local
     total = jnp.zeros((left_rows, right_rows), F32)
     for c in range(chunks):
-        left = feat_ref[:, :, c].reshape(left_rows, lanes)
+        left = jnp.concatenate(
+            [feat[:, c].reshape(docs * exp_local, lanes) for feat in feats], axis=0
+        )
         right = val_ref[:, :, :, c * lanes : (c + 1) * lanes].reshape(right_rows, lanes)
         total += lax.dot_general(left, right, NT, preferred_element_type=F32)
     row = lax.broadcasted_iota(jnp.int32, total.shape, 0) % exp_local
     col = lax.broadcasted_iota(jnp.int32, total.shape, 1) % exp_local
     total = jnp.where(row == col, total, 0.0)
-    total = jnp.sum(total.reshape(dp * docs, exp_local, right_rows), axis=1)
+    total = jnp.sum(total.reshape(parts * docs, exp_local, right_rows), axis=1)
     pick = (
-        lax.broadcasted_iota(jnp.int32, (right_rows, dp * vals), 0) // exp_local
-        == lax.broadcasted_iota(jnp.int32, (right_rows, dp * vals), 1)
+        lax.broadcasted_iota(jnp.int32, (right_rows, parts * vals), 0) // exp_local
+        == lax.broadcasted_iota(jnp.int32, (right_rows, parts * vals), 1)
     ).astype(F32)
     scores = jnp.dot(
         total, pick, preferred_element_type=F32, precision=lax.Precision.HIGHEST
     ) * scale
-    for i in range(out_ref.shape[0] // dp):
-        for j in range(dp):
-            out_ref[i * dp + j] = scores[j * docs : (j + 1) * docs, :]
+    for k in range(parts):
+        group = lax.bitwise_xor(me_ref[1], k)
+        for i in range(out_ref.shape[0] // parts):
+            out_ref[i * parts + group] = scores[k * docs : (k + 1) * docs, :]
 
 
 def layer(tokens, gates, routes, doc_ids, hidden_grad, proj_in, proj_out, val_features):
@@ -200,13 +220,14 @@
             jax.ShapeDtypeStruct((dp, vals, exp_local, entries // dp), BF16),
         ),
         in_specs=[hbm, hbm, hbm, vmem, vmem, vmem],
-        out_specs=(vmem, vmem),
+        out_specs=(vmem, hbm),
         scratch_shapes=[
             pltpu.VMEM((tok, width), BF16),
             pltpu.VMEM((rank, width), BF16),
             pltpu.VMEM((rank, tok), F32),
+            pltpu.VMEM((dp, vals, exp_local, entries // dp), BF16),
             pltpu.SemaphoreType.DMA((steps, 2)),
-            pltpu.SemaphoreType.DMA((dp,)),
+            pltpu.SemaphoreType.DMA((dp + 1,)),
         ],
         compiler_params=pltpu.CompilerParams(vmem_limit_bytes=63 << 20),
         cost_estimate=pl.CostEstimate(
@@ -222,13 +243,16 @@
     for k in range(1, groups):
         pays.append(lax.ppermute(pay, "expert", [(a, a ^ k) for a in range(groups)]))
 
-    me = lax.axis_index("expert").astype(jnp.int32).reshape(1)
+    me = jnp.stack([lax.axis_index("expert"), lax.axis_index("dp")]).astype(jnp.int32)
+    smem = pl.BlockSpec(memory_space=pltpu.SMEM)
+    block = jax.ShapeDtypeStruct((DOC_GRP, chunks, exp_local, LANES), BF16)
     feats = pl.pallas_call(
-        functools.partial(feature_kernel, groups, rank, top),
-        out_shape=jax.ShapeDtypeStruct((dp, DOC_GRP, chunks, exp_local, LANES), BF16),
-        in_specs=[pl.BlockSpec(memory_space=pltpu.SMEM)] + [vmem] * groups + [hbm, hbm],
-        out_specs=vmem,
+        functools.partial(feature_kernel, groups, dp, rank, top),
+        out_shape=(block,) * dp,
+        in_specs=[smem] + [vmem] * groups + [hbm, hbm],
+        out_specs=(vmem,) * dp,
         scratch_shapes=[
+            pltpu.VMEM((exp_local, rows, 2 * rank), BF16),
             pltpu.VMEM((exp_local, rows, 2 * rank), BF16),
             pltpu.VMEM((DOC_GRP * rank // 2 * exp_local, 2 * rank), F32),
             pltpu.VMEM((exp_local, rows, hidden), BF16),
@@ -242,16 +266,18 @@
             transcendentals=0,
         ),
     )(me, *pays, hidden_grad, proj_out.transpose(0, 2, 1))
-    feats_all = lax.all_to_all(feats, "dp", split_axis=0, concat_axis=0, tiled=True)
+    arrived = [feats[0]]
+    for k in range(1, dp):
+        arrived.append(lax.ppermute(feats[k], "dp", [(a, a ^ k) for a in range(dp)]))
 
     scale = 1.0 / float(experts * entries) ** 0.5
     part = pl.pallas_call(
-        functools.partial(score_kernel, scale),
+        functools.partial(score_kernel, dp, scale),
         out_shape=jax.ShapeDtypeStruct((groups * dp, DOC_GRP, dp * vals), F32),
-        in_specs=[vmem, vmem],
+        in_specs=[smem] + [vmem] * (dp + 1),
         out_specs=vmem,
         compiler_params=pltpu.CompilerParams(vmem_limit_bytes=40 << 20),
-    )(feats_all, val_all)
+    )(me, *arrived, val_all)
     parts = lax.all_to_all(part, ("expert", "dp"), split_axis=0, concat_axis=0, tiled=True)
     return jnp.sum(parts, axis=0)
 

time: 64.8 us -> 50.9 us (0.79)
  blocking collectives: 42.7 us -> 8.88 us
  starting transfers between devices: 3.18 us -> 20.4 us
  waiting for transfers between devices: 3.77 us -> 9.55 us
  Pallas kernels: 13.4 us -> 10.3 us
    all_to_all x2 -> x0, blocking collectives: 32 us -> none  [the longest x1 17.5 us: layer(): lax.all_to_all(val_split, 'dp', split_axis=0, concat_axis=0, tiled=True)]
    ppermute x0 -> x7, starting transfers between devices: none -> 11.2 us  [layer(): lax.ppermute(feats[k], 'dp', [(a, a ^ k) for a in range(dp)])]
    all_to_all x0 -> x1, starting transfers between devices: none -> 7.29 us  [layer(): lax.all_to_all(val_split, 'dp', split_axis=0, concat_axis=0, tiled=True)]
    ppermute x0 -> x7, waiting for transfers between devices: none -> 6.08 us  [layer(): lax.ppermute(feats[k], 'dp', [(a, a ^ k) for a in range(dp)])]
    pallas_call x2, Pallas kernels: 9.74 us -> 6.71 us  [the longest x1 5.48 us: layer(): pl.pallas_call(functools.partial(feature_kernel, groups, dp, rank, top),...]
    all_to_all x1, blocking collectives: 10.7 us -> 8.88 us  [layer(): lax.all_to_all(part, ('expert', 'dp'), split_axis=0, concat_axis=0, tiled...]
    ppermute x3, starting transfers between devices: 3.18 us -> 1.86 us  [layer(): lax.ppermute(pay, 'expert', [(a, a ^ k) for a in range(groups)])]
  transfers between devices with their start and end apart: 3 -> 11, of which waited for: 2 -> 5; matrix products, arithmetic and copies ran while one was open for 0% -> 0% of each run, Pallas kernels for 0% -> 11%
where the time goes in v4:
time: 50.9 us; the launch traced here: 50.6 us
  starting transfers between devices  20.4 us (40%)
  Pallas kernels  10.3 us (20%)
  waiting for transfers between devices  9.55 us (19%)
  blocking collectives  8.88 us (17%)
  local copies, waits for them, and re-layouts  0.79 us (2%)
  other arithmetic  0.68 us (1%)
    ppermute x7, starting transfers between devices, layer(): lax.ppermute(feats[k], 'dp', [(a, a ^ k) for a in range(dp)])  11.2 us
    all_to_all x1, blocking collectives, layer(): lax.all_to_all(part, ('expert', 'dp'), split_axis=0, concat_axis=0, tiled...  8.88 us
    all_to_all x1, starting transfers between devices, layer(): lax.all_to_all(val_split, 'dp', split_axis=0, concat_axis=0, tiled=True)  7.29 us
    ppermute x7, waiting for transfers between devices, layer(): lax.ppermute(feats[k], 'dp', [(a, a ^ k) for a in range(dp)])  6.08 us
    pallas_call x1, Pallas kernels, layer(): pl.pallas_call(functools.partial(feature_kernel, groups, dp, rank, top),...  5.48 us
    pallas_call x1, Pallas kernels, layer(): pl.pallas_call(act_kernel, out_shape=(jax.ShapeDtypeStruct((pay_rows, tok...  3.59 us
    ppermute x3, waiting for transfers between devices, layer(): lax.ppermute(pay, 'expert', [(a, a ^ k) for a in range(groups)])  3.47 us
    ppermute x3, starting transfers between devices, layer(): lax.ppermute(pay, 'expert', [(a, a ^ k) for a in range(groups)])  1.86 us
  transfers between devices with their start and end apart: 11, of which 5 were waited for; matrix products, arithmetic and copies ran while one was open for 0% of the time, Pallas kernels for 11%

profile of v4, /device:TPU:0, one launch (start us, length us, event | category | flops | bytes accessed | tf_op | source)
XLA Modules:
  0.0 50.6 jit_solution(6870070245916881124)
XLA Ops:
  0.0 3.6 %shard_map.82 = (f32[88,128]{1,0:T(8,128)}, bf16[8,4,16,512]{3,2,1,0:T(8,128)(2,1)}) custom-call(bf16[128,4096]{1,0:T(8,128)(2,1)} %tok_hbm.1, bf16[64,4096]{1,0:T(8,128)(2,1)} %bitcast.8, bf16[4,16,4096]{2,1,0:T(8,128)(2,1)} %val_hbm.1, s32[8,128]{1,0:T(8,128)} %bitcast.9, f32[8,128]{1,0:T(8,128)} %bitcast.10, s32[1,128]{1,0:T(1,128)} %bitcast.11), custom_call_target="tpu_custom_call" | custom-call | flops 67108864 | bytes 1572864 | tf_op jit(solution)/shard_map/pallas_call | solution.py:216
  3.6 7.3 %all-to-all-start = ((bf16[8,4,16,512]{3,2,1,0:T(8,128)(2,1)}), bf16[8,4,16,512]{3,2,1,0:T(8,128)(2,1)S(1)}, u32[]{:S(2)}, u32[]{:S(2)}) async-start(bf16[8,4,16,512]{3,2,1,0:T(8,128)(2,1)} %get-tuple-element.24), calls=%async_computation | async-start | bytes 1048576 | tf_op jit(solution)/shard_map/all_to_all | solution.py:240
  10.9 0.7 %collective-permute-start.2 = (f32[88,128]{1,0:T(8,128)}, f32[88,128]{1,0:T(8,128)S(1)}, u32[]{:S(2)}, u32[]{:S(2)}) collective-permute-start(f32[88,128]{1,0:T(8,128)} %get-tuple-element.15.refs_0_), channel_id=1, source_target_pairs={{0,24},{8,16},{16,8},{24,0},{1,25},{9,17},{17,9},{25,1},{2,26},{10... | collective-permute-start | bytes 135176 | tf_op jit(solution)/shard_map/ppermute | solution.py:244
  11.6 0.9 %collective-permute-start.1 = (f32[88,128]{1,0:T(8,128)}, f32[88,128]{1,0:T(8,128)S(1)}, u32[]{:S(2)}, u32[]{:S(2)}) collective-permute-start(f32[88,128]{1,0:T(8,128)} %get-tuple-element.15.refs_0_), channel_id=1, source_target_pairs={{0,16},{8,24},{16,0},{24,8},{1,17},{9,25},{17,1},{25,9},{2,18},{10... | collective-permute-start | bytes 135176 | tf_op jit(solution)/shard_map/ppermute | solution.py:244
  12.5 0.3 collective-permute-start
  12.8 0.1 pad_add_fusion.me_ref
  12.8 2.2 %collective-permute-done.2.refs_3_ = f32[88,128]{1,0:T(8,128)S(1)} collective-permute-done((f32[88,128]{1,0:T(8,128)}, f32[88,128]{1,0:T(8,128)S(1)}, u32[]{:S(2)}, u32[]{:S(2)}) %collective-permute-start.2) | collective-permute-done | bytes 45088 | tf_op jit(solution)/shard_map/ppermute | solution.py:244
  15.0 1.3 %collective-permute-done.1.refs_2_ = f32[88,128]{1,0:T(8,128)S(1)} collective-permute-done((f32[88,128]{1,0:T(8,128)}, f32[88,128]{1,0:T(8,128)S(1)}, u32[]{:S(2)}, u32[]{:S(2)}) %collective-permute-start.1) | collective-permute-done | bytes 45088 | tf_op jit(solution)/shard_map/ppermute | solution.py:244
  16.3 0.0 collective-permute-done.refs_1_
  16.3 0.0 copy-start
  16.3 0.8 %copy-done = f32[88,128]{1,0:T(8,128)S(1)} copy-done((f32[88,128]{1,0:T(8,128)S(1)}, f32[88,128]{1,0:T(8,128)}, u32[]{:S(2)}) %copy-start) | copy-done | bytes 45080
  17.1 5.5 %shard_map.83 = (bf16[2,4,16,128]{3,2,1,0:T(8,128)(2,1)S(1)}, bf16[2,4,16,128]{3,2,1,0:T(8,128)(2,1)S(1)}, bf16[2,4,16,128]{3,2,1,0:T(8,128)(2,1)S(1)}, bf16[2,4...) custom-call(s32[2]{0:T(128)S(1)} %pad_add_fusion.me_ref, ...), custom_call_target="tpu_custom_call" | custom-call | flops 402653184 | bytes 9437184 | tf_op jit(solution)/shard_map/pallas_call | solution.py:249
  22.6 1.5 %collective-permute-start.3 = (bf16[2,4,16,128]{3,2,1,0:T(8,128)(2,1)S(1)}, bf16[2,4,16,128]{3,2,1,0:T(8,128)(2,1)S(1)}, u32[]{:S(2)}, u32[]{:S(2)}) collective-permute-start(bf16[2,4,16,128]{3,2,1,0:T(8,128)(2,1)S(1)} %get-tuple-element.17), channel_id=1, source_target_pairs={{0,1},{1,0},{2,3},{3,2},{4,5},{5,4},{6,7},{7,6},{8,9},{9,8},{10,11... | collective-permute-start | bytes 98312 | tf_op jit(solution)/shard_map/ppermute | solution.py:271
  24.1 1.5 %collective-permute-start.4 = (bf16[2,4,16,128]{3,2,1,0:T(8,128)(2,1)S(1)}, bf16[2,4,16,128]{3,2,1,0:T(8,128)(2,1)S(1)}, u32[]{:S(2)}, u32[]{:S(2)}) collective-permute-start(bf16[2,4,16,128]{3,2,1,0:T(8,128)(2,1)S(1)} %get-tuple-element.18), channel_id=1, source_target_pairs={{0,2},{1,3},{2,0},{3,1},{4,6},{5,7},{6,4},{7,5},{8,10},{9,11},{10,... | collective-permute-start | bytes 98312 | tf_op jit(solution)/shard_map/ppermute | solution.py:271
  25.6 0.5 %collective-permute-start.5 = (bf16[2,4,16,128]{3,2,1,0:T(8,128)(2,1)S(1)}, bf16[2,4,16,128]{3,2,1,0:T(8,128)(2,1)S(1)}, u32[]{:S(2)}, u32[]{:S(2)}) collective-permute-start(bf16[2,4,16,128]{3,2,1,0:T(8,128)(2,1)S(1)} %get-tuple-element.19), channel_id=1, source_target_pairs={{0,3},{1,2},{2,1},{3,0},{4,7},{5,6},{6,5},{7,4},{8,11},{9,10},{10,... | collective-permute-start | bytes 98312 | tf_op jit(solution)/shard_map/ppermute | solution.py:271
  26.1 2.4 %collective-permute-start.6 = (bf16[2,4,16,128]{3,2,1,0:T(8,128)(2,1)S(1)}, bf16[2,4,16,128]{3,2,1,0:T(8,128)(2,1)S(1)}, u32[]{:S(2)}, u32[]{:S(2)}) collective-permute-start(bf16[2,4,16,128]{3,2,1,0:T(8,128)(2,1)S(1)} %get-tuple-element.20), channel_id=1, source_target_pairs={{0,4},{1,5},{2,6},{3,7},{4,0},{5,1},{6,2},{7,3},{8,12},{9,13},{10,... | collective-permute-start | bytes 98312 | tf_op jit(solution)/shard_map/ppermute | solution.py:271
  28.5 1.5 %collective-permute-start.7 = (bf16[2,4,16,128]{3,2,1,0:T(8,128)(2,1)S(1)}, bf16[2,4,16,128]{3,2,1,0:T(8,128)(2,1)S(1)}, u32[]{:S(2)}, u32[]{:S(2)}) collective-permute-start(bf16[2,4,16,128]{3,2,1,0:T(8,128)(2,1)S(1)} %get-tuple-element.21), channel_id=1, source_target_pairs={{0,5},{1,4},{2,7},{3,6},{4,1},{5,0},{6,3},{7,2},{8,13},{9,12},{10,... | collective-permute-start | bytes 98312 | tf_op jit(solution)/shard_map/ppermute | solution.py:271
  30.0 0.0 collective-permute-done.3.refs_1_
  30.0 3.3 %collective-permute-start.8 = (bf16[2,4,16,128]{3,2,1,0:T(8,128)(2,1)S(1)}, bf16[2,4,16,128]{3,2,1,0:T(8,128)(2,1)S(1)}, u32[]{:S(2)}, u32[]{:S(2)}) collective-permute-start(bf16[2,4,16,128]{3,2,1,0:T(8,128)(2,1)S(1)} %get-tuple-element.22), channel_id=1, source_target_pairs={{0,6},{1,7},{2,4},{3,5},{4,2},{5,3},{6,0},{7,1},{8,14},{9,15},{10,... | collective-permute-start | bytes 98312 | tf_op jit(solution)/shard_map/ppermute | solution.py:271
  33.3 0.0 collective-permute-done.4.refs_2_
  33.3 0.5 %collective-permute-start.9 = (bf16[2,4,16,128]{3,2,1,0:T(8,128)(2,1)S(1)}, bf16[2,4,16,128]{3,2,1,0:T(8,128)(2,1)S(1)}, u32[]{:S(2)}, u32[]{:S(2)}) collective-permute-start(bf16[2,4,16,128]{3,2,1,0:T(8,128)(2,1)S(1)} %get-tuple-element.23), channel_id=1, source_target_pairs={{0,7},{1,6},{2,5},{3,4},{4,3},{5,2},{6,1},{7,0},{8,15},{9,14},{10,... | collective-permute-start | bytes 98312 | tf_op jit(solution)/shard_map/ppermute | solution.py:271
  33.8 0.0 collective-permute-done.5.refs_3_
  33.8 0.0 collective-permute-done.6.refs_4_
  33.8 0.5 collective-permute-done.7.refs_5_
  34.3 1.4 %collective-permute-done.8.refs_6_ = bf16[2,4,16,128]{3,2,1,0:T(8,128)(2,1)S(1)} collective-permute-done((bf16[2,4,16,128]{3,2,1,0:T(8,128)(2,1)S(1)}, bf16[2,4,16,128]{3,2,1,0:T(8,128)(2,1)S(1)}, u32[]{:S(2)}, u32[]{:S(2)}) %collective-permute-start.8) | collective-permute-done | bytes 32800 | tf_op jit(solution)/shard_map/ppermute | solution.py:271
  35.7 4.2 %collective-permute-done.9.refs_7_ = bf16[2,4,16,128]{3,2,1,0:T(8,128)(2,1)S(1)} collective-permute-done((bf16[2,4,16,128]{3,2,1,0:T(8,128)(2,1)S(1)}, bf16[2,4,16,128]{3,2,1,0:T(8,128)(2,1)S(1)}, u32[]{:S(2)}, u32[]{:S(2)}) %collective-permute-start.9) | collective-permute-done | bytes 32800 | tf_op jit(solution)/shard_map/ppermute | solution.py:271
  39.9 0.0 all-to-all-done.refs_8_
  39.9 1.2 %shard_map.84 = f32[32,2,32]{2,1,0:T(2,128)S(1)} custom-call(s32[2]{0:T(128)S(1)} %pad_add_fusion.me_ref, bf16[2,4,16,128]{3,2,1,0:T(8,128)(2,1)S(1)} %get-tuple-element.16.refs_0_, bf16[2,4,16,128]{3,2,1,0:T(8,128)(2,1)S(1)} %collective-permute-done.3.refs_1_, bf16[2,4,16,128]{3,2,1,0:T(8,128)(2,1)S(1)} %collective-permute-done.4.refs_2_, ...), custom_call_target="tpu_custom_call" | custom-call | tf_op jit(solution)/shard_map/pallas_call | solution.py:274
  41.1 8.9 %all_to_all.10 = f32[32,2,32]{2,1,0:T(2,128)S(1)} all-to-all(f32[32,2,32]{2,1,0:T(2,128)S(1)} %shard_map.84), channel_id=1, replica_groups=mesh['expert'=4,'dp'=8] {'expert','dp'}, dimensions={0} | all-to-all | bytes 16384 | tf_op jit(solution)/shard_map/all_to_all | solution.py:281
  50.0 0.6 %reduce_sum.9 = f32[2,32]{1,0:T(2,128)} reduce(f32[32,2,32]{2,1,0:T(2,128)S(1)} %all_to_all.10, f32[]{:T(128)} %constant.9.clone.1), dimensions={0}, to_apply=%region_0.0 | reduce | flops 1984 | bytes 8452 | tf_op jit(solution)/shard_map/reduce_sum | solution.py:282
Async XLA Ops:
  3.6 36.3 %all-to-all-start = ((bf16[8,4,16,512]{3,2,1,0:T(8,128)(2,1)}), bf16[8,4,16,512]{3,2,1,0:T(8,128)(2,1)S(1)}, u32[]{:S(2)}, u32[]{:S(2)}) async-start(bf16[8,4,16,512]{3,2,1,0:T(8,128)(2,1)} %get-tuple-element.24), calls=%async_computation | async-start | bytes 1048576 | tf_op jit(solution)/shard_map/all_to_all | solution.py:240
  10.9 4.1 %collective-permute-start.2 = (f32[88,128]{1,0:T(8,128)}, f32[88,128]{1,0:T(8,128)S(1)}, u32[]{:S(2)}, u32[]{:S(2)}) collective-permute-start(f32[88,128]{1,0:T(8,128)} %get-tuple-element.15.refs_0_), channel_id=1, source_target_pairs={{0,24},{8,16},{16,8},{24,0},{1,25},{9,17},{17,9},{25,1},{2,26},{10... | collective-permute-start | bytes 135176 | tf_op jit(solution)/shard_map/ppermute | solution.py:244
  11.6 4.7 %collective-permute-start.1 = (f32[88,128]{1,0:T(8,128)}, f32[88,128]{1,0:T(8,128)S(1)}, u32[]{:S(2)}, u32[]{:S(2)}) collective-permute-start(f32[88,128]{1,0:T(8,128)} %get-tuple-element.15.refs_0_), channel_id=1, source_target_pairs={{0,16},{8,24},{16,0},{24,8},{1,17},{9,25},{17,1},{25,9},{2,18},{10... | collective-permute-start | bytes 135176 | tf_op jit(solution)/shard_map/ppermute | solution.py:244
  12.5 3.8 %collective-permute-start = (f32[88,128]{1,0:T(8,128)}, f32[88,128]{1,0:T(8,128)S(1)}, u32[]{:S(2)}, u32[]{:S(2)}) collective-permute-start(f32[88,128]{1,0:T(8,128)} %get-tuple-element.15.refs_0_), channel_id=1, source_target_pairs={{0,8},{8,0},{16,24},{24,16},{1,9},{9,1},{17,25},{25,17},{2,10},{10... | collective-permute-start | bytes 135176 | tf_op jit(solution)/shard_map/ppermute | solution.py:244
  16.3 0.8 %copy-start = (f32[88,128]{1,0:T(8,128)S(1)}, f32[88,128]{1,0:T(8,128)}, u32[]{:S(2)}) copy-start(f32[88,128]{1,0:T(8,128)} %get-tuple-element.15.refs_0_) | copy-start | bytes 135172
  22.6 7.4 %collective-permute-start.3 = (bf16[2,4,16,128]{3,2,1,0:T(8,128)(2,1)S(1)}, bf16[2,4,16,128]{3,2,1,0:T(8,128)(2,1)S(1)}, u32[]{:S(2)}, u32[]{:S(2)}) collective-permute-start(bf16[2,4,16,128]{3,2,1,0:T(8,128)(2,1)S(1)} %get-tuple-element.17), channel_id=1, source_target_pairs={{0,1},{1,0},{2,3},{3,2},{4,5},{5,4},{6,7},{7,6},{8,9},{9,8},{10,11... | collective-permute-start | bytes 98312 | tf_op jit(solution)/shard_map/ppermute | solution.py:271
  24.1 9.1 %collective-permute-start.4 = (bf16[2,4,16,128]{3,2,1,0:T(8,128)(2,1)S(1)}, bf16[2,4,16,128]{3,2,1,0:T(8,128)(2,1)S(1)}, u32[]{:S(2)}, u32[]{:S(2)}) collective-permute-start(bf16[2,4,16,128]{3,2,1,0:T(8,128)(2,1)S(1)} %get-tuple-element.18), channel_id=1, source_target_pairs={{0,2},{1,3},{2,0},{3,1},{4,6},{5,7},{6,4},{7,5},{8,10},{9,11},{10,... | collective-permute-start | bytes 98312 | tf_op jit(solution)/shard_map/ppermute | solution.py:271
  25.6 8.2 %collective-permute-start.5 = (bf16[2,4,16,128]{3,2,1,0:T(8,128)(2,1)S(1)}, bf16[2,4,16,128]{3,2,1,0:T(8,128)(2,1)S(1)}, u32[]{:S(2)}, u32[]{:S(2)}) collective-permute-start(bf16[2,4,16,128]{3,2,1,0:T(8,128)(2,1)S(1)} %get-tuple-element.19), channel_id=1, source_target_pairs={{0,3},{1,2},{2,1},{3,0},{4,7},{5,6},{6,5},{7,4},{8,11},{9,10},{10,... | collective-permute-start | bytes 98312 | tf_op jit(solution)/shard_map/ppermute | solution.py:271
  26.1 7.7 %collective-permute-start.6 = (bf16[2,4,16,128]{3,2,1,0:T(8,128)(2,1)S(1)}, bf16[2,4,16,128]{3,2,1,0:T(8,128)(2,1)S(1)}, u32[]{:S(2)}, u32[]{:S(2)}) collective-permute-start(bf16[2,4,16,128]{3,2,1,0:T(8,128)(2,1)S(1)} %get-tuple-element.20), channel_id=1, source_target_pairs={{0,4},{1,5},{2,6},{3,7},{4,0},{5,1},{6,2},{7,3},{8,12},{9,13},{10,... | collective-permute-start | bytes 98312 | tf_op jit(solution)/shard_map/ppermute | solution.py:271
  28.5 5.8 %collective-permute-start.7 = (bf16[2,4,16,128]{3,2,1,0:T(8,128)(2,1)S(1)}, bf16[2,4,16,128]{3,2,1,0:T(8,128)(2,1)S(1)}, u32[]{:S(2)}, u32[]{:S(2)}) collective-permute-start(bf16[2,4,16,128]{3,2,1,0:T(8,128)(2,1)S(1)} %get-tuple-element.21), channel_id=1, source_target_pairs={{0,5},{1,4},{2,7},{3,6},{4,1},{5,0},{6,3},{7,2},{8,13},{9,12},{10,... | collective-permute-start | bytes 98312 | tf_op jit(solution)/shard_map/ppermute | solution.py:271
  30.0 5.7 %collective-permute-start.8 = (bf16[2,4,16,128]{3,2,1,0:T(8,128)(2,1)S(1)}, bf16[2,4,16,128]{3,2,1,0:T(8,128)(2,1)S(1)}, u32[]{:S(2)}, u32[]{:S(2)}) collective-permute-start(bf16[2,4,16,128]{3,2,1,0:T(8,128)(2,1)S(1)} %get-tuple-element.22), channel_id=1, source_target_pairs={{0,6},{1,7},{2,4},{3,5},{4,2},{5,3},{6,0},{7,1},{8,14},{9,15},{10,... | collective-permute-start | bytes 98312 | tf_op jit(solution)/shard_map/ppermute | solution.py:271
  33.3 6.6 %collective-permute-start.9 = (bf16[2,4,16,128]{3,2,1,0:T(8,128)(2,1)S(1)}, bf16[2,4,16,128]{3,2,1,0:T(8,128)(2,1)S(1)}, u32[]{:S(2)}, u32[]{:S(2)}) collective-permute-start(bf16[2,4,16,128]{3,2,1,0:T(8,128)(2,1)S(1)} %get-tuple-element.23), channel_id=1, source_target_pairs={{0,7},{1,6},{2,5},{3,4},{4,3},{5,2},{6,1},{7,0},{8,15},{9,14},{10,... | collective-permute-start | bytes 98312 | tf_op jit(solution)/shard_map/ppermute | solution.py:271

commit v5 on v4

--- a/solution.py
+++ b/solution.py
@@ -10,17 +10,30 @@
 
 DOC_GRP = 2
 LANES = 128
-VL_F = 53 << 20
+VL_S = 53 << 20
+VL_A = 63 << 20
+VL_L = 53 << 20
+VL_F = 16 << 20
 F32 = jnp.float32
 BF16 = jnp.bfloat16
 NT = (((1,), (1,)), ((), ()))
 TN = (((0,), (0,)), ((), ()))
 
 
-def act_kernel(
-    tok_hbm, proj_hbm, val_hbm, routes_ref, gates_ref, docs_ref, out_ref, split_ref, *scratch
-):
-    tok_ref, proj_ref, acc_ref, piece_ref, sems, split_sems = scratch
+def split_kernel(val_hbm, out_ref, sems):
+    parts, _, _, piece = out_ref.shape
+    copies = [
+        pltpu.make_async_copy(val_hbm.at[:, :, pl.ds(j * piece, piece)], out_ref.at[j], sems.at[j])
+        for j in range(parts)
+    ]
+    for copy in copies:
+        copy.start()
+    for copy in copies:
+        copy.wait()
+
+
+def act_kernel(tok_hbm, proj_hbm, routes_hbm, gates_hbm, docs_hbm, out_ref, *scratch):
+    tok_ref, proj_ref, routes_ref, gates_ref, docs_ref, acc_ref, sems, small_sems = scratch
     rank = proj_ref.shape[0]
     top = routes_ref.shape[0]
     half = rank // 2
@@ -35,27 +48,25 @@
                 pltpu.make_async_copy(tok_hbm.at[:, cols], tok_ref.at[:, cols], sems.at[s, 1]),
             )
         )
-    parts, _, _, piece = piece_ref.shape
-    splits = [
-        pltpu.make_async_copy(
-            val_hbm.at[:, :, pl.ds(j * piece, piece)], piece_ref.at[j], split_sems.at[j]
-        )
-        for j in range(parts)
+    smalls = [
+        pltpu.make_async_copy(routes_hbm, routes_ref, small_sems.at[0]),
+        pltpu.make_async_copy(gates_hbm, gates_ref, small_sems.at[1]),
+        pltpu.make_async_copy(docs_hbm, docs_ref, small_sems.at[2]),
     ]
-    whole = pltpu.make_async_copy(piece_ref, split_ref, split_sems.at[parts])
-    for copy in splits:
+    for copy in copies[0]:
         copy.start()
-    for pair in copies:
+    for copy in smalls:
+        copy.start()
+    for pair in copies[1:]:
         for copy in pair:
             copy.start()
+    for copy in smalls:
+        copy.wait()
     out_ref[rank : rank + top, :] = routes_ref[...].astype(F32)
     out_ref[rank + top : rank + 2 * top, :] = gates_ref[...]
     out_ref[rank + 2 * top :, :] = jnp.broadcast_to(
         docs_ref[...].astype(F32), (out_ref.shape[0] - rank - 2 * top, out_ref.shape[1])
     )
-    for copy in splits:
-        copy.wait()
-    whole.start()
     total = jnp.zeros(acc_ref.shape, F32)
     for s in range(steps):
         for copy in copies[s]:
@@ -67,18 +78,13 @@
     acc_ref[...] = total
     out_ref[0:half, :] = acc_ref[pl.ds(0, half, stride=2), :]
     out_ref[half:rank, :] = acc_ref[pl.ds(1, half, stride=2), :]
-    whole.wait()
-
-
-def feature_kernel(groups, parts, rank, top, me_ref, *refs):
-    pays = refs[:groups]
-    grad_hbm, proj_hbm = refs[groups : groups + 2]
-    outs = refs[groups + 2 : groups + 2 + parts]
-    a_ref, low_ref, f_ref, grad_ref, proj_ref, sems = refs[groups + 2 + parts :]
-    exp_local, rows, _ = grad_ref.shape
-    batch = exp_local // sems.shape[0]
+
+
+def lowered_kernel(grad_hbm, proj_hbm, out_ref, grad_ref, proj_ref, sems):
+    count = sems.shape[0]
+    batch = grad_ref.shape[0] // count
     copies = []
-    for n in range(sems.shape[0]):
+    for n in range(count):
         part = pl.ds(n * batch, batch)
         copies.append(
             (
@@ -89,6 +95,20 @@
     for pair in copies:
         for copy in pair:
             copy.start()
+    for n in range(count):
+        for copy in copies[n]:
+            copy.wait()
+        for e in range(n * batch, (n + 1) * batch):
+            low = lax.dot_general(grad_ref[e], proj_ref[e], NT, preferred_element_type=F32)
+            out_ref[e] = jnp.concatenate([low, low], axis=1).astype(BF16)
+
+
+def feature_kernel(groups, parts, rank, top, me_ref, *refs):
+    pays = refs[:groups]
+    low_ref = refs[groups]
+    outs = refs[groups + 1 : groups + 1 + parts]
+    a_ref, f_ref = refs[groups + 1 + parts :]
+    exp_local, rows, _ = low_ref.shape
     cap = rows // groups
     tok = pays[0].shape[1]
     half = rank // 2
@@ -137,26 +157,11 @@
             a_ref[e, pl.ds(source, cap), :] = sent[e * cap : (e + 1) * cap, :]
     wide = DOC_GRP * half
     lane = lax.broadcasted_iota(jnp.int32, (wide, 2 * rank), 1)
-
-    def project(n):
-        for copy in copies[n]:
-            copy.wait()
-        for e in range(n * batch, (n + 1) * batch):
-            low = lax.dot_general(grad_ref[e], proj_ref[e], NT, preferred_element_type=F32)
-            low_ref[e] = jnp.concatenate([low, low], axis=1).astype(BF16)
-
-    def outer(n):
-        for e in range(n * batch, (n + 1) * batch):
-            feat = lax.dot_general(a_ref[e], low_ref[e], TN, preferred_element_type=F32)
-            f_ref[pl.ds(e, wide, stride=exp_local), :] = jnp.where(
-                lane < rank, feat[:wide], feat[wide:]
-            )
-
-    for n in range(sems.shape[0]):
-        project(n)
-        if n:
-            outer(n - 1)
-    outer(sems.shape[0] - 1)
+    for e in range(exp_local):
+        feat = lax.dot_general(a_ref[e], low_ref[e], TN, preferred_element_type=F32)
+        f_ref[pl.ds(e, wide, stride=exp_local), :] = jnp.where(
+            lane < rank, feat[:wide], feat[wide:]
+        )
     _, chunks, _, _ = outs[0].shape
     size = chunks * exp_local
     for k in range(parts):
@@ -211,37 +216,62 @@
 
     vmem = pl.BlockSpec(memory_space=pltpu.VMEM)
     hbm = pl.BlockSpec(memory_space=pltpu.HBM)
+    val_split = pl.pallas_call(
+        split_kernel,
+        out_shape=jax.ShapeDtypeStruct((dp, vals, exp_local, entries // dp), BF16),
+        in_specs=[hbm],
+        out_specs=vmem,
+        scratch_shapes=[pltpu.SemaphoreType.DMA((dp,))],
+        compiler_params=pltpu.CompilerParams(vmem_limit_bytes=VL_S),
+    )(val_features)
+    val_all = lax.all_to_all(val_split, "dp", split_axis=0, concat_axis=0, tiled=True)
+
     pay_rows = rank + 2 * top + 8
     steps = 2
-    pay, val_split = pl.pallas_call(
+    pay = pl.pallas_call(
         act_kernel,
-        out_shape=(
-            jax.ShapeDtypeStruct((pay_rows, tok), F32),
-            jax.ShapeDtypeStruct((dp, vals, exp_local, entries // dp), BF16),
-        ),
-        in_specs=[hbm, hbm, hbm, vmem, vmem, vmem],
-        out_specs=(vmem, hbm),
+        out_shape=jax.ShapeDtypeStruct((pay_rows, tok), F32),
+        in_specs=[hbm] * 5,
+        out_specs=vmem,
         scratch_shapes=[
             pltpu.VMEM((tok, width), BF16),
             pltpu.VMEM((rank, width), BF16),
+            pltpu.VMEM((top, tok), jnp.int32),
+            pltpu.VMEM((top, tok), F32),
+            pltpu.VMEM((1, tok), jnp.int32),
             pltpu.VMEM((rank, tok), F32),
-            pltpu.VMEM((dp, vals, exp_local, entries // dp), BF16),
             pltpu.SemaphoreType.DMA((steps, 2)),
-            pltpu.SemaphoreType.DMA((dp + 1,)),
+            pltpu.SemaphoreType.DMA((3,)),
         ],
-        compiler_params=pltpu.CompilerParams(vmem_limit_bytes=63 << 20),
+        compiler_params=pltpu.CompilerParams(vmem_limit_bytes=VL_A),
         cost_estimate=pl.CostEstimate(
             flops=2 * tok * width * rank,
             bytes_accessed=2 * width * (tok + rank),
             transcendentals=0,
         ),
-    )(tokens, proj_in.T, val_features, routes.T, gates.T, doc_ids.reshape(1, tok))
-
-    val_all = lax.all_to_all(val_split, "dp", split_axis=0, concat_axis=0, tiled=True)
+    )(tokens, proj_in.T, routes.T, gates.T, doc_ids.reshape(1, tok))
 
     pays = [pay]
     for k in range(1, groups):
         pays.append(lax.ppermute(pay, "expert", [(a, a ^ k) for a in range(groups)]))
+
+    low = pl.pallas_call(
+        lowered_kernel,
+        out_shape=jax.ShapeDtypeStruct((exp_local, rows, 2 * rank), BF16),
+        in_specs=[hbm, hbm],
+        out_specs=vmem,
+        scratch_shapes=[
+            pltpu.VMEM((exp_local, rows, hidden), BF16),
+            pltpu.VMEM((exp_local, rank, hidden), BF16),
+            pltpu.SemaphoreType.DMA((4, 2)),
+        ],
+        compiler_params=pltpu.CompilerParams(vmem_limit_bytes=VL_L),
+        cost_estimate=pl.CostEstimate(
+            flops=2 * exp_local * rows * hidden * rank,
+            bytes_accessed=2 * exp_local * hidden * (rows + rank),
+            transcendentals=0,
+        ),
+    )(hidden_grad, proj_out.transpose(0, 2, 1))
 
     me = jnp.stack([lax.axis_index("expert"), lax.axis_index("dp")]).astype(jnp.int32)
     smem = pl.BlockSpec(memory_space=pltpu.SMEM)
@@ -249,23 +279,17 @@
     feats = pl.pallas_call(
         functools.partial(feature_kernel, groups, dp, rank, top),
         out_shape=(block,) * dp,
-        in_specs=[smem] + [vmem] * groups + [hbm, hbm],
+        in_specs=[smem] + [vmem] * (groups + 1),
         out_specs=(vmem,) * dp,
         scratch_shapes=[
             pltpu.VMEM((exp_local, rows, 2 * rank), BF16),
-            pltpu.VMEM((exp_local, rows, 2 * rank), BF16),
             pltpu.VMEM((DOC_GRP * rank // 2 * exp_local, 2 * rank), F32),
-            pltpu.VMEM((exp_local, rows, hidden), BF16),
-            pltpu.VMEM((exp_local, rank, hidden), BF16),
-            pltpu.SemaphoreType.DMA((4, 2)),
         ],
         compiler_params=pltpu.CompilerParams(vmem_limit_bytes=VL_F),
         cost_estimate=pl.CostEstimate(
-            flops=2 * exp_local * rows * hidden * rank,
-            bytes_accessed=2 * exp_local * hidden * (rows + rank),
-            transcendentals=0,
+            flops=8 * exp_local * rows * rank * tok, bytes_accessed=1 << 20, transcendentals=0
         ),
-    )(me, *pays, hidden_grad, proj_out.transpose(0, 2, 1))
+    )(me, *pays, low)
     arrived = [feats[0]]
     for k in range(1, dp):
         arrived.append(lax.ppermute(feats[k], "dp", [(a, a ^ k) for a in range(dp)]))

time: 50.9 us -> 49.1 us (0.965)
  waiting for transfers between devices: 9.55 us -> 6.55 us
  Pallas kernels: 10.3 us -> 12.1 us
  local copies, waits for them, and re-layouts: 0.79 us -> 0.01 us
    pallas_call x1 -> x3, Pallas kernels: 3.59 us -> 8.93 us  [the longest x1 4.44 us: layer(): pl.pallas_call(lowered_kernel, out_shape=jax.ShapeDtypeStruct((exp_local,...]
    pallas_call x1, Pallas kernels: 5.48 us -> 1.9 us  [layer(): pl.pallas_call(functools.partial(feature_kernel, groups, dp, rank, top),...]
    ppermute x3, waiting for transfers between devices: 3.47 us -> 0.01 us  [layer(): lax.ppermute(pay, 'expert', [(a, a ^ k) for a in range(groups)])]
    unnamed x2, local copies, waits for them, and re-layouts: 0.79 us -> 0.01 us
  transfers between devices with their start and end apart: 11 -> 11, of which waited for: 5 -> 3; matrix products, arithmetic and copies ran while one was open for 0% -> 0% of each run, Pallas kernels for 11% -> 18%
where the time goes in v5:
time: 49.1 us; the launch traced here: 48.8 us
  starting transfers between devices  20.5 us (42%)
  Pallas kernels  12.1 us (25%)
  blocking collectives  8.89 us (18%)
  waiting for transfers between devices  6.55 us (13%)
  other arithmetic  0.68 us (1%)
    ppermute x7, starting transfers between devices, layer(): lax.ppermute(feats[k], 'dp', [(a, a ^ k) for a in range(dp)])  11.3 us
    all_to_all x1, blocking collectives, layer(): lax.all_to_all(part, ('expert', 'dp'), split_axis=0, concat_axis=0, tiled...  8.89 us
    all_to_all x1, starting transfers between devices, layer(): lax.all_to_all(val_split, 'dp', split_axis=0, concat_axis=0, tiled=True)  7.29 us
    ppermute x7, waiting for transfers between devices, layer(): lax.ppermute(feats[k], 'dp', [(a, a ^ k) for a in range(dp)])  6.54 us
    pallas_call x1, Pallas kernels, layer(): pl.pallas_call(lowered_kernel, out_shape=jax.ShapeDtypeStruct((exp_local,...  4.44 us
    pallas_call x1, Pallas kernels, layer(): pl.pallas_call(act_kernel, out_shape=jax.ShapeDtypeStruct((pay_rows, tok)...  2.57 us
    ppermute x3, starting transfers between devices, layer(): lax.ppermute(pay, 'expert', [(a, a ^ k) for a in range(groups)])  1.93 us
    pallas_call x1, Pallas kernels, layer(): pl.pallas_call(split_kernel, out_shape=jax.ShapeDtypeStruct((dp, vals, ex...  1.92 us
  transfers between devices with their start and end apart: 11, of which 3 were waited for; matrix products, arithmetic and copies ran while one was open for 0% of the time, Pallas kernels for 18%

profile of v5, /device:TPU:0, one launch (start us, length us, event | category | flops | bytes accessed | tf_op | source)
XLA Modules:
  0.0 48.8 jit_solution(14333101327037506292)
XLA Ops:
  0.0 1.9 %shard_map.85 = bf16[8,4,16,512]{3,2,1,0:T(8,128)(2,1)} custom-call(bf16[4,16,4096]{2,1,0:T(8,128)(2,1)} %val_hbm.1), custom_call_target="tpu_custom_call" | custom-call | tf_op jit(solution)/shard_map/pallas_call | solution.py:219
  1.9 7.3 %all-to-all-start = ((bf16[8,4,16,512]{3,2,1,0:T(8,128)(2,1)}), bf16[8,4,16,512]{3,2,1,0:T(8,128)(2,1)S(1)}, u32[]{:S(2)}, u32[]{:S(2)}) async-start(bf16[8,4,16,512]{3,2,1,0:T(8,128)(2,1)} %shard_map.85), calls=%async_computation | async-start | bytes 1048576 | tf_op jit(solution)/shard_map/all_to_all | solution.py:227
  9.2 2.6 %shard_map.82.refs_0_ = f32[88,128]{1,0:T(8,128)} custom-call(bf16[128,4096]{1,0:T(8,128)(2,1)} %tok_hbm.1, bf16[64,4096]{1,0:T(8,128)(2,1)} %bitcast.8, s32[8,128]{1,0:T(8,128)} %bitcast.9, f32[8,128]{1,0:T(8,128)} %bitcast.10, s32[1,128]{1,0:T(1,128)} %bitcast.11), custom_call_target="tpu_custom_call" | custom-call | flops 67108864 | bytes 1572864 | tf_op jit(solution)/shard_map/pallas_call | solution.py:231
  11.8 0.0 copy-start
  11.8 0.7 %collective-permute-start.2 = (f32[88,128]{1,0:T(8,128)}, f32[88,128]{1,0:T(8,128)S(1)}, u32[]{:S(2)}, u32[]{:S(2)}) collective-permute-start(f32[88,128]{1,0:T(8,128)} %shard_map.82.refs_0_), channel_id=1, source_target_pairs={{0,24},{8,16},{16,8},{24,0},{1,25},{9,17},{17,9},{25,1},{2,26},{10... | collective-permute-start | bytes 135176 | tf_op jit(solution)/shard_map/ppermute | solution.py:256
  12.6 0.9 %collective-permute-start.1 = (f32[88,128]{1,0:T(8,128)}, f32[88,128]{1,0:T(8,128)S(1)}, u32[]{:S(2)}, u32[]{:S(2)}) collective-permute-start(f32[88,128]{1,0:T(8,128)} %shard_map.82.refs_0_), channel_id=1, source_target_pairs={{0,16},{8,24},{16,0},{24,8},{1,17},{9,25},{17,1},{25,9},{2,18},{10... | collective-permute-start | bytes 135176 | tf_op jit(solution)/shard_map/ppermute | solution.py:256
  13.5 0.3 collective-permute-start
  13.7 0.1 pad_add_fusion.me_ref
  13.8 4.4 %shard_map.83.refs_4_ = bf16[16,128,128]{2,1,0:T(8,128)(2,1)S(1)} custom-call(bf16[16,128,1536]{2,1,0:T(8,128)(2,1)} %grad_hbm.1, bf16[16,64,1536]{2,1,0:T(8,128)(2,1)} %bitcast.7), custom_call_target="tpu_custom_call" | custom-call | flops 402653184 | bytes 9437184 | tf_op jit(solution)/shard_map/pallas_call | solution.py:258
  18.3 0.0 collective-permute-done.2.refs_3_
  18.3 0.0 collective-permute-done.1.refs_2_
  18.3 0.0 collective-permute-done.refs_1_
  18.3 0.0 copy-done
  18.3 1.9 %shard_map.84 = (bf16[2,4,16,128]{3,2,1,0:T(8,128)(2,1)S(1)}, bf16[2,4,16,128]{3,2,1,0:T(8,128)(2,1)S(1)}, bf16[2,4,16,128]{3,2,1,0:T(8,128)(2,1)S(1)}, bf16[2,4...) custom-call(s32[2]{0:T(128)S(1)} %pad_add_fusion.me_ref, ...), custom_call_target="tpu_custom_call" | custom-call | flops 134217728 | bytes 1048576 | tf_op jit(solution)/shard_map/pallas_call | solution.py:279
  20.2 2.1 %collective-permute-start.3 = (bf16[2,4,16,128]{3,2,1,0:T(8,128)(2,1)S(1)}, bf16[2,4,16,128]{3,2,1,0:T(8,128)(2,1)S(1)}, u32[]{:S(2)}, u32[]{:S(2)}) collective-permute-start(bf16[2,4,16,128]{3,2,1,0:T(8,128)(2,1)S(1)} %get-tuple-element.14), channel_id=1, source_target_pairs={{0,1},{1,0},{2,3},{3,2},{4,5},{5,4},{6,7},{7,6},{8,9},{9,8},{10,11... | collective-permute-start | bytes 98312 | tf_op jit(solution)/shard_map/ppermute | solution.py:295
  22.3 1.5 %collective-permute-start.4 = (bf16[2,4,16,128]{3,2,1,0:T(8,128)(2,1)S(1)}, bf16[2,4,16,128]{3,2,1,0:T(8,128)(2,1)S(1)}, u32[]{:S(2)}, u32[]{:S(2)}) collective-permute-start(bf16[2,4,16,128]{3,2,1,0:T(8,128)(2,1)S(1)} %get-tuple-element.15), channel_id=1, source_target_pairs={{0,2},{1,3},{2,0},{3,1},{4,6},{5,7},{6,4},{7,5},{8,10},{9,11},{10,... | collective-permute-start | bytes 98312 | tf_op jit(solution)/shard_map/ppermute | solution.py:295
  23.8 0.1 collective-permute-start.5
  23.8 2.8 %collective-permute-start.6 = (bf16[2,4,16,128]{3,2,1,0:T(8,128)(2,1)S(1)}, bf16[2,4,16,128]{3,2,1,0:T(8,128)(2,1)S(1)}, u32[]{:S(2)}, u32[]{:S(2)}) collective-permute-start(bf16[2,4,16,128]{3,2,1,0:T(8,128)(2,1)S(1)} %get-tuple-element.17), channel_id=1, source_target_pairs={{0,4},{1,5},{2,6},{3,7},{4,0},{5,1},{6,2},{7,3},{8,12},{9,13},{10,... | collective-permute-start | bytes 98312 | tf_op jit(solution)/shard_map/ppermute | solution.py:295
  26.7 1.5 %collective-permute-start.7 = (bf16[2,4,16,128]{3,2,1,0:T(8,128)(2,1)S(1)}, bf16[2,4,16,128]{3,2,1,0:T(8,128)(2,1)S(1)}, u32[]{:S(2)}, u32[]{:S(2)}) collective-permute-start(bf16[2,4,16,128]{3,2,1,0:T(8,128)(2,1)S(1)} %get-tuple-element.18), channel_id=1, source_target_pairs={{0,5},{1,4},{2,7},{3,6},{4,1},{5,0},{6,3},{7,2},{8,13},{9,12},{10,... | collective-permute-start | bytes 98312 | tf_op jit(solution)/shard_map/ppermute | solution.py:295
  28.1 0.0 collective-permute-done.3.refs_1_
  28.2 3.3 %collective-permute-start.8 = (bf16[2,4,16,128]{3,2,1,0:T(8,128)(2,1)S(1)}, bf16[2,4,16,128]{3,2,1,0:T(8,128)(2,1)S(1)}, u32[]{:S(2)}, u32[]{:S(2)}) collective-permute-start(bf16[2,4,16,128]{3,2,1,0:T(8,128)(2,1)S(1)} %get-tuple-element.19), channel_id=1, source_target_pairs={{0,6},{1,7},{2,4},{3,5},{4,2},{5,3},{6,0},{7,1},{8,14},{9,15},{10,... | collective-permute-start | bytes 98312 | tf_op jit(solution)/shard_map/ppermute | solution.py:295
  31.4 0.0 collective-permute-done.4.refs_2_
  31.4 0.1 collective-permute-start.9
  31.5 0.0 collective-permute-done.5.refs_3_
  31.5 0.0 collective-permute-done.6.refs_4_
  31.5 0.9 %collective-permute-done.7.refs_5_ = bf16[2,4,16,128]{3,2,1,0:T(8,128)(2,1)S(1)} collective-permute-done((bf16[2,4,16,128]{3,2,1,0:T(8,128)(2,1)S(1)}, bf16[2,4,16,128]{3,2,1,0:T(8,128)(2,1)S(1)}, u32[]{:S(2)}, u32[]{:S(2)}) %collective-permute-start.7) | collective-permute-done | bytes 32800 | tf_op jit(solution)/shard_map/ppermute | solution.py:295
  32.4 1.5 %collective-permute-done.8.refs_6_ = bf16[2,4,16,128]{3,2,1,0:T(8,128)(2,1)S(1)} collective-permute-done((bf16[2,4,16,128]{3,2,1,0:T(8,128)(2,1)S(1)}, bf16[2,4,16,128]{3,2,1,0:T(8,128)(2,1)S(1)}, u32[]{:S(2)}, u32[]{:S(2)}) %collective-permute-start.8) | collective-permute-done | bytes 32800 | tf_op jit(solution)/shard_map/ppermute | solution.py:295
  33.9 4.2 %collective-permute-done.9.refs_7_ = bf16[2,4,16,128]{3,2,1,0:T(8,128)(2,1)S(1)} collective-permute-done((bf16[2,4,16,128]{3,2,1,0:T(8,128)(2,1)S(1)}, bf16[2,4,16,128]{3,2,1,0:T(8,128)(2,1)S(1)}, u32[]{:S(2)}, u32[]{:S(2)}) %collective-permute-start.9) | collective-permute-done | bytes 32800 | tf_op jit(solution)/shard_map/ppermute | solution.py:295
  38.0 0.0 all-to-all-done.refs_8_
  38.0 1.2 %shard_map.86 = f32[32,2,32]{2,1,0:T(2,128)S(1)} custom-call(s32[2]{0:T(128)S(1)} %pad_add_fusion.me_ref, bf16[2,4,16,128]{3,2,1,0:T(8,128)(2,1)S(1)} %get-tuple-element.13.refs_0_, bf16[2,4,16,128]{3,2,1,0:T(8,128)(2,1)S(1)} %collective-permute-done.3.refs_1_, bf16[2,4,16,128]{3,2,1,0:T(8,128)(2,1)S(1)} %collective-permute-done.4.refs_2_, ...), custom_call_target="tpu_custom_call" | custom-call | tf_op jit(solution)/shard_map/pallas_call | solution.py:298
  39.3 8.9 %all_to_all.10 = f32[32,2,32]{2,1,0:T(2,128)S(1)} all-to-all(f32[32,2,32]{2,1,0:T(2,128)S(1)} %shard_map.86), channel_id=1, replica_groups=mesh['expert'=4,'dp'=8] {'expert','dp'}, dimensions={0} | all-to-all | bytes 16384 | tf_op jit(solution)/shard_map/all_to_all | solution.py:305
  48.2 0.6 %reduce_sum.9 = f32[2,32]{1,0:T(2,128)} reduce(f32[32,2,32]{2,1,0:T(2,128)S(1)} %all_to_all.10, f32[]{:T(128)} %constant.9.clone.1), dimensions={0}, to_apply=%region_0.0 | reduce | flops 1984 | bytes 8452 | tf_op jit(solution)/shard_map/reduce_sum | solution.py:306
Async XLA Ops:
  1.9 36.1 %all-to-all-start = ((bf16[8,4,16,512]{3,2,1,0:T(8,128)(2,1)}), bf16[8,4,16,512]{3,2,1,0:T(8,128)(2,1)S(1)}, u32[]{:S(2)}, u32[]{:S(2)}) async-start(bf16[8,4,16,512]{3,2,1,0:T(8,128)(2,1)} %shard_map.85), calls=%async_computation | async-start | bytes 1048576 | tf_op jit(solution)/shard_map/all_to_all | solution.py:227
  11.8 6.5 %copy-start = (f32[88,128]{1,0:T(8,128)S(1)}, f32[88,128]{1,0:T(8,128)}, u32[]{:S(2)}) copy-start(f32[88,128]{1,0:T(8,128)} %shard_map.82.refs_0_) | copy-start | bytes 135172
  11.8 6.5 %collective-permute-start.2 = (f32[88,128]{1,0:T(8,128)}, f32[88,128]{1,0:T(8,128)S(1)}, u32[]{:S(2)}, u32[]{:S(2)}) collective-permute-start(f32[88,128]{1,0:T(8,128)} %shard_map.82.refs_0_), channel_id=1, source_target_pairs={{0,24},{8,16},{16,8},{24,0},{1,25},{9,17},{17,9},{25,1},{2,26},{10... | collective-permute-start | bytes 135176 | tf_op jit(solution)/shard_map/ppermute | solution.py:256
  12.6 5.7 %collective-permute-start.1 = (f32[88,128]{1,0:T(8,128)}, f32[88,128]{1,0:T(8,128)S(1)}, u32[]{:S(2)}, u32[]{:S(2)}) collective-permute-start(f32[88,128]{1,0:T(8,128)} %shard_map.82.refs_0_), channel_id=1, source_target_pairs={{0,16},{8,24},{16,0},{24,8},{1,17},{9,25},{17,1},{25,9},{2,18},{10... | collective-permute-start | bytes 135176 | tf_op jit(solution)/shard_map/ppermute | solution.py:256
  13.5 4.8 %collective-permute-start = (f32[88,128]{1,0:T(8,128)}, f32[88,128]{1,0:T(8,128)S(1)}, u32[]{:S(2)}, u32[]{:S(2)}) collective-permute-start(f32[88,128]{1,0:T(8,128)} %shard_map.82.refs_0_), channel_id=1, source_target_pairs={{0,8},{8,0},{16,24},{24,16},{1,9},{9,1},{17,25},{25,17},{2,10},{10... | collective-permute-start | bytes 135176 | tf_op jit(solution)/shard_map/ppermute | solution.py:256
  20.2 7.9 %collective-permute-start.3 = (bf16[2,4,16,128]{3,2,1,0:T(8,128)(2,1)S(1)}, bf16[2,4,16,128]{3,2,1,0:T(8,128)(2,1)S(1)}, u32[]{:S(2)}, u32[]{:S(2)}) collective-permute-start(bf16[2,4,16,128]{3,2,1,0:T(8,128)(2,1)S(1)} %get-tuple-element.14), channel_id=1, source_target_pairs={{0,1},{1,0},{2,3},{3,2},{4,5},{5,4},{6,7},{7,6},{8,9},{9,8},{10,11... | collective-permute-start | bytes 98312 | tf_op jit(solution)/shard_map/ppermute | solution.py:295
  22.3 9.1 %collective-permute-start.4 = (bf16[2,4,16,128]{3,2,1,0:T(8,128)(2,1)S(1)}, bf16[2,4,16,128]{3,2,1,0:T(8,128)(2,1)S(1)}, u32[]{:S(2)}, u32[]{:S(2)}) collective-permute-start(bf16[2,4,16,128]{3,2,1,0:T(8,128)(2,1)S(1)} %get-tuple-element.15), channel_id=1, source_target_pairs={{0,2},{1,3},{2,0},{3,1},{4,6},{5,7},{6,4},{7,5},{8,10},{9,11},{10,... | collective-permute-start | bytes 98312 | tf_op jit(solution)/shard_map/ppermute | solution.py:295
  23.8 7.7 %collective-permute-start.5 = (bf16[2,4,16,128]{3,2,1,0:T(8,128)(2,1)S(1)}, bf16[2,4,16,128]{3,2,1,0:T(8,128)(2,1)S(1)}, u32[]{:S(2)}, u32[]{:S(2)}) collective-permute-start(bf16[2,4,16,128]{3,2,1,0:T(8,128)(2,1)S(1)} %get-tuple-element.16), channel_id=1, source_target_pairs={{0,3},{1,2},{2,1},{3,0},{4,7},{5,6},{6,5},{7,4},{8,11},{9,10},{10,... | collective-permute-start | bytes 98312 | tf_op jit(solution)/shard_map/ppermute | solution.py:295
  23.8 7.7 %collective-permute-start.6 = (bf16[2,4,16,128]{3,2,1,0:T(8,128)(2,1)S(1)}, bf16[2,4,16,128]{3,2,1,0:T(8,128)(2,1)S(1)}, u32[]{:S(2)}, u32[]{:S(2)}) collective-permute-start(bf16[2,4,16,128]{3,2,1,0:T(8,128)(2,1)S(1)} %get-tuple-element.17), channel_id=1, source_target_pairs={{0,4},{1,5},{2,6},{3,7},{4,0},{5,1},{6,2},{7,3},{8,12},{9,13},{10,... | collective-permute-start | bytes 98312 | tf_op jit(solution)/shard_map/ppermute | solution.py:295
  26.7 5.7 %collective-permute-start.7 = (bf16[2,4,16,128]{3,2,1,0:T(8,128)(2,1)S(1)}, bf16[2,4,16,128]{3,2,1,0:T(8,128)(2,1)S(1)}, u32[]{:S(2)}, u32[]{:S(2)}) collective-permute-start(bf16[2,4,16,128]{3,2,1,0:T(8,128)(2,1)S(1)} %get-tuple-element.18), channel_id=1, source_target_pairs={{0,5},{1,4},{2,7},{3,6},{4,1},{5,0},{6,3},{7,2},{8,13},{9,12},{10,... | collective-permute-start | bytes 98312 | tf_op jit(solution)/shard_map/ppermute | solution.py:295
  28.2 5.7 %collective-permute-start.8 = (bf16[2,4,16,128]{3,2,1,0:T(8,128)(2,1)S(1)}, bf16[2,4,16,128]{3,2,1,0:T(8,128)(2,1)S(1)}, u32[]{:S(2)}, u32[]{:S(2)}) collective-permute-start(bf16[2,4,16,128]{3,2,1,0:T(8,128)(2,1)S(1)} %get-tuple-element.19), channel_id=1, source_target_pairs={{0,6},{1,7},{2,4},{3,5},{4,2},{5,3},{6,0},{7,1},{8,14},{9,15},{10,... | collective-permute-start | bytes 98312 | tf_op jit(solution)/shard_map/ppermute | solution.py:295
  31.4 6.6 %collective-permute-start.9 = (bf16[2,4,16,128]{3,2,1,0:T(8,128)(2,1)S(1)}, bf16[2,4,16,128]{3,2,1,0:T(8,128)(2,1)S(1)}, u32[]{:S(2)}, u32[]{:S(2)}) collective-permute-start(bf16[2,4,16,128]{3,2,1,0:T(8,128)(2,1)S(1)} %get-tuple-element.20), channel_id=1, source_target_pairs={{0,7},{1,6},{2,5},{3,4},{4,3},{5,2},{6,1},{7,0},{8,15},{9,14},{10,... | collective-permute-start | bytes 98312 | tf_op jit(solution)/shard_map/ppermute | solution.py:295

commit v6 on v5

--- a/solution.py
+++ b/solution.py
@@ -5,12 +5,13 @@
 from jax import lax
 from jax.experimental import pallas as pl
 from jax.experimental.pallas import tpu as pltpu
+from jax.sharding import Mesh
 from jax.sharding import PartitionSpec as P
 
 
 DOC_GRP = 2
+SPLIT = 4
 LANES = 128
-VL_S = 53 << 20
 VL_A = 63 << 20
 VL_L = 53 << 20
 VL_F = 16 << 20
@@ -20,15 +21,22 @@
 TN = (((0,), (0,)), ((), ()))
 
 
-def split_kernel(val_hbm, out_ref, sems):
-    parts, _, _, piece = out_ref.shape
-    copies = [
-        pltpu.make_async_copy(val_hbm.at[:, :, pl.ds(j * piece, piece)], out_ref.at[j], sems.at[j])
-        for j in range(parts)
-    ]
-    for copy in copies:
-        copy.start()
-    for copy in copies:
+def split_kernel(val_hbm, out_hbm, piece_ref, in_sems, out_sems):
+    parts, _, _, piece = piece_ref.shape
+    ins = []
+    for j in range(parts):
+        cols = pl.ds(j * piece, piece)
+        ins.append(pltpu.make_async_copy(val_hbm.at[:, :, cols], piece_ref.at[j], in_sems.at[j]))
+        ins[j].start()
+    outs = []
+    for j in range(parts):
+        ins[j].wait()
+        for t in range(j, out_hbm.shape[0], parts):
+            outs.append(
+                pltpu.make_async_copy(piece_ref.at[j], out_hbm.at[t], out_sems.at[t])
+            )
+            outs[-1].start()
+    for copy in outs:
         copy.wait()
 
 
@@ -103,7 +111,7 @@
             out_ref[e] = jnp.concatenate([low, low], axis=1).astype(BF16)
 
 
-def feature_kernel(groups, parts, rank, top, me_ref, *refs):
+def feature_kernel(groups, parts, rank, top, me_ref, mine_ref, *refs):
     pays = refs[:groups]
     low_ref = refs[groups]
     outs = refs[groups + 1 : groups + 1 + parts]
@@ -165,7 +173,7 @@
     _, chunks, _, _ = outs[0].shape
     size = chunks * exp_local
     for k in range(parts):
-        part = lax.bitwise_xor(me_ref[1], k)
+        part = lax.bitwise_xor(mine_ref[0], k)
         for d in range(DOC_GRP):
             start = pl.multiple_of((d * half + part * chunks) * exp_local, size)
             outs[k][d] = (
@@ -173,11 +181,11 @@
             )
 
 
-def score_kernel(parts, scale, me_ref, *refs):
+def score_kernel(parts, scale, mine_ref, *refs):
     feats, val_ref, out_ref = refs[:parts], refs[parts], refs[parts + 1]
     docs, chunks, exp_local, lanes = feats[0].shape
-    vals = val_ref.shape[1]
-    left_rows, right_rows = parts * docs * exp_local, parts * vals * exp_local
+    vals = val_ref.shape[0] * val_ref.shape[1]
+    left_rows, right_rows = parts * docs * exp_local, vals * exp_local
     total = jnp.zeros((left_rows, right_rows), F32)
     for c in range(chunks):
         left = jnp.concatenate(
@@ -190,14 +198,14 @@
     total = jnp.where(row == col, total, 0.0)
     total = jnp.sum(total.reshape(parts * docs, exp_local, right_rows), axis=1)
     pick = (
-        lax.broadcasted_iota(jnp.int32, (right_rows, parts * vals), 0) // exp_local
-        == lax.broadcasted_iota(jnp.int32, (right_rows, parts * vals), 1)
+        lax.broadcasted_iota(jnp.int32, (right_rows, vals), 0) // exp_local
+        == lax.broadcasted_iota(jnp.int32, (right_rows, vals), 1)
     ).astype(F32)
     scores = jnp.dot(
         total, pick, preferred_element_type=F32, precision=lax.Precision.HIGHEST
     ) * scale
     for k in range(parts):
-        group = lax.bitwise_xor(me_ref[1], k)
+        group = lax.bitwise_xor(mine_ref[0], k)
         for i in range(out_ref.shape[0] // parts):
             out_ref[i * parts + group] = scores[k * docs : (k + 1) * docs, :]
 
@@ -207,24 +215,31 @@
     top = routes.shape[1]
     rank = proj_in.shape[1]
     groups = lax.axis_size("expert")
-    dp = lax.axis_size("dp")
+    lo = lax.axis_size("lo")
+    dp = lax.axis_size("hi") * lo
     exp_local, rows, hidden = hidden_grad.shape
     vals = val_features.shape[0]
     entries = rank * rank
     experts = exp_local * groups
-    chunks = entries // LANES // dp
+    chunks = entries // LANES // lo
 
     vmem = pl.BlockSpec(memory_space=pltpu.VMEM)
     hbm = pl.BlockSpec(memory_space=pltpu.HBM)
     val_split = pl.pallas_call(
         split_kernel,
-        out_shape=jax.ShapeDtypeStruct((dp, vals, exp_local, entries // dp), BF16),
+        out_shape=jax.ShapeDtypeStruct((dp, vals, exp_local, entries // lo), BF16),
         in_specs=[hbm],
-        out_specs=vmem,
-        scratch_shapes=[pltpu.SemaphoreType.DMA((dp,))],
-        compiler_params=pltpu.CompilerParams(vmem_limit_bytes=VL_S),
+        out_specs=hbm,
+        scratch_shapes=[
+            pltpu.VMEM((lo, vals, exp_local, entries // lo), BF16),
+            pltpu.SemaphoreType.DMA((lo,)),
+            pltpu.SemaphoreType.DMA((dp,)),
+        ],
+        compiler_params=pltpu.CompilerParams(vmem_limit_bytes=VL_A),
     )(val_features)
-    val_all = lax.all_to_all(val_split, "dp", split_axis=0, concat_axis=0, tiled=True)
+    val_all = lax.all_to_all(
+        val_split, ("hi", "lo"), split_axis=0, concat_axis=0, tiled=True
+    )
 
     pay_rows = rank + 2 * top + 8
     steps = 2
@@ -273,14 +288,15 @@
         ),
     )(hidden_grad, proj_out.transpose(0, 2, 1))
 
-    me = jnp.stack([lax.axis_index("expert"), lax.axis_index("dp")]).astype(jnp.int32)
+    me = lax.axis_index("expert").astype(jnp.int32).reshape(1)
+    mine = lax.axis_index("lo").astype(jnp.int32).reshape(1)
     smem = pl.BlockSpec(memory_space=pltpu.SMEM)
     block = jax.ShapeDtypeStruct((DOC_GRP, chunks, exp_local, LANES), BF16)
     feats = pl.pallas_call(
-        functools.partial(feature_kernel, groups, dp, rank, top),
-        out_shape=(block,) * dp,
-        in_specs=[smem] + [vmem] * (groups + 1),
-        out_specs=(vmem,) * dp,
+        functools.partial(feature_kernel, groups, lo, rank, top),
+        out_shape=(block,) * lo,
+        in_specs=[smem, smem] + [vmem] * (groups + 1),
+        out_specs=(vmem,) * lo,
         scratch_shapes=[
             pltpu.VMEM((exp_local, rows, 2 * rank), BF16),
             pltpu.VMEM((DOC_GRP * rank // 2 * exp_local, 2 * rank), F32),
@@ -289,33 +305,37 @@
         cost_estimate=pl.CostEstimate(
             flops=8 * exp_local * rows * rank * tok, bytes_accessed=1 << 20, transcendentals=0
         ),
-    )(me, *pays, low)
+    )(me, mine, *pays, low)
     arrived = [feats[0]]
-    for k in range(1, dp):
-        arrived.append(lax.ppermute(feats[k], "dp", [(a, a ^ k) for a in range(dp)]))
+    for k in range(1, lo):
+        arrived.append(lax.ppermute(feats[k], "lo", [(a, a ^ k) for a in range(lo)]))
 
     scale = 1.0 / float(experts * entries) ** 0.5
     part = pl.pallas_call(
-        functools.partial(score_kernel, dp, scale),
-        out_shape=jax.ShapeDtypeStruct((groups * dp, DOC_GRP, dp * vals), F32),
-        in_specs=[smem] + [vmem] * (dp + 1),
+        functools.partial(score_kernel, lo, scale),
+        out_shape=jax.ShapeDtypeStruct((groups * lo, DOC_GRP, dp * vals), F32),
+        in_specs=[smem] + [vmem] * (lo + 1),
         out_specs=vmem,
         compiler_params=pltpu.CompilerParams(vmem_limit_bytes=40 << 20),
-    )(me, *arrived, val_all)
-    parts = lax.all_to_all(part, ("expert", "dp"), split_axis=0, concat_axis=0, tiled=True)
+    )(mine, *arrived, val_all)
+    parts = lax.all_to_all(part, ("expert", "lo"), split_axis=0, concat_axis=0, tiled=True)
     return jnp.sum(parts, axis=0)
 
 
 def solution(mesh):
+    groups, dp = mesh.shape["expert"], mesh.shape["dp"]
+    lo = min(SPLIT, dp)
+    grid = Mesh(mesh.devices.reshape(groups, dp // lo, lo), ("expert", "hi", "lo"))
+    everyone = ("expert", "hi", "lo")
     in_specs = (
-        P(("expert", "dp"), None),
-        P(("expert", "dp"), None),
-        P(("expert", "dp"), None),
-        P(("expert", "dp")),
-        P("expert", "dp", None),
+        P(everyone, None),
+        P(everyone, None),
+        P(everyone, None),
+        P(everyone),
+        P("expert", ("hi", "lo"), None),
         P(),
         P("expert", None, None),
-        P("dp", "expert", None),
+        P(("hi", "lo"), "expert", None),
     )
-    out_specs = P("dp", None)
-    return jax.shard_map(layer, mesh=mesh, in_specs=in_specs, out_specs=out_specs, check_vma=False)
+    out_specs = P(("hi", "lo"), None)
+    return jax.shard_map(layer, mesh=grid, in_specs=in_specs, out_specs=out_specs, check_vma=False)

time: 49.1 us -> 47.1 us (0.959)
  starting transfers between devices: 20.5 us -> 12.8 us
  waiting for transfers between devices: 6.55 us -> 11.9 us
    ppermute x7 -> x3, starting transfers between devices: 11.3 us -> 3.63 us  [layer(): lax.ppermute(feats[k], 'lo', [(a, a ^ k) for a in range(lo)])]
    all_to_all x1, waiting for transfers between devices: 0.01 us -> 5.44 us  [layer(): lax.all_to_all(val_split, ('hi', 'lo'), split_axis=0, concat_axis=0, tile...]
    ppermute x7 -> x3, waiting for transfers between devices: 6.54 us -> 6.43 us  [layer(): lax.ppermute(feats[k], 'lo', [(a, a ^ k) for a in range(lo)])]
  transfers between devices with their start and end apart: 11 -> 7, of which waited for: 3 -> 4; matrix products, arithmetic and copies ran while one was open for 0% -> 0% of each run, Pallas kernels for 18% -> 18%
where the time goes in v6:
time: 47.1 us; the launch traced here: 46.8 us
  starting transfers between devices  12.8 us (27%)
  Pallas kernels  12.3 us (26%)
  waiting for transfers between devices  11.9 us (25%)
  blocking collectives  9.08 us (19%)
  other arithmetic  0.59 us (1%)
    all_to_all x1, blocking collectives, layer(): lax.all_to_all(part, ('expert', 'lo'), split_axis=0, concat_axis=0, tiled...  9.08 us
    all_to_all x1, starting transfers between devices, layer(): lax.all_to_all(val_split, ('hi', 'lo'), split_axis=0, concat_axis=0, tile...  7.29 us
    ppermute x3, waiting for transfers between devices, layer(): lax.ppermute(feats[k], 'lo', [(a, a ^ k) for a in range(lo)])  6.43 us
    all_to_all x1, waiting for transfers between devices, layer(): lax.all_to_all(val_split, ('hi', 'lo'), split_axis=0, concat_axis=0, tile...  5.44 us
    pallas_call x1, Pallas kernels, layer(): pl.pallas_call(lowered_kernel, out_shape=jax.ShapeDtypeStruct((exp_local,...  4.44 us
    ppermute x3, starting transfers between devices, layer(): lax.ppermute(feats[k], 'lo', [(a, a ^ k) for a in range(lo)])  3.63 us
    pallas_call x1, Pallas kernels, layer(): pl.pallas_call(act_kernel, out_shape=jax.ShapeDtypeStruct((pay_rows, tok)...  2.57 us
    pallas_call x1, Pallas kernels, layer(): pl.pallas_call(split_kernel, out_shape=jax.ShapeDtypeStruct((dp, vals, ex...  2.03 us
  transfers between devices with their start and end apart: 7, of which 4 were waited for; matrix products, arithmetic and copies ran while one was open for 0% of the time, Pallas kernels for 18%

profile of v6, /device:TPU:0, one launch (start us, length us, event | category | flops | bytes accessed | tf_op | source)
XLA Modules:
  0.0 46.8 jit_solution(13638782512675865821)
XLA Ops:
  0.0 2.0 %shard_map.85 = bf16[8,4,16,1024]{3,2,1,0:T(8,128)(2,1)} custom-call(bf16[4,16,4096]{2,1,0:T(8,128)(2,1)} %val_hbm.1), custom_call_target="tpu_custom_call" | custom-call | tf_op jit(solution)/shard_map/pallas_call | solution.py:228
  2.0 7.3 %all-to-all-start = ((bf16[8,4,16,1024]{3,2,1,0:T(8,128)(2,1)}), bf16[8,4,16,1024]{3,2,1,0:T(8,128)(2,1)}, u32[]{:S(2)}, u32[]{:S(2)}) async-start(bf16[8,4,16,1024]{3,2,1,0:T(8,128)(2,1)} %shard_map.85), calls=%async_computation | async-start | bytes 2097152 | tf_op jit(solution)/shard_map/all_to_all | solution.py:240
  9.3 2.6 %shard_map.82.refs_0_ = f32[88,128]{1,0:T(8,128)} custom-call(bf16[128,4096]{1,0:T(8,128)(2,1)} %tok_hbm.1, bf16[64,4096]{1,0:T(8,128)(2,1)} %bitcast.8, s32[8,128]{1,0:T(8,128)} %bitcast.9, f32[8,128]{1,0:T(8,128)} %bitcast.10, s32[1,128]{1,0:T(1,128)} %bitcast.11), custom_call_target="tpu_custom_call" | custom-call | flops 67108864 | bytes 1572864 | tf_op jit(solution)/shard_map/pallas_call | solution.py:246
  11.9 0.0 copy-start
  11.9 0.7 %collective-permute-start.2 = (f32[88,128]{1,0:T(8,128)}, f32[88,128]{1,0:T(8,128)S(1)}, u32[]{:S(2)}, u32[]{:S(2)}) collective-permute-start(f32[88,128]{1,0:T(8,128)} %shard_map.82.refs_0_), channel_id=1, source_target_pairs={{0,24},{8,16},{16,8},{24,0},{1,25},{9,17},{17,9},{25,1},{2,26},{10... | collective-permute-start | bytes 135176 | tf_op jit(solution)/shard_map/ppermute | solution.py:271
  12.7 0.9 %collective-permute-start.1 = (f32[88,128]{1,0:T(8,128)}, f32[88,128]{1,0:T(8,128)S(1)}, u32[]{:S(2)}, u32[]{:S(2)}) collective-permute-start(f32[88,128]{1,0:T(8,128)} %shard_map.82.refs_0_), channel_id=1, source_target_pairs={{0,16},{8,24},{16,0},{24,8},{1,17},{9,25},{17,1},{25,9},{2,18},{10... | collective-permute-start | bytes 135176 | tf_op jit(solution)/shard_map/ppermute | solution.py:271
  13.6 0.3 collective-permute-start
  13.8 4.4 %shard_map.83.refs_4_ = bf16[16,128,128]{2,1,0:T(8,128)(2,1)S(1)} custom-call(bf16[16,128,1536]{2,1,0:T(8,128)(2,1)} %grad_hbm.1, bf16[16,64,1536]{2,1,0:T(8,128)(2,1)} %bitcast.7), custom_call_target="tpu_custom_call" | custom-call | flops 402653184 | bytes 9437184 | tf_op jit(solution)/shard_map/pallas_call | solution.py:273
  18.3 0.0 collective-permute-done.2.refs_3_
  18.3 0.0 collective-permute-done.1.refs_2_
  18.3 0.0 collective-permute-done.refs_1_
  18.3 0.0 copy-done
  18.3 1.4 %shard_map.84 = (bf16[2,8,16,128]{3,2,1,0:T(8,128)(2,1)S(1)}, bf16[2,8,16,128]{3,2,1,0:T(8,128)(2,1)S(1)}, bf16[2,8,16,128]{3,2,1,0:T(8,128)(2,1)S(1)}, bf16[2,8,16,128]{3,2,1,0:T(8,128)(2,1)S(1)}) custom-call(s32[1]{0:T(128)} %bitcast.1.me_ref, s32[1]{0:T(128)} %bitcast.mine_ref, f32[88,128]{1,0:T(8,128)S(1)} %copy-done, ...), custom_call_target="tpu_custom_call" | custom-call | flops 134217728 | bytes 1048576 | tf_op jit(solution)/shard_map/pallas_call | solution.py:295
  19.7 2.1 %collective-permute-start.3 = (bf16[2,8,16,128]{3,2,1,0:T(8,128)(2,1)S(1)}, bf16[2,8,16,128]{3,2,1,0:T(8,128)(2,1)S(1)}, u32[]{:S(2)}, u32[]{:S(2)}) collective-permute-start(bf16[2,8,16,128]{3,2,1,0:T(8,128)(2,1)S(1)} %get-tuple-element.10), channel_id=1, source_target_pairs={{0,1},{1,0},{2,3},{3,2},{4,5},{5,4},{6,7},{7,6},{8,9},{9,8},{10,11... | collective-permute-start | bytes 196616 | tf_op jit(solution)/shard_map/ppermute | solution.py:311
  21.8 1.5 %collective-permute-start.4 = (bf16[2,8,16,128]{3,2,1,0:T(8,128)(2,1)S(1)}, bf16[2,8,16,128]{3,2,1,0:T(8,128)(2,1)S(1)}, u32[]{:S(2)}, u32[]{:S(2)}) collective-permute-start(bf16[2,8,16,128]{3,2,1,0:T(8,128)(2,1)S(1)} %get-tuple-element.11), channel_id=1, source_target_pairs={{0,2},{1,3},{2,0},{3,1},{4,6},{5,7},{6,4},{7,5},{8,10},{9,11},{10,... | collective-permute-start | bytes 196616 | tf_op jit(solution)/shard_map/ppermute | solution.py:311
  23.3 0.1 collective-permute-start.5
  23.3 1.5 %collective-permute-done.3.refs_1_ = bf16[2,8,16,128]{3,2,1,0:T(8,128)(2,1)S(1)} collective-permute-done((bf16[2,8,16,128]{3,2,1,0:T(8,128)(2,1)S(1)}, bf16[2,8,16,128]{3,2,1,0:T(8,128)(2,1)S(1)}, u32[]{:S(2)}, u32[]{:S(2)}) %collective-permute-start.3) | collective-permute-done | bytes 65568 | tf_op jit(solution)/shard_map/ppermute | solution.py:311
  24.8 3.8 %collective-permute-done.4.refs_2_ = bf16[2,8,16,128]{3,2,1,0:T(8,128)(2,1)S(1)} collective-permute-done((bf16[2,8,16,128]{3,2,1,0:T(8,128)(2,1)S(1)}, bf16[2,8,16,128]{3,2,1,0:T(8,128)(2,1)S(1)}, u32[]{:S(2)}, u32[]{:S(2)}) %collective-permute-start.4) | collective-permute-done | bytes 65568 | tf_op jit(solution)/shard_map/ppermute | solution.py:311
  28.6 1.2 %collective-permute-done.5.refs_3_ = bf16[2,8,16,128]{3,2,1,0:T(8,128)(2,1)S(1)} collective-permute-done((bf16[2,8,16,128]{3,2,1,0:T(8,128)(2,1)S(1)}, bf16[2,8,16,128]{3,2,1,0:T(8,128)(2,1)S(1)}, u32[]{:S(2)}, u32[]{:S(2)}) %collective-permute-start.5) | collective-permute-done | bytes 65568 | tf_op jit(solution)/shard_map/ppermute | solution.py:311
  29.8 5.4 %all-to-all-done.refs_4_ = bf16[8,4,16,1024]{3,2,1,0:T(8,128)(2,1)} async-done(((bf16[8,4,16,1024]{3,2,1,0:T(8,128)(2,1)}), bf16[8,4,16,1024]{3,2,1,0:T(8,128)(2,1)}, u32[]{:S(2)}, u32[]{:S(2)}) %all-to-all-start) | async-done | bytes 1048608 | tf_op jit(solution)/shard_map/all_to_all | solution.py:240
  35.2 1.9 %shard_map.86 = f32[16,2,32]{2,1,0:T(2,128)S(1)} custom-call(s32[1]{0:T(128)} %bitcast.mine_ref, bf16[2,8,16,128]{3,2,1,0:T(8,128)(2,1)S(1)} %get-tuple-element.9.refs_0_, bf16[2,8,16,128]{3,2,1,0:T(8,128)(2,1)S(1)} %collective-permute-done.3.refs_1_, bf16[2,8,16,128]{3,2,1,0:T(8,128)(2,1)S(1)} %collective-permute-done.4.refs_2_, ...), custom_call_target="tpu_custom_call" | custom-call | tf_op jit(solution)/shard_map/pallas_call | solution.py:314
  37.1 9.1 %all_to_all.10 = f32[16,2,32]{2,1,0:T(2,128)S(1)} all-to-all(f32[16,2,32]{2,1,0:T(2,128)S(1)} %shard_map.86), channel_id=1, replica_groups=mesh['expert'=4,'hi'=2,'lo'=4] {'expert','lo'}, dimensions={0} | all-to-all | bytes 8192 | tf_op jit(solution)/shard_map/all_to_all | solution.py:321
  46.2 0.6 %reduce_sum.9 = f32[2,32]{1,0:T(2,128)} reduce(f32[16,2,32]{2,1,0:T(2,128)S(1)} %all_to_all.10, f32[]{:T(128)} %constant.8.clone.1), dimensions={0}, to_apply=%region_0.0 | reduce | flops 960 | bytes 4356 | tf_op jit(solution)/shard_map/reduce_sum | solution.py:322
Async XLA Ops:
  2.0 33.2 %all-to-all-start = ((bf16[8,4,16,1024]{3,2,1,0:T(8,128)(2,1)}), bf16[8,4,16,1024]{3,2,1,0:T(8,128)(2,1)}, u32[]{:S(2)}, u32[]{:S(2)}) async-start(bf16[8,4,16,1024]{3,2,1,0:T(8,128)(2,1)} %shard_map.85), calls=%async_computation | async-start | bytes 2097152 | tf_op jit(solution)/shard_map/all_to_all | solution.py:240
  11.9 6.4 %copy-start = (f32[88,128]{1,0:T(8,128)S(1)}, f32[88,128]{1,0:T(8,128)}, u32[]{:S(2)}) copy-start(f32[88,128]{1,0:T(8,128)} %shard_map.82.refs_0_) | copy-start | bytes 135172
  11.9 6.4 %collective-permute-start.2 = (f32[88,128]{1,0:T(8,128)}, f32[88,128]{1,0:T(8,128)S(1)}, u32[]{:S(2)}, u32[]{:S(2)}) collective-permute-start(f32[88,128]{1,0:T(8,128)} %shard_map.82.refs_0_), channel_id=1, source_target_pairs={{0,24},{8,16},{16,8},{24,0},{1,25},{9,17},{17,9},{25,1},{2,26},{10... | collective-permute-start | bytes 135176 | tf_op jit(solution)/shard_map/ppermute | solution.py:271
  12.7 5.6 %collective-permute-start.1 = (f32[88,128]{1,0:T(8,128)}, f32[88,128]{1,0:T(8,128)S(1)}, u32[]{:S(2)}, u32[]{:S(2)}) collective-permute-start(f32[88,128]{1,0:T(8,128)} %shard_map.82.refs_0_), channel_id=1, source_target_pairs={{0,16},{8,24},{16,0},{24,8},{1,17},{9,25},{17,1},{25,9},{2,18},{10... | collective-permute-start | bytes 135176 | tf_op jit(solution)/shard_map/ppermute | solution.py:271
  13.6 4.7 %collective-permute-start = (f32[88,128]{1,0:T(8,128)}, f32[88,128]{1,0:T(8,128)S(1)}, u32[]{:S(2)}, u32[]{:S(2)}) collective-permute-start(f32[88,128]{1,0:T(8,128)} %shard_map.82.refs_0_), channel_id=1, source_target_pairs={{0,8},{8,0},{16,24},{24,16},{1,9},{9,1},{17,25},{25,17},{2,10},{10... | collective-permute-start | bytes 135176 | tf_op jit(solution)/shard_map/ppermute | solution.py:271
  19.7 5.1 %collective-permute-start.3 = (bf16[2,8,16,128]{3,2,1,0:T(8,128)(2,1)S(1)}, bf16[2,8,16,128]{3,2,1,0:T(8,128)(2,1)S(1)}, u32[]{:S(2)}, u32[]{:S(2)}) collective-permute-start(bf16[2,8,16,128]{3,2,1,0:T(8,128)(2,1)S(1)} %get-tuple-element.10), channel_id=1, source_target_pairs={{0,1},{1,0},{2,3},{3,2},{4,5},{5,4},{6,7},{7,6},{8,9},{9,8},{10,11... | collective-permute-start | bytes 196616 | tf_op jit(solution)/shard_map/ppermute | solution.py:311
  21.8 6.8 %collective-permute-start.4 = (bf16[2,8,16,128]{3,2,1,0:T(8,128)(2,1)S(1)}, bf16[2,8,16,128]{3,2,1,0:T(8,128)(2,1)S(1)}, u32[]{:S(2)}, u32[]{:S(2)}) collective-permute-start(bf16[2,8,16,128]{3,2,1,0:T(8,128)(2,1)S(1)} %get-tuple-element.11), channel_id=1, source_target_pairs={{0,2},{1,3},{2,0},{3,1},{4,6},{5,7},{6,4},{7,5},{8,10},{9,11},{10,... | collective-permute-start | bytes 196616 | tf_op jit(solution)/shard_map/ppermute | solution.py:311
  23.3 6.5 %collective-permute-start.5 = (bf16[2,8,16,128]{3,2,1,0:T(8,128)(2,1)S(1)}, bf16[2,8,16,128]{3,2,1,0:T(8,128)(2,1)S(1)}, u32[]{:S(2)}, u32[]{:S(2)}) collective-permute-start(bf16[2,8,16,128]{3,2,1,0:T(8,128)(2,1)S(1)} %get-tuple-element.12), channel_id=1, source_target_pairs={{0,3},{1,2},{2,1},{3,0},{4,7},{5,6},{6,5},{7,4},{8,11},{9,10},{10,... | collective-permute-start | bytes 196616 | tf_op jit(solution)/shard_map/ppermute | solution.py:311

commit v7 on v6

--- a/solution.py
+++ b/solution.py
@@ -21,22 +21,21 @@
 TN = (((0,), (0,)), ((), ()))
 
 
-def split_kernel(val_hbm, out_hbm, piece_ref, in_sems, out_sems):
+def split_kernel(mine_ref, val_hbm, *refs):
+    outs, (piece_ref, sems) = refs[:-2], refs[-2:]
     parts, _, _, piece = piece_ref.shape
-    ins = []
-    for j in range(parts):
-        cols = pl.ds(j * piece, piece)
-        ins.append(pltpu.make_async_copy(val_hbm.at[:, :, cols], piece_ref.at[j], in_sems.at[j]))
-        ins[j].start()
-    outs = []
-    for j in range(parts):
-        ins[j].wait()
-        for t in range(j, out_hbm.shape[0], parts):
-            outs.append(
-                pltpu.make_async_copy(piece_ref.at[j], out_hbm.at[t], out_sems.at[t])
-            )
-            outs[-1].start()
-    for copy in outs:
+    ins, puts = [], []
+    for k in range(parts):
+        part = lax.bitwise_xor(mine_ref[0], k)
+        cols = pl.ds(pl.multiple_of(part * piece, piece), piece)
+        ins.append(pltpu.make_async_copy(val_hbm.at[:, :, cols], piece_ref.at[k], sems.at[k, 0]))
+        puts.append(pltpu.make_async_copy(piece_ref.at[k], outs[k], sems.at[k, 1]))
+    for copy in ins:
+        copy.start()
+    for k in range(parts):
+        ins[k].wait()
+        puts[k].start()
+    for copy in puts:
         copy.wait()
 
 
@@ -182,30 +181,36 @@
 
 
 def score_kernel(parts, scale, mine_ref, *refs):
-    feats, val_ref, out_ref = refs[:parts], refs[parts], refs[parts + 1]
+    feats, pieces, out_ref = refs[:parts], refs[parts:-1], refs[-1]
     docs, chunks, exp_local, lanes = feats[0].shape
-    vals = val_ref.shape[0] * val_ref.shape[1]
+    each = pieces[0].shape[0]
+    vals = len(pieces) * each
     left_rows, right_rows = parts * docs * exp_local, vals * exp_local
     total = jnp.zeros((left_rows, right_rows), F32)
     for c in range(chunks):
         left = jnp.concatenate(
             [feat[:, c].reshape(docs * exp_local, lanes) for feat in feats], axis=0
         )
-        right = val_ref[:, :, :, c * lanes : (c + 1) * lanes].reshape(right_rows, lanes)
+        right = jnp.concatenate(
+            [
+                val[:, :, c * lanes : (c + 1) * lanes].reshape(each * exp_local, lanes)
+                for val in pieces
+            ],
+            axis=0,
+        )
         total += lax.dot_general(left, right, NT, preferred_element_type=F32)
     row = lax.broadcasted_iota(jnp.int32, total.shape, 0) % exp_local
     col = lax.broadcasted_iota(jnp.int32, total.shape, 1) % exp_local
     total = jnp.where(row == col, total, 0.0)
     total = jnp.sum(total.reshape(parts * docs, exp_local, right_rows), axis=1)
-    pick = (
-        lax.broadcasted_iota(jnp.int32, (right_rows, vals), 0) // exp_local
-        == lax.broadcasted_iota(jnp.int32, (right_rows, vals), 1)
-    ).astype(F32)
+    owner = lax.broadcasted_iota(jnp.int32, (right_rows, vals), 0) // exp_local
+    owner = lax.bitwise_xor(owner, mine_ref[0] * each)
+    pick = (owner == lax.broadcasted_iota(jnp.int32, (right_rows, vals), 1)).astype(F32)
     scores = jnp.dot(
         total, pick, preferred_element_type=F32, precision=lax.Precision.HIGHEST
     ) * scale
     for k in range(parts):
-        group = lax.bitwise_xor(mine_ref[0], k)
+        group = lax.bitwise_xor(mine_ref[0] % parts, k)
         for i in range(out_ref.shape[0] // parts):
             out_ref[i * parts + group] = scores[k * docs : (k + 1) * docs, :]
 
@@ -225,21 +230,24 @@
 
     vmem = pl.BlockSpec(memory_space=pltpu.VMEM)
     hbm = pl.BlockSpec(memory_space=pltpu.HBM)
-    val_split = pl.pallas_call(
+    smem = pl.BlockSpec(memory_space=pltpu.SMEM)
+    mine = lax.axis_index("lo").astype(jnp.int32).reshape(1)
+    pieces = pl.pallas_call(
         split_kernel,
-        out_shape=jax.ShapeDtypeStruct((dp, vals, exp_local, entries // lo), BF16),
-        in_specs=[hbm],
-        out_specs=hbm,
+        out_shape=(jax.ShapeDtypeStruct((vals, exp_local, entries // lo), BF16),) * lo,
+        in_specs=[smem, hbm],
+        out_specs=(hbm,) * lo,
         scratch_shapes=[
             pltpu.VMEM((lo, vals, exp_local, entries // lo), BF16),
-            pltpu.SemaphoreType.DMA((lo,)),
-            pltpu.SemaphoreType.DMA((dp,)),
+            pltpu.SemaphoreType.DMA((lo, 2)),
         ],
         compiler_params=pltpu.CompilerParams(vmem_limit_bytes=VL_A),
-    )(val_features)
-    val_all = lax.all_to_all(
-        val_split, ("hi", "lo"), split_axis=0, concat_axis=0, tiled=True
-    )
+    )(mine, val_features)
+    val_all = [pieces[0]] * dp
+    for k in range(dp - 1, 0, -1):
+        val_all[k] = lax.ppermute(
+            pieces[k % lo], ("hi", "lo"), [(a, a ^ k) for a in range(dp)]
+        )
 
     pay_rows = rank + 2 * top + 8
     steps = 2
@@ -289,8 +297,6 @@
     )(hidden_grad, proj_out.transpose(0, 2, 1))
 
     me = lax.axis_index("expert").astype(jnp.int32).reshape(1)
-    mine = lax.axis_index("lo").astype(jnp.int32).reshape(1)
-    smem = pl.BlockSpec(memory_space=pltpu.SMEM)
     block = jax.ShapeDtypeStruct((DOC_GRP, chunks, exp_local, LANES), BF16)
     feats = pl.pallas_call(
         functools.partial(feature_kernel, groups, lo, rank, top),
@@ -314,10 +320,10 @@
     part = pl.pallas_call(
         functools.partial(score_kernel, lo, scale),
         out_shape=jax.ShapeDtypeStruct((groups * lo, DOC_GRP, dp * vals), F32),
-        in_specs=[smem] + [vmem] * (lo + 1),
+        in_specs=[smem] + [vmem] * (lo + dp),
         out_specs=vmem,
         compiler_params=pltpu.CompilerParams(vmem_limit_bytes=40 << 20),
-    )(mine, *arrived, val_all)
+    )(lax.axis_index(("hi", "lo")).astype(jnp.int32).reshape(1), *arrived, *val_all)
     parts = lax.all_to_all(part, ("expert", "lo"), split_axis=0, concat_axis=0, tiled=True)
     return jnp.sum(parts, axis=0)
 

time: 47.1 us -> 49.7 us (1.055)
  starting transfers between devices: 12.8 us -> 17.7 us
  Pallas kernels: 12.3 us -> 10.8 us
    ppermute x0 -> x7, starting transfers between devices: none -> 12.2 us  [layer(): lax.ppermute(pieces[k % lo], ('hi', 'lo'), [(a, a ^ k) for a in range(dp)])]
    ppermute x0 -> x7, waiting for transfers between devices: none -> 8.56 us  [layer(): lax.ppermute(pieces[k % lo], ('hi', 'lo'), [(a, a ^ k) for a in range(dp)])]
    all_to_all x1 -> x0, starting transfers between devices: 7.29 us -> none  [layer(): lax.all_to_all(val_split, ('hi', 'lo'), split_axis=0, concat_axis=0, tile...]
    all_to_all x1 -> x0, waiting for transfers between devices: 5.44 us -> none  [layer(): lax.all_to_all(val_split, ('hi', 'lo'), split_axis=0, concat_axis=0, tile...]
    ppermute x3, waiting for transfers between devices: 6.43 us -> 2.96 us  [layer(): lax.ppermute(feats[k], 'lo', [(a, a ^ k) for a in range(lo)])]
    pallas_call x1, Pallas kernels: 1.89 us -> 0.67 us  [layer(): pl.pallas_call(functools.partial(score_kernel, lo, scale), out_shape=jax....]
  transfers between devices with their start and end apart: 7 -> 13, of which waited for: 4 -> 6; matrix products, arithmetic and copies ran while one was open for 0% -> 0% of each run, Pallas kernels for 18% -> 17%
where the time goes in v7:
time: 49.7 us; the launch traced here: 49.5 us
  starting transfers between devices  17.7 us (36%)
  waiting for transfers between devices  11.5 us (23%)
  Pallas kernels  10.8 us (22%)
  blocking collectives  8.65 us (17%)
  other arithmetic  0.59 us (1%)
    ppermute x7, starting transfers between devices, layer(): lax.ppermute(pieces[k % lo], ('hi', 'lo'), [(a, a ^ k) for a in range(dp)])  12.2 us
    all_to_all x1, blocking collectives, layer(): lax.all_to_all(part, ('expert', 'lo'), split_axis=0, concat_axis=0, tiled...  8.65 us
    ppermute x7, waiting for transfers between devices, layer(): lax.ppermute(pieces[k % lo], ('hi', 'lo'), [(a, a ^ k) for a in range(dp)])  8.56 us
    pallas_call x1, Pallas kernels, layer(): pl.pallas_call(lowered_kernel, out_shape=jax.ShapeDtypeStruct((exp_local,...  4.44 us
    ppermute x3, starting transfers between devices, layer(): lax.ppermute(feats[k], 'lo', [(a, a ^ k) for a in range(lo)])  3.55 us
    ppermute x3, waiting for transfers between devices, layer(): lax.ppermute(feats[k], 'lo', [(a, a ^ k) for a in range(lo)])  2.96 us
    pallas_call x1, Pallas kernels, layer(): pl.pallas_call(act_kernel, out_shape=jax.ShapeDtypeStruct((pay_rows, tok)...  2.57 us
    ppermute x3, starting transfers between devices, layer(): lax.ppermute(pay, 'expert', [(a, a ^ k) for a in range(groups)])  1.92 us
  transfers between devices with their start and end apart: 13, of which 6 were waited for; matrix products, arithmetic and copies ran while one was open for 0% of the time, Pallas kernels for 17%

profile of v7, /device:TPU:0, one launch (start us, length us, event | category | flops | bytes accessed | tf_op | source)
XLA Modules:
  0.0 49.5 jit_solution(13794378807632022001)
XLA Ops:
  0.0 1.8 %shard_map.85 = (bf16[4,16,1024]{2,1,0:T(8,128)(2,1)}, bf16[4,16,1024]{2,1,0:T(8,128)(2,1)}, bf16[4,16,1024]{2,1,0:T(8,128)(2,1)}, bf16[4,16,1024]{2,1,0:T(8,128)(2,1)}) custom-call(s32[1]{0:T(128)} %bitcast.2.mine_ref, bf16[4,16,4096]{2,1,0:T(8,128)(2,1)} %val_hbm.1), custom_call_target="tpu_custom_call" | custom-call | tf_op jit(solution)/shard_map/pallas_call | solution.py:235
  1.8 0.0 copy-start.4
  1.8 0.0 copy-start.3
  1.8 0.0 copy-start.2
  1.8 0.0 copy-start.1
  1.9 5.1 %collective-permute-start.10 = (bf16[4,16,1024]{2,1,0:T(8,128)(2,1)}, bf16[4,16,1024]{2,1,0:T(8,128)(2,1)S(1)}, u32[]{:S(2)}, u32[]{:S(2)}) collective-permute-start(bf16[4,16,1024]{2,1,0:T(8,128)(2,1)} %get-tuple-element.18), channel_id=1, source_target_pairs={{0,5},{1,4},{2,7},{3,6},{4,1},{5,0},{6,3},{7,2},{8,13},{9,12},{10,... | collective-permute-start | bytes 393224 | tf_op jit(solution)/shard_map/ppermute | solution.py:248
  6.9 1.3 %collective-permute-start.11 = (bf16[4,16,1024]{2,1,0:T(8,128)(2,1)}, bf16[4,16,1024]{2,1,0:T(8,128)(2,1)S(1)}, u32[]{:S(2)}, u32[]{:S(2)}) collective-permute-start(bf16[4,16,1024]{2,1,0:T(8,128)(2,1)} %get-tuple-element.19), channel_id=1, source_target_pairs={{0,6},{1,7},{2,4},{3,5},{4,2},{5,3},{6,0},{7,1},{8,14},{9,15},{10,... | collective-permute-start | bytes 393224 | tf_op jit(solution)/shard_map/ppermute | solution.py:248
  8.3 2.6 %shard_map.82.refs_0_ = f32[88,128]{1,0:T(8,128)} custom-call(bf16[128,4096]{1,0:T(8,128)(2,1)} %tok_hbm.1, bf16[64,4096]{1,0:T(8,128)(2,1)} %bitcast.9, s32[8,128]{1,0:T(8,128)} %bitcast.10, f32[8,128]{1,0:T(8,128)} %bitcast.11, s32[1,128]{1,0:T(1,128)} %bitcast.12), custom_call_target="tpu_custom_call" | custom-call | flops 67108864 | bytes 1572864 | tf_op jit(solution)/shard_map/pallas_call | solution.py:254
  10.8 0.0 copy-start
  10.8 0.1 collective-permute-start
  10.9 1.6 %collective-permute-start.1 = (f32[88,128]{1,0:T(8,128)}, f32[88,128]{1,0:T(8,128)S(1)}, u32[]{:S(2)}, u32[]{:S(2)}) collective-permute-start(f32[88,128]{1,0:T(8,128)} %shard_map.82.refs_0_), channel_id=1, source_target_pairs={{0,16},{8,24},{16,0},{24,8},{1,17},{9,25},{17,1},{25,9},{2,18},{10... | collective-permute-start | bytes 135176 | tf_op jit(solution)/shard_map/ppermute | solution.py:279
  12.5 0.3 collective-permute-start.2
  12.8 4.4 %shard_map.83.refs_4_ = bf16[16,128,128]{2,1,0:T(8,128)(2,1)S(1)} custom-call(bf16[16,128,1536]{2,1,0:T(8,128)(2,1)} %grad_hbm.1, bf16[16,64,1536]{2,1,0:T(8,128)(2,1)} %bitcast.8), custom_call_target="tpu_custom_call" | custom-call | flops 402653184 | bytes 9437184 | tf_op jit(solution)/shard_map/pallas_call | solution.py:281
  17.2 0.0 collective-permute-done.refs_1_
  17.2 0.0 collective-permute-done.1.refs_2_
  17.2 0.0 collective-permute-done.2.refs_3_
  17.3 0.0 copy-done
  17.3 1.4 %shard_map.84 = (bf16[2,8,16,128]{3,2,1,0:T(8,128)(2,1)S(1)}, bf16[2,8,16,128]{3,2,1,0:T(8,128)(2,1)S(1)}, bf16[2,8,16,128]{3,2,1,0:T(8,128)(2,1)S(1)}, bf16[2,8,16,128]{3,2,1,0:T(8,128)(2,1)S(1)}) custom-call(s32[1]{0:T(128)} %bitcast.1.me_ref, s32[1]{0:T(128)} %bitcast.2.mine_ref, f32[88,128]{1,0:T(8,128)S(1)} %copy-done, ...), custom_call_target="tpu_custom_call" | custom-call | flops 134217728 | bytes 1048576 | tf_op jit(solution)/shard_map/pallas_call | solution.py:301
  18.6 0.6 %collective-permute-start.3 = (bf16[2,8,16,128]{3,2,1,0:T(8,128)(2,1)S(1)}, bf16[2,8,16,128]{3,2,1,0:T(8,128)(2,1)S(1)}, u32[]{:S(2)}, u32[]{:S(2)}) collective-permute-start(bf16[2,8,16,128]{3,2,1,0:T(8,128)(2,1)S(1)} %get-tuple-element.14), channel_id=1, source_target_pairs={{0,1},{1,0},{2,3},{3,2},{4,5},{5,4},{6,7},{7,6},{8,9},{9,8},{10,11... | collective-permute-start | bytes 196616 | tf_op jit(solution)/shard_map/ppermute | solution.py:317
  19.2 0.2 collective-permute-start.4
  19.5 2.7 %collective-permute-start.5 = (bf16[2,8,16,128]{3,2,1,0:T(8,128)(2,1)S(1)}, bf16[2,8,16,128]{3,2,1,0:T(8,128)(2,1)S(1)}, u32[]{:S(2)}, u32[]{:S(2)}) collective-permute-start(bf16[2,8,16,128]{3,2,1,0:T(8,128)(2,1)S(1)} %get-tuple-element.16), channel_id=1, source_target_pairs={{0,3},{1,2},{2,1},{3,0},{4,7},{5,6},{6,5},{7,4},{8,11},{9,10},{10,... | collective-permute-start | bytes 196616 | tf_op jit(solution)/shard_map/ppermute | solution.py:317
  22.2 0.9 %collective-permute-done.3.refs_1_ = bf16[2,8,16,128]{3,2,1,0:T(8,128)(2,1)S(1)} collective-permute-done((bf16[2,8,16,128]{3,2,1,0:T(8,128)(2,1)S(1)}, bf16[2,8,16,128]{3,2,1,0:T(8,128)(2,1)S(1)}, u32[]{:S(2)}, u32[]{:S(2)}) %collective-permute-start.3) | collective-permute-done | bytes 65568 | tf_op jit(solution)/shard_map/ppermute | solution.py:317
  23.1 0.0 copy-done.4
  23.1 0.5 %collective-permute-start.6 = (bf16[4,16,1024]{2,1,0:T(8,128)(2,1)S(1)}, bf16[4,16,1024]{2,1,0:T(8,128)(2,1)S(1)}, u32[]{:S(2)}, u32[]{:S(2)}) collective-permute-start(bf16[4,16,1024]{2,1,0:T(8,128)(2,1)S(1)} %copy-done.4), channel_id=1, source_target_pairs={{0,1},{1,0},{2,3},{3,2},{4,5},{5,4},{6,7},{7,6},{8,9},{9,8},{10,11... | collective-permute-start | bytes 393224 | tf_op jit(solution)/shard_map/ppermute | solution.py:248
  23.6 0.6 %collective-permute-done.4.refs_2_ = bf16[2,8,16,128]{3,2,1,0:T(8,128)(2,1)S(1)} collective-permute-done((bf16[2,8,16,128]{3,2,1,0:T(8,128)(2,1)S(1)}, bf16[2,8,16,128]{3,2,1,0:T(8,128)(2,1)S(1)}, u32[]{:S(2)}, u32[]{:S(2)}) %collective-permute-start.4) | collective-permute-done | bytes 65568 | tf_op jit(solution)/shard_map/ppermute | solution.py:317
  24.2 0.0 copy-done.3
  24.2 0.0 collective-permute-start.7
  24.2 1.5 %collective-permute-done.5.refs_3_ = bf16[2,8,16,128]{3,2,1,0:T(8,128)(2,1)S(1)} collective-permute-done((bf16[2,8,16,128]{3,2,1,0:T(8,128)(2,1)S(1)}, bf16[2,8,16,128]{3,2,1,0:T(8,128)(2,1)S(1)}, u32[]{:S(2)}, u32[]{:S(2)}) %collective-permute-start.5) | collective-permute-done | bytes 65568 | tf_op jit(solution)/shard_map/ppermute | solution.py:317
  25.7 0.0 copy-done.2
  25.7 2.9 %collective-permute-start.12 = (bf16[4,16,1024]{2,1,0:T(8,128)(2,1)S(1)}, bf16[4,16,1024]{2,1,0:T(8,128)(2,1)S(1)}, u32[]{:S(2)}, u32[]{:S(2)}) collective-permute-start(bf16[4,16,1024]{2,1,0:T(8,128)(2,1)S(1)} %copy-done.2), channel_id=1, source_target_pairs={{0,7},{1,6},{2,5},{3,4},{4,3},{5,2},{6,1},{7,0},{8,15},{9,14},{10,... | collective-permute-start | bytes 393224 | tf_op jit(solution)/shard_map/ppermute | solution.py:248
  28.6 0.0 collective-permute-done.10.refs_9_
  28.6 0.5 collective-permute-start.8
  29.1 0.0 collective-permute-done.11.refs_10_
  29.1 0.0 copy-done.1
  29.1 1.9 %collective-permute-start.9 = (bf16[4,16,1024]{2,1,0:T(8,128)(2,1)S(1)}, bf16[4,16,1024]{2,1,0:T(8,128)(2,1)S(1)}, u32[]{:S(2)}, u32[]{:S(2)}) collective-permute-start(bf16[4,16,1024]{2,1,0:T(8,128)(2,1)S(1)} %copy-done.1), channel_id=1, source_target_pairs={{0,4},{1,5},{2,6},{3,7},{4,0},{5,1},{6,2},{7,3},{8,12},{9,13},{10,... | collective-permute-start | bytes 393224 | tf_op jit(solution)/shard_map/ppermute | solution.py:248
  31.0 4.1 %collective-permute-done.12.refs_11_ = bf16[4,16,1024]{2,1,0:T(8,128)(2,1)S(1)} collective-permute-done((bf16[4,16,1024]{2,1,0:T(8,128)(2,1)S(1)}, bf16[4,16,1024]{2,1,0:T(8,128)(2,1)S(1)}, u32[]{:S(2)}, u32[]{:S(2)}) %collective-permute-start.12) | collective-permute-done | bytes 131104 | tf_op jit(solution)/shard_map/ppermute | solution.py:248
  35.1 0.0 collective-permute-done.6.refs_5_
  35.1 0.0 collective-permute-done.7.refs_6_
  35.1 3.1 %collective-permute-done.8.refs_7_ = bf16[4,16,1024]{2,1,0:T(8,128)(2,1)S(1)} collective-permute-done((bf16[4,16,1024]{2,1,0:T(8,128)(2,1)S(1)}, bf16[4,16,1024]{2,1,0:T(8,128)(2,1)S(1)}, u32[]{:S(2)}, u32[]{:S(2)}) %collective-permute-start.8) | collective-permute-done | bytes 131104 | tf_op jit(solution)/shard_map/ppermute | solution.py:248
  38.2 1.4 %collective-permute-done.9.refs_8_ = bf16[4,16,1024]{2,1,0:T(8,128)(2,1)S(1)} collective-permute-done((bf16[4,16,1024]{2,1,0:T(8,128)(2,1)S(1)}, bf16[4,16,1024]{2,1,0:T(8,128)(2,1)S(1)}, u32[]{:S(2)}, u32[]{:S(2)}) %collective-permute-start.9) | collective-permute-done | bytes 131104 | tf_op jit(solution)/shard_map/ppermute | solution.py:248
  39.5 0.7 %shard_map.86 = f32[16,2,32]{2,1,0:T(2,128)S(1)} custom-call(s32[1]{0:T(128)} %bitcast.mine_ref, bf16[2,8,16,128]{3,2,1,0:T(8,128)(2,1)S(1)} %get-tuple-element.13.refs_0_, bf16[2,8,16,128]{3,2,1,0:T(8,128)(2,1)S(1)} %collective-permute-done.3.refs_1_, bf16[2,8,16,128]{3,2,1,0:T(8,128)(2,1)S(1)} %collective-permute-done.4.refs_2_, ...), custom_call_target="tpu_custom_call" | custom-call | tf_op jit(solution)/shard_map/pallas_call | solution.py:320
  40.2 8.7 %all_to_all.5 = f32[16,2,32]{2,1,0:T(2,128)S(1)} all-to-all(f32[16,2,32]{2,1,0:T(2,128)S(1)} %shard_map.86), channel_id=1, replica_groups=mesh['expert'=4,'hi'=2,'lo'=4] {'expert','lo'}, dimensions={0} | all-to-all | bytes 8192 | tf_op jit(solution)/shard_map/all_to_all | solution.py:327
  48.9 0.6 %reduce_sum.9 = f32[2,32]{1,0:T(2,128)} reduce(f32[16,2,32]{2,1,0:T(2,128)S(1)} %all_to_all.5, f32[]{:T(128)} %constant.15.clone.1), dimensions={0}, to_apply=%region_0.0 | reduce | flops 960 | bytes 4356 | tf_op jit(solution)/shard_map/reduce_sum | solution.py:328
Async XLA Ops:
  1.8 21.2 %copy-start.4 = (bf16[4,16,1024]{2,1,0:T(8,128)(2,1)S(1)}, bf16[4,16,1024]{2,1,0:T(8,128)(2,1)}, u32[]{:S(2)}) copy-start(bf16[4,16,1024]{2,1,0:T(8,128)(2,1)} %get-tuple-element.18) | copy-start | bytes 393220
  1.8 22.3 %copy-start.3 = (bf16[4,16,1024]{2,1,0:T(8,128)(2,1)S(1)}, bf16[4,16,1024]{2,1,0:T(8,128)(2,1)}, u32[]{:S(2)}) copy-start(bf16[4,16,1024]{2,1,0:T(8,128)(2,1)} %get-tuple-element.19) | copy-start | bytes 393220
  1.8 23.9 %copy-start.2 = (bf16[4,16,1024]{2,1,0:T(8,128)(2,1)S(1)}, bf16[4,16,1024]{2,1,0:T(8,128)(2,1)}, u32[]{:S(2)}) copy-start(bf16[4,16,1024]{2,1,0:T(8,128)(2,1)} %get-tuple-element.20) | copy-start | bytes 393220
  1.8 27.2 %copy-start.1 = (bf16[4,16,1024]{2,1,0:T(8,128)(2,1)S(1)}, bf16[4,16,1024]{2,1,0:T(8,128)(2,1)}, u32[]{:S(2)}) copy-start(bf16[4,16,1024]{2,1,0:T(8,128)(2,1)} %get-tuple-element.17.refs_4_) | copy-start | bytes 393220
  1.9 26.7 %collective-permute-start.10 = (bf16[4,16,1024]{2,1,0:T(8,128)(2,1)}, bf16[4,16,1024]{2,1,0:T(8,128)(2,1)S(1)}, u32[]{:S(2)}, u32[]{:S(2)}) collective-permute-start(bf16[4,16,1024]{2,1,0:T(8,128)(2,1)} %get-tuple-element.18), channel_id=1, source_target_pairs={{0,5},{1,4},{2,7},{3,6},{4,1},{5,0},{6,3},{7,2},{8,13},{9,12},{10,... | collective-permute-start | bytes 393224 | tf_op jit(solution)/shard_map/ppermute | solution.py:248
  6.9 22.2 %collective-permute-start.11 = (bf16[4,16,1024]{2,1,0:T(8,128)(2,1)}, bf16[4,16,1024]{2,1,0:T(8,128)(2,1)S(1)}, u32[]{:S(2)}, u32[]{:S(2)}) collective-permute-start(bf16[4,16,1024]{2,1,0:T(8,128)(2,1)} %get-tuple-element.19), channel_id=1, source_target_pairs={{0,6},{1,7},{2,4},{3,5},{4,2},{5,3},{6,0},{7,1},{8,14},{9,15},{10,... | collective-permute-start | bytes 393224 | tf_op jit(solution)/shard_map/ppermute | solution.py:248
  10.8 6.4 %copy-start = (f32[88,128]{1,0:T(8,128)S(1)}, f32[88,128]{1,0:T(8,128)}, u32[]{:S(2)}) copy-start(f32[88,128]{1,0:T(8,128)} %shard_map.82.refs_0_) | copy-start | bytes 135172
  10.8 6.4 %collective-permute-start = (f32[88,128]{1,0:T(8,128)}, f32[88,128]{1,0:T(8,128)S(1)}, u32[]{:S(2)}, u32[]{:S(2)}) collective-permute-start(f32[88,128]{1,0:T(8,128)} %shard_map.82.refs_0_), channel_id=1, source_target_pairs={{0,8},{8,0},{16,24},{24,16},{1,9},{9,1},{17,25},{25,17},{2,10},{10... | collective-permute-start | bytes 135176 | tf_op jit(solution)/shard_map/ppermute | solution.py:279
  10.9 6.3 %collective-permute-start.1 = (f32[88,128]{1,0:T(8,128)}, f32[88,128]{1,0:T(8,128)S(1)}, u32[]{:S(2)}, u32[]{:S(2)}) collective-permute-start(f32[88,128]{1,0:T(8,128)} %shard_map.82.refs_0_), channel_id=1, source_target_pairs={{0,16},{8,24},{16,0},{24,8},{1,17},{9,25},{17,1},{25,9},{2,18},{10... | collective-permute-start | bytes 135176 | tf_op jit(solution)/shard_map/ppermute | solution.py:279
  12.5 4.7 %collective-permute-start.2 = (f32[88,128]{1,0:T(8,128)}, f32[88,128]{1,0:T(8,128)S(1)}, u32[]{:S(2)}, u32[]{:S(2)}) collective-permute-start(f32[88,128]{1,0:T(8,128)} %shard_map.82.refs_0_), channel_id=1, source_target_pairs={{0,24},{8,16},{16,8},{24,0},{1,25},{9,17},{17,9},{25,1},{2,26},{10... | collective-permute-start | bytes 135176 | tf_op jit(solution)/shard_map/ppermute | solution.py:279
  18.6 4.4 %collective-permute-start.3 = (bf16[2,8,16,128]{3,2,1,0:T(8,128)(2,1)S(1)}, bf16[2,8,16,128]{3,2,1,0:T(8,128)(2,1)S(1)}, u32[]{:S(2)}, u32[]{:S(2)}) collective-permute-start(bf16[2,8,16,128]{3,2,1,0:T(8,128)(2,1)S(1)} %get-tuple-element.14), channel_id=1, source_target_pairs={{0,1},{1,0},{2,3},{3,2},{4,5},{5,4},{6,7},{7,6},{8,9},{9,8},{10,11... | collective-permute-start | bytes 196616 | tf_op jit(solution)/shard_map/ppermute | solution.py:317
  19.2 4.9 %collective-permute-start.4 = (bf16[2,8,16,128]{3,2,1,0:T(8,128)(2,1)S(1)}, bf16[2,8,16,128]{3,2,1,0:T(8,128)(2,1)S(1)}, u32[]{:S(2)}, u32[]{:S(2)}) collective-permute-start(bf16[2,8,16,128]{3,2,1,0:T(8,128)(2,1)S(1)} %get-tuple-element.15), channel_id=1, source_target_pairs={{0,2},{1,3},{2,0},{3,1},{4,6},{5,7},{6,4},{7,5},{8,10},{9,11},{10,... | collective-permute-start | bytes 196616 | tf_op jit(solution)/shard_map/ppermute | solution.py:317
  19.5 6.2 %collective-permute-start.5 = (bf16[2,8,16,128]{3,2,1,0:T(8,128)(2,1)S(1)}, bf16[2,8,16,128]{3,2,1,0:T(8,128)(2,1)S(1)}, u32[]{:S(2)}, u32[]{:S(2)}) collective-permute-start(bf16[2,8,16,128]{3,2,1,0:T(8,128)(2,1)S(1)} %get-tuple-element.16), channel_id=1, source_target_pairs={{0,3},{1,2},{2,1},{3,0},{4,7},{5,6},{6,5},{7,4},{8,11},{9,10},{10,... | collective-permute-start | bytes 196616 | tf_op jit(solution)/shard_map/ppermute | solution.py:317
  23.1 12.0 %collective-permute-start.6 = (bf16[4,16,1024]{2,1,0:T(8,128)(2,1)S(1)}, bf16[4,16,1024]{2,1,0:T(8,128)(2,1)S(1)}, u32[]{:S(2)}, u32[]{:S(2)}) collective-permute-start(bf16[4,16,1024]{2,1,0:T(8,128)(2,1)S(1)} %copy-done.4), channel_id=1, source_target_pairs={{0,1},{1,0},{2,3},{3,2},{4,5},{5,4},{6,7},{7,6},{8,9},{9,8},{10,11... | collective-permute-start | bytes 393224 | tf_op jit(solution)/shard_map/ppermute | solution.py:248
  24.2 10.9 %collective-permute-start.7 = (bf16[4,16,1024]{2,1,0:T(8,128)(2,1)S(1)}, bf16[4,16,1024]{2,1,0:T(8,128)(2,1)S(1)}, u32[]{:S(2)}, u32[]{:S(2)}) collective-permute-start(bf16[4,16,1024]{2,1,0:T(8,128)(2,1)S(1)} %copy-done.3), channel_id=1, source_target_pairs={{0,2},{1,3},{2,0},{3,1},{4,6},{5,7},{6,4},{7,5},{8,10},{9,11},{10,... | collective-permute-start | bytes 393224 | tf_op jit(solution)/shard_map/ppermute | solution.py:248
  25.7 9.4 %collective-permute-start.12 = (bf16[4,16,1024]{2,1,0:T(8,128)(2,1)S(1)}, bf16[4,16,1024]{2,1,0:T(8,128)(2,1)S(1)}, u32[]{:S(2)}, u32[]{:S(2)}) collective-permute-start(bf16[4,16,1024]{2,1,0:T(8,128)(2,1)S(1)} %copy-done.2), channel_id=1, source_target_pairs={{0,7},{1,6},{2,5},{3,4},{4,3},{5,2},{6,1},{7,0},{8,15},{9,14},{10,... | collective-permute-start | bytes 393224 | tf_op jit(solution)/shard_map/ppermute | solution.py:248
  28.6 9.6 %collective-permute-start.8 = (bf16[4,16,1024]{2,1,0:T(8,128)(2,1)S(1)}, bf16[4,16,1024]{2,1,0:T(8,128)(2,1)S(1)}, u32[]{:S(2)}, u32[]{:S(2)}) collective-permute-start(bf16[4,16,1024]{2,1,0:T(8,128)(2,1)S(1)} %copy-done.2), channel_id=1, source_target_pairs={{0,3},{1,2},{2,1},{3,0},{4,7},{5,6},{6,5},{7,4},{8,11},{9,10},{10,... | collective-permute-start | bytes 393224 | tf_op jit(solution)/shard_map/ppermute | solution.py:248
  29.1 10.5 %collective-permute-start.9 = (bf16[4,16,1024]{2,1,0:T(8,128)(2,1)S(1)}, bf16[4,16,1024]{2,1,0:T(8,128)(2,1)S(1)}, u32[]{:S(2)}, u32[]{:S(2)}) collective-permute-start(bf16[4,16,1024]{2,1,0:T(8,128)(2,1)S(1)} %copy-done.1), channel_id=1, source_target_pairs={{0,4},{1,5},{2,6},{3,7},{4,0},{5,1},{6,2},{7,3},{8,12},{9,13},{10,... | collective-permute-start | bytes 393224 | tf_op jit(solution)/shard_map/ppermute | solution.py:248

commit v8 on v7

--- a/solution.py
+++ b/solution.py
@@ -21,22 +21,8 @@
 TN = (((0,), (0,)), ((), ()))
 
 
-def split_kernel(mine_ref, val_hbm, *refs):
-    outs, (piece_ref, sems) = refs[:-2], refs[-2:]
-    parts, _, _, piece = piece_ref.shape
-    ins, puts = [], []
-    for k in range(parts):
-        part = lax.bitwise_xor(mine_ref[0], k)
-        cols = pl.ds(pl.multiple_of(part * piece, piece), piece)
-        ins.append(pltpu.make_async_copy(val_hbm.at[:, :, cols], piece_ref.at[k], sems.at[k, 0]))
-        puts.append(pltpu.make_async_copy(piece_ref.at[k], outs[k], sems.at[k, 1]))
-    for copy in ins:
-        copy.start()
-    for k in range(parts):
-        ins[k].wait()
-        puts[k].start()
-    for copy in puts:
-        copy.wait()
+def start_order(dp, lo):
+    return sorted(range(dp - 1, 0, -1), key=lambda k: (k < lo, k % 2 if k >= lo else 0))
 
 
 def act_kernel(tok_hbm, proj_hbm, routes_hbm, gates_hbm, docs_hbm, out_ref, *scratch):
@@ -232,25 +218,19 @@
     hbm = pl.BlockSpec(memory_space=pltpu.HBM)
     smem = pl.BlockSpec(memory_space=pltpu.SMEM)
     mine = lax.axis_index("lo").astype(jnp.int32).reshape(1)
-    pieces = pl.pallas_call(
-        split_kernel,
-        out_shape=(jax.ShapeDtypeStruct((vals, exp_local, entries // lo), BF16),) * lo,
-        in_specs=[smem, hbm],
-        out_specs=(hbm,) * lo,
-        scratch_shapes=[
-            pltpu.VMEM((lo, vals, exp_local, entries // lo), BF16),
-            pltpu.SemaphoreType.DMA((lo, 2)),
-        ],
-        compiler_params=pltpu.CompilerParams(vmem_limit_bytes=VL_A),
-    )(mine, val_features)
+    piece = entries // lo
+    pieces = [
+        lax.dynamic_slice_in_dim(val_features, lax.bitwise_xor(mine[0], k) * piece, piece, 2)
+        for k in range(lo)
+    ]
     val_all = [pieces[0]] * dp
-    for k in range(dp - 1, 0, -1):
+    for k in start_order(dp, lo):
         val_all[k] = lax.ppermute(
             pieces[k % lo], ("hi", "lo"), [(a, a ^ k) for a in range(dp)]
         )
 
     pay_rows = rank + 2 * top + 8
-    steps = 2
+    steps = 1
     pay = pl.pallas_call(
         act_kernel,
         out_shape=jax.ShapeDtypeStruct((pay_rows, tok), F32),
@@ -312,9 +292,9 @@
             flops=8 * exp_local * rows * rank * tok, bytes_accessed=1 << 20, transcendentals=0
         ),
     )(me, mine, *pays, low)
-    arrived = [feats[0]]
-    for k in range(1, lo):
-        arrived.append(lax.ppermute(feats[k], "lo", [(a, a ^ k) for a in range(lo)]))
+    arrived = [feats[0]] * lo
+    for k in range(lo - 1, 0, -1):
+        arrived[k] = lax.ppermute(feats[k], "lo", [(a, a ^ k) for a in range(lo)])
 
     scale = 1.0 / float(experts * entries) ** 0.5
     part = pl.pallas_call(

time: 49.7 us -> 56.6 us (1.14)
  blocking collectives: 8.65 us -> 13.9 us
  starting transfers between devices: 17.7 us -> 19.9 us
  Pallas kernels: 10.8 us -> 9.06 us
  local copies, waits for them, and re-layouts: 0.02 us -> 1.14 us
    all_to_all x1, blocking collectives: 8.65 us -> 13.9 us  [layer(): lax.all_to_all(part, ('expert', 'lo'), split_axis=0, concat_axis=0, tiled...]
    ppermute x7, waiting for transfers between devices: 8.56 us -> 10.9 us  [layer(): lax.ppermute(pieces[k % lo], ('hi', 'lo'), [(a, a ^ k) for a in range(dp)])]
    ppermute x7, starting transfers between devices: 12.2 us -> 14.4 us  [layer(): lax.ppermute(pieces[k % lo], ('hi', 'lo'), [(a, a ^ k) for a in range(dp)])]
    ppermute x3, waiting for transfers between devices: 2.96 us -> 0.87 us  [layer(): arrived[k] = lax.ppermute(feats[k], 'lo', [(a, a ^ k) for a in range(lo)])]
    pallas_call x1 -> x0, Pallas kernels: 1.81 us -> none  [layer(): pl.pallas_call(split_kernel, out_shape=(jax.ShapeDtypeStruct((vals, exp_l...]
    dynamic_slice x0 -> x1, local copies, waits for them, and re-layouts: none -> 1.13 us  [layer(): lax.dynamic_slice_in_dim(val_features, lax.bitwise_xor(mine[0], k) * piec...]
  transfers between devices with their start and end apart: 13 -> 13, of which waited for: 6 -> 3; matrix products, arithmetic and copies ran while one was open for 0% -> 0% of each run, Pallas kernels for 17% -> 15%
where the time goes in v8:
time: 56.6 us; the launch traced here: 56.4 us
  starting transfers between devices  19.9 us (35%)
  blocking collectives  13.9 us (25%)
  waiting for transfers between devices  11.8 us (21%)
  Pallas kernels  9.06 us (16%)
  local copies, waits for them, and re-layouts  1.14 us (2%)
  other arithmetic  0.59 us (1%)
    ppermute x7, starting transfers between devices, layer(): lax.ppermute(pieces[k % lo], ('hi', 'lo'), [(a, a ^ k) for a in range(dp)])  14.4 us
    all_to_all x1, blocking collectives, layer(): lax.all_to_all(part, ('expert', 'lo'), split_axis=0, concat_axis=0, tiled...  13.9 us
    ppermute x7, waiting for transfers between devices, layer(): lax.ppermute(pieces[k % lo], ('hi', 'lo'), [(a, a ^ k) for a in range(dp)])  10.9 us
    pallas_call x1, Pallas kernels, layer(): pl.pallas_call(lowered_kernel, out_shape=jax.ShapeDtypeStruct((exp_local,...  4.44 us
    ppermute x3, starting transfers between devices, layer(): arrived[k] = lax.ppermute(feats[k], 'lo', [(a, a ^ k) for a in range(lo)])  3.55 us
    pallas_call x1, Pallas kernels, layer(): pl.pallas_call(act_kernel, out_shape=jax.ShapeDtypeStruct((pay_rows, tok)...  2.57 us
    ppermute x3, starting transfers between devices, layer(): lax.ppermute(pay, 'expert', [(a, a ^ k) for a in range(groups)])  1.92 us
    pallas_call x1, Pallas kernels, layer(): pl.pallas_call(functools.partial(feature_kernel, groups, lo, rank, top),...  1.36 us
  transfers between devices with their start and end apart: 13, of which 3 were waited for; matrix products, arithmetic and copies ran while one was open for 0% of the time, Pallas kernels for 15%

profile of v8, /device:TPU:0, one launch (start us, length us, event | category | flops | bytes accessed | tf_op | source)
XLA Modules:
  0.0 56.4 jit_solution(9940718214236613598)
XLA Ops:
  0.0 1.1 %constant_dynamic-slice_fusion = (bf16[4,16,1024]{2,1,0:T(8,128)(2,1)S(1)}, bf16[4,16,1024]{2,1,0:T(8,128)(2,1)S(1)}, bf16[4,16,1024]{2,1,0:T(8,128)(2,1)S(1)}, bf16[4,16,1024]{2,1,0:T(8,128)(2,1)S(1)}) fusion(bf16[4,16,4096]{2,1,0:T(8,128)(2,1)} %param.15, s32[]{:T(128)S(6)} %select_n.15, s32[]{:T(128)S(6)} %select_n.13, s32[]{:T(128)S(6)} %select_n.12, ...), kind=kLoop, calls=%fused_computation | loop fusion | bytes 1048592 | tf_op jit(solution)/shard_map/dynamic_slice | solution.py:223
  1.1 3.0 %collective-permute-start.6 = (bf16[4,16,1024]{2,1,0:T(8,128)(2,1)S(1)}, bf16[4,16,1024]{2,1,0:T(8,128)(2,1)S(1)}, u32[]{:S(2)}, u32[]{:S(2)}) collective-permute-start(bf16[4,16,1024]{2,1,0:T(8,128)(2,1)S(1)} %get-tuple-element.14), channel_id=1, source_target_pairs={{0,1},{1,0},{2,3},{3,2},{4,5},{5,4},{6,7},{7,6},{8,9},{9,8},{10,11... | collective-permute-start | bytes 393224 | tf_op jit(solution)/shard_map/ppermute | solution.py:228
  4.2 1.6 %collective-permute-start.7 = (bf16[4,16,1024]{2,1,0:T(8,128)(2,1)S(1)}, bf16[4,16,1024]{2,1,0:T(8,128)(2,1)S(1)}, u32[]{:S(2)}, u32[]{:S(2)}) collective-permute-start(bf16[4,16,1024]{2,1,0:T(8,128)(2,1)S(1)} %get-tuple-element.16), channel_id=1, source_target_pairs={{0,2},{1,3},{2,0},{3,1},{4,6},{5,7},{6,4},{7,5},{8,10},{9,11},{10,... | collective-permute-start | bytes 393224 | tf_op jit(solution)/shard_map/ppermute | solution.py:228
  5.8 2.6 %shard_map.82.refs_0_ = f32[88,128]{1,0:T(8,128)} custom-call(bf16[128,4096]{1,0:T(8,128)(2,1)} %tok_hbm.1, bf16[64,4096]{1,0:T(8,128)(2,1)} %bitcast.9, s32[8,128]{1,0:T(8,128)} %bitcast.10, f32[8,128]{1,0:T(8,128)} %bitcast.11, s32[1,128]{1,0:T(1,128)} %bitcast.12), custom_call_target="tpu_custom_call" | custom-call | flops 67108864 | bytes 1572864 | tf_op jit(solution)/shard_map/pallas_call | solution.py:234
  8.3 0.0 copy-start
  8.3 0.1 collective-permute-start
  8.4 1.6 %collective-permute-start.1 = (f32[88,128]{1,0:T(8,128)}, f32[88,128]{1,0:T(8,128)S(1)}, u32[]{:S(2)}, u32[]{:S(2)}) collective-permute-start(f32[88,128]{1,0:T(8,128)} %shard_map.82.refs_0_), channel_id=1, source_target_pairs={{0,16},{8,24},{16,0},{24,8},{1,17},{9,25},{17,1},{25,9},{2,18},{10... | collective-permute-start | bytes 135176 | tf_op jit(solution)/shard_map/ppermute | solution.py:259
  10.0 0.3 collective-permute-start.2
  10.3 4.4 %shard_map.83.refs_4_ = bf16[16,128,128]{2,1,0:T(8,128)(2,1)S(1)} custom-call(bf16[16,128,1536]{2,1,0:T(8,128)(2,1)} %grad_hbm.1, bf16[16,64,1536]{2,1,0:T(8,128)(2,1)} %bitcast.8), custom_call_target="tpu_custom_call" | custom-call | flops 402653184 | bytes 9437184 | tf_op jit(solution)/shard_map/pallas_call | solution.py:261
  14.7 0.0 collective-permute-done.refs_1_
  14.7 0.0 collective-permute-done.1.refs_2_
  14.7 0.0 collective-permute-done.2.refs_3_
  14.7 0.0 copy-done
  14.8 1.4 %shard_map.84 = (bf16[2,8,16,128]{3,2,1,0:T(8,128)(2,1)S(1)}, bf16[2,8,16,128]{3,2,1,0:T(8,128)(2,1)S(1)}, bf16[2,8,16,128]{3,2,1,0:T(8,128)(2,1)S(1)}, bf16[2,8,16,128]{3,2,1,0:T(8,128)(2,1)S(1)}) custom-call(s32[1]{0:T(128)} %bitcast.1.me_ref, s32[1]{0:T(128)} %bitcast.2.mine_ref, f32[88,128]{1,0:T(8,128)S(1)} %copy-done, ...), custom_call_target="tpu_custom_call" | custom-call | flops 134217728 | bytes 1048576 | tf_op jit(solution)/shard_map/pallas_call | solution.py:281
  16.1 0.6 %collective-permute-start.3 = (bf16[2,8,16,128]{3,2,1,0:T(8,128)(2,1)S(1)}, bf16[2,8,16,128]{3,2,1,0:T(8,128)(2,1)S(1)}, u32[]{:S(2)}, u32[]{:S(2)}) collective-permute-start(bf16[2,8,16,128]{3,2,1,0:T(8,128)(2,1)S(1)} %get-tuple-element.10), channel_id=1, source_target_pairs={{0,1},{1,0},{2,3},{3,2},{4,5},{5,4},{6,7},{7,6},{8,9},{9,8},{10,11... | collective-permute-start | bytes 196616 | tf_op jit(solution)/shard_map/ppermute | solution.py:297
  16.7 0.2 collective-permute-start.4
  17.0 2.7 %collective-permute-start.5 = (bf16[2,8,16,128]{3,2,1,0:T(8,128)(2,1)S(1)}, bf16[2,8,16,128]{3,2,1,0:T(8,128)(2,1)S(1)}, u32[]{:S(2)}, u32[]{:S(2)}) collective-permute-start(bf16[2,8,16,128]{3,2,1,0:T(8,128)(2,1)S(1)} %get-tuple-element.12), channel_id=1, source_target_pairs={{0,3},{1,2},{2,1},{3,0},{4,7},{5,6},{6,5},{7,4},{8,11},{9,10},{10,... | collective-permute-start | bytes 196616 | tf_op jit(solution)/shard_map/ppermute | solution.py:297
  19.7 0.9 %collective-permute-done.3.refs_1_ = bf16[2,8,16,128]{3,2,1,0:T(8,128)(2,1)S(1)} collective-permute-done((bf16[2,8,16,128]{3,2,1,0:T(8,128)(2,1)S(1)}, bf16[2,8,16,128]{3,2,1,0:T(8,128)(2,1)S(1)}, u32[]{:S(2)}, u32[]{:S(2)}) %collective-permute-start.3) | collective-permute-done | bytes 65568 | tf_op jit(solution)/shard_map/ppermute | solution.py:297
  20.5 2.6 %collective-permute-start.10 = (bf16[4,16,1024]{2,1,0:T(8,128)(2,1)S(1)}, bf16[4,16,1024]{2,1,0:T(8,128)(2,1)S(1)}, u32[]{:S(2)}, u32[]{:S(2)}) collective-permute-start(bf16[4,16,1024]{2,1,0:T(8,128)(2,1)S(1)} %get-tuple-element.14), channel_id=1, source_target_pairs={{0,5},{1,4},{2,7},{3,6},{4,1},{5,0},{6,3},{7,2},{8,13},{9,12},{10,... | collective-permute-start | bytes 393224 | tf_op jit(solution)/shard_map/ppermute | solution.py:228
  23.1 0.0 collective-permute-done.4.refs_2_
  23.1 1.4 %collective-permute-start.8 = (bf16[4,16,1024]{2,1,0:T(8,128)(2,1)S(1)}, bf16[4,16,1024]{2,1,0:T(8,128)(2,1)S(1)}, u32[]{:S(2)}, u32[]{:S(2)}) collective-permute-start(bf16[4,16,1024]{2,1,0:T(8,128)(2,1)S(1)} %get-tuple-element.13), channel_id=1, source_target_pairs={{0,3},{1,2},{2,1},{3,0},{4,7},{5,6},{6,5},{7,4},{8,11},{9,10},{10,... | collective-permute-start | bytes 393224 | tf_op jit(solution)/shard_map/ppermute | solution.py:228
  24.5 0.0 collective-permute-done.5.refs_3_
  24.5 2.1 %collective-permute-start.9 = (bf16[4,16,1024]{2,1,0:T(8,128)(2,1)S(1)}, bf16[4,16,1024]{2,1,0:T(8,128)(2,1)S(1)}, u32[]{:S(2)}, u32[]{:S(2)}) collective-permute-start(bf16[4,16,1024]{2,1,0:T(8,128)(2,1)S(1)} %get-tuple-element.15.refs_4_), channel_id=1, source_target_pairs={{0,4},{1,5},{2,6},{3,7},{4,0},{5,1},{6,2},{7,3},{8,12},{9,13},{10,... | collective-permute-start | bytes 393224 | tf_op jit(solution)/shard_map/ppermute | solution.py:228
  26.6 0.0 collective-permute-done.6.refs_5_
  26.6 1.9 %collective-permute-start.11 = (bf16[4,16,1024]{2,1,0:T(8,128)(2,1)S(1)}, bf16[4,16,1024]{2,1,0:T(8,128)(2,1)S(1)}, u32[]{:S(2)}, u32[]{:S(2)}) collective-permute-start(bf16[4,16,1024]{2,1,0:T(8,128)(2,1)S(1)} %get-tuple-element.16), channel_id=1, source_target_pairs={{0,6},{1,7},{2,4},{3,5},{4,2},{5,3},{6,0},{7,1},{8,14},{9,15},{10,... | collective-permute-start | bytes 393224 | tf_op jit(solution)/shard_map/ppermute | solution.py:228
  28.4 0.0 collective-permute-done.7.refs_6_
  28.4 1.9 %collective-permute-start.12 = (bf16[4,16,1024]{2,1,0:T(8,128)(2,1)S(1)}, bf16[4,16,1024]{2,1,0:T(8,128)(2,1)S(1)}, u32[]{:S(2)}, u32[]{:S(2)}) collective-permute-start(bf16[4,16,1024]{2,1,0:T(8,128)(2,1)S(1)} %get-tuple-element.13), channel_id=1, source_target_pairs={{0,7},{1,6},{2,5},{3,4},{4,3},{5,2},{6,1},{7,0},{8,15},{9,14},{10,... | collective-permute-start | bytes 393224 | tf_op jit(solution)/shard_map/ppermute | solution.py:228
  30.4 1.5 %collective-permute-done.8.refs_7_ = bf16[4,16,1024]{2,1,0:T(8,128)(2,1)S(1)} collective-permute-done((bf16[4,16,1024]{2,1,0:T(8,128)(2,1)S(1)}, bf16[4,16,1024]{2,1,0:T(8,128)(2,1)S(1)}, u32[]{:S(2)}, u32[]{:S(2)}) %collective-permute-start.8) | collective-permute-done | bytes 131104 | tf_op jit(solution)/shard_map/ppermute | solution.py:228
  31.9 9.4 %collective-permute-done.9.refs_8_ = bf16[4,16,1024]{2,1,0:T(8,128)(2,1)S(1)} collective-permute-done((bf16[4,16,1024]{2,1,0:T(8,128)(2,1)S(1)}, bf16[4,16,1024]{2,1,0:T(8,128)(2,1)S(1)}, u32[]{:S(2)}, u32[]{:S(2)}) %collective-permute-start.9) | collective-permute-done | bytes 131104 | tf_op jit(solution)/shard_map/ppermute | solution.py:228
  41.3 0.0 collective-permute-done.10.refs_9_
  41.3 0.0 collective-permute-done.11.refs_10_
  41.3 0.0 collective-permute-done.12.refs_11_
  41.3 0.7 %shard_map.85 = f32[16,2,32]{2,1,0:T(2,128)S(1)} custom-call(s32[1]{0:T(128)} %bitcast.mine_ref, bf16[2,8,16,128]{3,2,1,0:T(8,128)(2,1)S(1)} %get-tuple-element.9.refs_0_, bf16[2,8,16,128]{3,2,1,0:T(8,128)(2,1)S(1)} %collective-permute-done.3.refs_1_, bf16[2,8,16,128]{3,2,1,0:T(8,128)(2,1)S(1)} %collective-permute-done.4.refs_2_, ...), custom_call_target="tpu_custom_call" | custom-call | tf_op jit(solution)/shard_map/pallas_call | solution.py:300
  42.0 13.9 %all_to_all.5 = f32[16,2,32]{2,1,0:T(2,128)S(1)} all-to-all(f32[16,2,32]{2,1,0:T(2,128)S(1)} %shard_map.85), channel_id=1, replica_groups=mesh['expert'=4,'hi'=2,'lo'=4] {'expert','lo'}, dimensions={0} | all-to-all | bytes 8192 | tf_op jit(solution)/shard_map/all_to_all | solution.py:307
  55.8 0.6 %reduce_sum.9 = f32[2,32]{1,0:T(2,128)} reduce(f32[16,2,32]{2,1,0:T(2,128)S(1)} %all_to_all.5, f32[]{:T(128)} %constant.27.clone.1), dimensions={0}, to_apply=%region_0.0 | reduce | flops 960 | bytes 4356 | tf_op jit(solution)/shard_map/reduce_sum | solution.py:308
Async XLA Ops:
  1.1 25.4 %collective-permute-start.6 = (bf16[4,16,1024]{2,1,0:T(8,128)(2,1)S(1)}, bf16[4,16,1024]{2,1,0:T(8,128)(2,1)S(1)}, u32[]{:S(2)}, u32[]{:S(2)}) collective-permute-start(bf16[4,16,1024]{2,1,0:T(8,128)(2,1)S(1)} %get-tuple-element.14), channel_id=1, source_target_pairs={{0,1},{1,0},{2,3},{3,2},{4,5},{5,4},{6,7},{7,6},{8,9},{9,8},{10,11... | collective-permute-start | bytes 393224 | tf_op jit(solution)/shard_map/ppermute | solution.py:228
  4.2 24.3 %collective-permute-start.7 = (bf16[4,16,1024]{2,1,0:T(8,128)(2,1)S(1)}, bf16[4,16,1024]{2,1,0:T(8,128)(2,1)S(1)}, u32[]{:S(2)}, u32[]{:S(2)}) collective-permute-start(bf16[4,16,1024]{2,1,0:T(8,128)(2,1)S(1)} %get-tuple-element.16), channel_id=1, source_target_pairs={{0,2},{1,3},{2,0},{3,1},{4,6},{5,7},{6,4},{7,5},{8,10},{9,11},{10,... | collective-permute-start | bytes 393224 | tf_op jit(solution)/shard_map/ppermute | solution.py:228
  8.3 6.4 %copy-start = (f32[88,128]{1,0:T(8,128)S(1)}, f32[88,128]{1,0:T(8,128)}, u32[]{:S(2)}) copy-start(f32[88,128]{1,0:T(8,128)} %shard_map.82.refs_0_) | copy-start | bytes 135172
  8.3 6.4 %collective-permute-start = (f32[88,128]{1,0:T(8,128)}, f32[88,128]{1,0:T(8,128)S(1)}, u32[]{:S(2)}, u32[]{:S(2)}) collective-permute-start(f32[88,128]{1,0:T(8,128)} %shard_map.82.refs_0_), channel_id=1, source_target_pairs={{0,8},{8,0},{16,24},{24,16},{1,9},{9,1},{17,25},{25,17},{2,10},{10... | collective-permute-start | bytes 135176 | tf_op jit(solution)/shard_map/ppermute | solution.py:259
  8.4 6.3 %collective-permute-start.1 = (f32[88,128]{1,0:T(8,128)}, f32[88,128]{1,0:T(8,128)S(1)}, u32[]{:S(2)}, u32[]{:S(2)}) collective-permute-start(f32[88,128]{1,0:T(8,128)} %shard_map.82.refs_0_), channel_id=1, source_target_pairs={{0,16},{8,24},{16,0},{24,8},{1,17},{9,25},{17,1},{25,9},{2,18},{10... | collective-permute-start | bytes 135176 | tf_op jit(solution)/shard_map/ppermute | solution.py:259
  10.0 4.7 %collective-permute-start.2 = (f32[88,128]{1,0:T(8,128)}, f32[88,128]{1,0:T(8,128)S(1)}, u32[]{:S(2)}, u32[]{:S(2)}) collective-permute-start(f32[88,128]{1,0:T(8,128)} %shard_map.82.refs_0_), channel_id=1, source_target_pairs={{0,24},{8,16},{16,8},{24,0},{1,25},{9,17},{17,9},{25,1},{2,26},{10... | collective-permute-start | bytes 135176 | tf_op jit(solution)/shard_map/ppermute | solution.py:259
  16.1 4.4 %collective-permute-start.3 = (bf16[2,8,16,128]{3,2,1,0:T(8,128)(2,1)S(1)}, bf16[2,8,16,128]{3,2,1,0:T(8,128)(2,1)S(1)}, u32[]{:S(2)}, u32[]{:S(2)}) collective-permute-start(bf16[2,8,16,128]{3,2,1,0:T(8,128)(2,1)S(1)} %get-tuple-element.10), channel_id=1, source_target_pairs={{0,1},{1,0},{2,3},{3,2},{4,5},{5,4},{6,7},{7,6},{8,9},{9,8},{10,11... | collective-permute-start | bytes 196616 | tf_op jit(solution)/shard_map/ppermute | solution.py:297
  16.7 6.4 %collective-permute-start.4 = (bf16[2,8,16,128]{3,2,1,0:T(8,128)(2,1)S(1)}, bf16[2,8,16,128]{3,2,1,0:T(8,128)(2,1)S(1)}, u32[]{:S(2)}, u32[]{:S(2)}) collective-permute-start(bf16[2,8,16,128]{3,2,1,0:T(8,128)(2,1)S(1)} %get-tuple-element.11), channel_id=1, source_target_pairs={{0,2},{1,3},{2,0},{3,1},{4,6},{5,7},{6,4},{7,5},{8,10},{9,11},{10,... | collective-permute-start | bytes 196616 | tf_op jit(solution)/shard_map/ppermute | solution.py:297
  17.0 7.5 %collective-permute-start.5 = (bf16[2,8,16,128]{3,2,1,0:T(8,128)(2,1)S(1)}, bf16[2,8,16,128]{3,2,1,0:T(8,128)(2,1)S(1)}, u32[]{:S(2)}, u32[]{:S(2)}) collective-permute-start(bf16[2,8,16,128]{3,2,1,0:T(8,128)(2,1)S(1)} %get-tuple-element.12), channel_id=1, source_target_pairs={{0,3},{1,2},{2,1},{3,0},{4,7},{5,6},{6,5},{7,4},{8,11},{9,10},{10,... | collective-permute-start | bytes 196616 | tf_op jit(solution)/shard_map/ppermute | solution.py:297
  20.5 20.7 %collective-permute-start.10 = (bf16[4,16,1024]{2,1,0:T(8,128)(2,1)S(1)}, bf16[4,16,1024]{2,1,0:T(8,128)(2,1)S(1)}, u32[]{:S(2)}, u32[]{:S(2)}) collective-permute-start(bf16[4,16,1024]{2,1,0:T(8,128)(2,1)S(1)} %get-tuple-element.14), channel_id=1, source_target_pairs={{0,5},{1,4},{2,7},{3,6},{4,1},{5,0},{6,3},{7,2},{8,13},{9,12},{10,... | collective-permute-start | bytes 393224 | tf_op jit(solution)/shard_map/ppermute | solution.py:228
  23.1 8.8 %collective-permute-start.8 = (bf16[4,16,1024]{2,1,0:T(8,128)(2,1)S(1)}, bf16[4,16,1024]{2,1,0:T(8,128)(2,1)S(1)}, u32[]{:S(2)}, u32[]{:S(2)}) collective-permute-start(bf16[4,16,1024]{2,1,0:T(8,128)(2,1)S(1)} %get-tuple-element.13), channel_id=1, source_target_pairs={{0,3},{1,2},{2,1},{3,0},{4,7},{5,6},{6,5},{7,4},{8,11},{9,10},{10,... | collective-permute-start | bytes 393224 | tf_op jit(solution)/shard_map/ppermute | solution.py:228
  24.5 16.8 %collective-permute-start.9 = (bf16[4,16,1024]{2,1,0:T(8,128)(2,1)S(1)}, bf16[4,16,1024]{2,1,0:T(8,128)(2,1)S(1)}, u32[]{:S(2)}, u32[]{:S(2)}) collective-permute-start(bf16[4,16,1024]{2,1,0:T(8,128)(2,1)S(1)} %get-tuple-element.15.refs_4_), channel_id=1, source_target_pairs={{0,4},{1,5},{2,6},{3,7},{4,0},{5,1},{6,2},{7,3},{8,12},{9,13},{10,... | collective-permute-start | bytes 393224 | tf_op jit(solution)/shard_map/ppermute | solution.py:228
  26.6 14.7 %collective-permute-start.11 = (bf16[4,16,1024]{2,1,0:T(8,128)(2,1)S(1)}, bf16[4,16,1024]{2,1,0:T(8,128)(2,1)S(1)}, u32[]{:S(2)}, u32[]{:S(2)}) collective-permute-start(bf16[4,16,1024]{2,1,0:T(8,128)(2,1)S(1)} %get-tuple-element.16), channel_id=1, source_target_pairs={{0,6},{1,7},{2,4},{3,5},{4,2},{5,3},{6,0},{7,1},{8,14},{9,15},{10,... | collective-permute-start | bytes 393224 | tf_op jit(solution)/shard_map/ppermute | solution.py:228
  28.4 12.8 %collective-permute-start.12 = (bf16[4,16,1024]{2,1,0:T(8,128)(2,1)S(1)}, bf16[4,16,1024]{2,1,0:T(8,128)(2,1)S(1)}, u32[]{:S(2)}, u32[]{:S(2)}) collective-permute-start(bf16[4,16,1024]{2,1,0:T(8,128)(2,1)S(1)} %get-tuple-element.13), channel_id=1, source_target_pairs={{0,7},{1,6},{2,5},{3,4},{4,3},{5,2},{6,1},{7,0},{8,15},{9,14},{10,... | collective-permute-start | bytes 393224 | tf_op jit(solution)/shard_map/ppermute | solution.py:228

commit v9 on v7

--- a/solution.py
+++ b/solution.py
@@ -19,6 +19,10 @@
 BF16 = jnp.bfloat16
 NT = (((1,), (1,)), ((), ()))
 TN = (((0,), (0,)), ((), ()))
+
+
+def start_order(dp, lo):
+    return sorted(range(dp - 1, 0, -1), key=lambda k: (k < lo, k % 2 if k >= lo else 0))
 
 
 def split_kernel(mine_ref, val_hbm, *refs):
@@ -244,7 +248,7 @@
         compiler_params=pltpu.CompilerParams(vmem_limit_bytes=VL_A),
     )(mine, val_features)
     val_all = [pieces[0]] * dp
-    for k in range(dp - 1, 0, -1):
+    for k in start_order(dp, lo):
         val_all[k] = lax.ppermute(
             pieces[k % lo], ("hi", "lo"), [(a, a ^ k) for a in range(dp)]
         )
@@ -286,7 +290,7 @@
         scratch_shapes=[
             pltpu.VMEM((exp_local, rows, hidden), BF16),
             pltpu.VMEM((exp_local, rank, hidden), BF16),
-            pltpu.SemaphoreType.DMA((4, 2)),
+            pltpu.SemaphoreType.DMA((2, 2)),
         ],
         compiler_params=pltpu.CompilerParams(vmem_limit_bytes=VL_L),
         cost_estimate=pl.CostEstimate(
@@ -312,9 +316,9 @@
             flops=8 * exp_local * rows * rank * tok, bytes_accessed=1 << 20, transcendentals=0
         ),
     )(me, mine, *pays, low)
-    arrived = [feats[0]]
-    for k in range(1, lo):
-        arrived.append(lax.ppermute(feats[k], "lo", [(a, a ^ k) for a in range(lo)]))
+    arrived = [feats[0]] * lo
+    for k in range(lo - 1, 0, -1):
+        arrived[k] = lax.ppermute(feats[k], "lo", [(a, a ^ k) for a in range(lo)])
 
     scale = 1.0 / float(experts * entries) ** 0.5
     part = pl.pallas_call(

time: 49.7 us -> 50.1 us (level)
  transfers between devices with their start and end apart: 13 -> 13, of which waited for: 6 -> 6; matrix products, arithmetic and copies ran while one was open for 0% -> 0% of each run, Pallas kernels for 17% -> 18%
where the time goes in v9:
time: 50.1 us; the launch traced here: 49.9 us
  starting transfers between devices  17.7 us (35%)
  waiting for transfers between devices  11.5 us (23%)
  Pallas kernels  11.2 us (22%)
  blocking collectives  8.66 us (17%)
  other arithmetic  0.59 us (1%)
    ppermute x7, starting transfers between devices, layer(): lax.ppermute(pieces[k % lo], ('hi', 'lo'), [(a, a ^ k) for a in range(dp)])  12.2 us
    all_to_all x1, blocking collectives, layer(): lax.all_to_all(part, ('expert', 'lo'), split_axis=0, concat_axis=0, tiled...  8.66 us
    ppermute x7, waiting for transfers between devices, layer(): lax.ppermute(pieces[k % lo], ('hi', 'lo'), [(a, a ^ k) for a in range(dp)])  8.55 us
    pallas_call x1, Pallas kernels, layer(): pl.pallas_call(lowered_kernel, out_shape=jax.ShapeDtypeStruct((exp_local,...  4.84 us
    ppermute x3, starting transfers between devices, layer(): arrived[k] = lax.ppermute(feats[k], 'lo', [(a, a ^ k) for a in range(lo)])  3.55 us
    ppermute x3, waiting for transfers between devices, layer(): arrived[k] = lax.ppermute(feats[k], 'lo', [(a, a ^ k) for a in range(lo)])  2.96 us
    pallas_call x1, Pallas kernels, layer(): pl.pallas_call(act_kernel, out_shape=jax.ShapeDtypeStruct((pay_rows, tok)...  2.57 us
    ppermute x3, starting transfers between devices, layer(): lax.ppermute(pay, 'expert', [(a, a ^ k) for a in range(groups)])  1.92 us
  transfers between devices with their start and end apart: 13, of which 6 were waited for; matrix products, arithmetic and copies ran while one was open for 0% of the time, Pallas kernels for 18%

profile of v9, /device:TPU:0, one launch (start us, length us, event | category | flops | bytes accessed | tf_op | source)
XLA Modules:
  0.0 49.9 jit_solution(545264919778981366)
XLA Ops:
  0.0 1.8 %shard_map.85 = (bf16[4,16,1024]{2,1,0:T(8,128)(2,1)}, bf16[4,16,1024]{2,1,0:T(8,128)(2,1)}, bf16[4,16,1024]{2,1,0:T(8,128)(2,1)}, bf16[4,16,1024]{2,1,0:T(8,128)(2,1)}) custom-call(s32[1]{0:T(128)} %bitcast.2.mine_ref, bf16[4,16,4096]{2,1,0:T(8,128)(2,1)} %val_hbm.1), custom_call_target="tpu_custom_call" | custom-call | tf_op jit(solution)/shard_map/pallas_call | solution.py:239
  1.8 0.0 copy-start.4
  1.8 0.0 copy-start.3
  1.8 0.0 copy-start.2
  1.8 0.0 copy-start.1
  1.9 5.1 %collective-permute-start.10 = (bf16[4,16,1024]{2,1,0:T(8,128)(2,1)}, bf16[4,16,1024]{2,1,0:T(8,128)(2,1)S(1)}, u32[]{:S(2)}, u32[]{:S(2)}) collective-permute-start(bf16[4,16,1024]{2,1,0:T(8,128)(2,1)} %get-tuple-element.18), channel_id=1, source_target_pairs={{0,5},{1,4},{2,7},{3,6},{4,1},{5,0},{6,3},{7,2},{8,13},{9,12},{10,... | collective-permute-start | bytes 393224 | tf_op jit(solution)/shard_map/ppermute | solution.py:252
  6.9 1.3 %collective-permute-start.11 = (bf16[4,16,1024]{2,1,0:T(8,128)(2,1)}, bf16[4,16,1024]{2,1,0:T(8,128)(2,1)S(1)}, u32[]{:S(2)}, u32[]{:S(2)}) collective-permute-start(bf16[4,16,1024]{2,1,0:T(8,128)(2,1)} %get-tuple-element.19), channel_id=1, source_target_pairs={{0,6},{1,7},{2,4},{3,5},{4,2},{5,3},{6,0},{7,1},{8,14},{9,15},{10,... | collective-permute-start | bytes 393224 | tf_op jit(solution)/shard_map/ppermute | solution.py:252
  8.3 2.6 %shard_map.82.refs_0_ = f32[88,128]{1,0:T(8,128)} custom-call(bf16[128,4096]{1,0:T(8,128)(2,1)} %tok_hbm.1, bf16[64,4096]{1,0:T(8,128)(2,1)} %bitcast.9, s32[8,128]{1,0:T(8,128)} %bitcast.10, f32[8,128]{1,0:T(8,128)} %bitcast.11, s32[1,128]{1,0:T(1,128)} %bitcast.12), custom_call_target="tpu_custom_call" | custom-call | flops 67108864 | bytes 1572864 | tf_op jit(solution)/shard_map/pallas_call | solution.py:258
  10.8 0.0 copy-start
  10.8 0.1 collective-permute-start
  10.9 1.6 %collective-permute-start.1 = (f32[88,128]{1,0:T(8,128)}, f32[88,128]{1,0:T(8,128)S(1)}, u32[]{:S(2)}, u32[]{:S(2)}) collective-permute-start(f32[88,128]{1,0:T(8,128)} %shard_map.82.refs_0_), channel_id=1, source_target_pairs={{0,16},{8,24},{16,0},{24,8},{1,17},{9,25},{17,1},{25,9},{2,18},{10... | collective-permute-start | bytes 135176 | tf_op jit(solution)/shard_map/ppermute | solution.py:283
  12.5 0.3 collective-permute-start.2
  12.8 4.8 %shard_map.83.refs_4_ = bf16[16,128,128]{2,1,0:T(8,128)(2,1)S(1)} custom-call(bf16[16,128,1536]{2,1,0:T(8,128)(2,1)} %grad_hbm.1, bf16[16,64,1536]{2,1,0:T(8,128)(2,1)} %bitcast.8), custom_call_target="tpu_custom_call" | custom-call | flops 402653184 | bytes 9437184 | tf_op jit(solution)/shard_map/pallas_call | solution.py:285
  17.6 0.0 collective-permute-done.refs_1_
  17.6 0.0 collective-permute-done.1.refs_2_
  17.6 0.0 collective-permute-done.2.refs_3_
  17.7 0.0 copy-done
  17.7 1.4 %shard_map.84 = (bf16[2,8,16,128]{3,2,1,0:T(8,128)(2,1)S(1)}, bf16[2,8,16,128]{3,2,1,0:T(8,128)(2,1)S(1)}, bf16[2,8,16,128]{3,2,1,0:T(8,128)(2,1)S(1)}, bf16[2,8,16,128]{3,2,1,0:T(8,128)(2,1)S(1)}) custom-call(s32[1]{0:T(128)} %bitcast.1.me_ref, s32[1]{0:T(128)} %bitcast.2.mine_ref, f32[88,128]{1,0:T(8,128)S(1)} %copy-done, ...), custom_call_target="tpu_custom_call" | custom-call | flops 134217728 | bytes 1048576 | tf_op jit(solution)/shard_map/pallas_call | solution.py:305
  19.0 0.6 %collective-permute-start.3 = (bf16[2,8,16,128]{3,2,1,0:T(8,128)(2,1)S(1)}, bf16[2,8,16,128]{3,2,1,0:T(8,128)(2,1)S(1)}, u32[]{:S(2)}, u32[]{:S(2)}) collective-permute-start(bf16[2,8,16,128]{3,2,1,0:T(8,128)(2,1)S(1)} %get-tuple-element.14), channel_id=1, source_target_pairs={{0,1},{1,0},{2,3},{3,2},{4,5},{5,4},{6,7},{7,6},{8,9},{9,8},{10,11... | collective-permute-start | bytes 196616 | tf_op jit(solution)/shard_map/ppermute | solution.py:321
  19.6 0.2 collective-permute-start.4
  19.9 2.7 %collective-permute-start.5 = (bf16[2,8,16,128]{3,2,1,0:T(8,128)(2,1)S(1)}, bf16[2,8,16,128]{3,2,1,0:T(8,128)(2,1)S(1)}, u32[]{:S(2)}, u32[]{:S(2)}) collective-permute-start(bf16[2,8,16,128]{3,2,1,0:T(8,128)(2,1)S(1)} %get-tuple-element.16), channel_id=1, source_target_pairs={{0,3},{1,2},{2,1},{3,0},{4,7},{5,6},{6,5},{7,4},{8,11},{9,10},{10,... | collective-permute-start | bytes 196616 | tf_op jit(solution)/shard_map/ppermute | solution.py:321
  22.6 0.9 %collective-permute-done.3.refs_1_ = bf16[2,8,16,128]{3,2,1,0:T(8,128)(2,1)S(1)} collective-permute-done((bf16[2,8,16,128]{3,2,1,0:T(8,128)(2,1)S(1)}, bf16[2,8,16,128]{3,2,1,0:T(8,128)(2,1)S(1)}, u32[]{:S(2)}, u32[]{:S(2)}) %collective-permute-start.3) | collective-permute-done | bytes 65568 | tf_op jit(solution)/shard_map/ppermute | solution.py:321
  23.5 0.0 copy-done.4
  23.5 0.5 %collective-permute-start.6 = (bf16[4,16,1024]{2,1,0:T(8,128)(2,1)S(1)}, bf16[4,16,1024]{2,1,0:T(8,128)(2,1)S(1)}, u32[]{:S(2)}, u32[]{:S(2)}) collective-permute-start(bf16[4,16,1024]{2,1,0:T(8,128)(2,1)S(1)} %copy-done.4), channel_id=1, source_target_pairs={{0,1},{1,0},{2,3},{3,2},{4,5},{5,4},{6,7},{7,6},{8,9},{9,8},{10,11... | collective-permute-start | bytes 393224 | tf_op jit(solution)/shard_map/ppermute | solution.py:252
  24.0 0.6 %collective-permute-done.4.refs_2_ = bf16[2,8,16,128]{3,2,1,0:T(8,128)(2,1)S(1)} collective-permute-done((bf16[2,8,16,128]{3,2,1,0:T(8,128)(2,1)S(1)}, bf16[2,8,16,128]{3,2,1,0:T(8,128)(2,1)S(1)}, u32[]{:S(2)}, u32[]{:S(2)}) %collective-permute-start.4) | collective-permute-done | bytes 65568 | tf_op jit(solution)/shard_map/ppermute | solution.py:321
  24.6 0.0 copy-done.3
  24.6 0.0 collective-permute-start.7
  24.6 1.5 %collective-permute-done.5.refs_3_ = bf16[2,8,16,128]{3,2,1,0:T(8,128)(2,1)S(1)} collective-permute-done((bf16[2,8,16,128]{3,2,1,0:T(8,128)(2,1)S(1)}, bf16[2,8,16,128]{3,2,1,0:T(8,128)(2,1)S(1)}, u32[]{:S(2)}, u32[]{:S(2)}) %collective-permute-start.5) | collective-permute-done | bytes 65568 | tf_op jit(solution)/shard_map/ppermute | solution.py:321
  26.1 0.0 copy-done.2
  26.1 2.9 %collective-permute-start.12 = (bf16[4,16,1024]{2,1,0:T(8,128)(2,1)S(1)}, bf16[4,16,1024]{2,1,0:T(8,128)(2,1)S(1)}, u32[]{:S(2)}, u32[]{:S(2)}) collective-permute-start(bf16[4,16,1024]{2,1,0:T(8,128)(2,1)S(1)} %copy-done.2), channel_id=1, source_target_pairs={{0,7},{1,6},{2,5},{3,4},{4,3},{5,2},{6,1},{7,0},{8,15},{9,14},{10,... | collective-permute-start | bytes 393224 | tf_op jit(solution)/shard_map/ppermute | solution.py:252
  29.0 0.0 collective-permute-done.10.refs_9_
  29.0 0.5 collective-permute-start.8
  29.5 0.0 collective-permute-done.11.refs_10_
  29.5 0.0 copy-done.1
  29.5 1.9 %collective-permute-start.9 = (bf16[4,16,1024]{2,1,0:T(8,128)(2,1)S(1)}, bf16[4,16,1024]{2,1,0:T(8,128)(2,1)S(1)}, u32[]{:S(2)}, u32[]{:S(2)}) collective-permute-start(bf16[4,16,1024]{2,1,0:T(8,128)(2,1)S(1)} %copy-done.1), channel_id=1, source_target_pairs={{0,4},{1,5},{2,6},{3,7},{4,0},{5,1},{6,2},{7,3},{8,12},{9,13},{10,... | collective-permute-start | bytes 393224 | tf_op jit(solution)/shard_map/ppermute | solution.py:252
  31.4 4.1 %collective-permute-done.12.refs_11_ = bf16[4,16,1024]{2,1,0:T(8,128)(2,1)S(1)} collective-permute-done((bf16[4,16,1024]{2,1,0:T(8,128)(2,1)S(1)}, bf16[4,16,1024]{2,1,0:T(8,128)(2,1)S(1)}, u32[]{:S(2)}, u32[]{:S(2)}) %collective-permute-start.12) | collective-permute-done | bytes 131104 | tf_op jit(solution)/shard_map/ppermute | solution.py:252
  35.5 0.0 collective-permute-done.6.refs_5_
  35.5 0.0 collective-permute-done.7.refs_6_
  35.5 3.1 %collective-permute-done.8.refs_7_ = bf16[4,16,1024]{2,1,0:T(8,128)(2,1)S(1)} collective-permute-done((bf16[4,16,1024]{2,1,0:T(8,128)(2,1)S(1)}, bf16[4,16,1024]{2,1,0:T(8,128)(2,1)S(1)}, u32[]{:S(2)}, u32[]{:S(2)}) %collective-permute-start.8) | collective-permute-done | bytes 131104 | tf_op jit(solution)/shard_map/ppermute | solution.py:252
  38.6 1.3 %collective-permute-done.9.refs_8_ = bf16[4,16,1024]{2,1,0:T(8,128)(2,1)S(1)} collective-permute-done((bf16[4,16,1024]{2,1,0:T(8,128)(2,1)S(1)}, bf16[4,16,1024]{2,1,0:T(8,128)(2,1)S(1)}, u32[]{:S(2)}, u32[]{:S(2)}) %collective-permute-start.9) | collective-permute-done | bytes 131104 | tf_op jit(solution)/shard_map/ppermute | solution.py:252
  39.9 0.7 %shard_map.86 = f32[16,2,32]{2,1,0:T(2,128)S(1)} custom-call(s32[1]{0:T(128)} %bitcast.mine_ref, bf16[2,8,16,128]{3,2,1,0:T(8,128)(2,1)S(1)} %get-tuple-element.13.refs_0_, bf16[2,8,16,128]{3,2,1,0:T(8,128)(2,1)S(1)} %collective-permute-done.3.refs_1_, bf16[2,8,16,128]{3,2,1,0:T(8,128)(2,1)S(1)} %collective-permute-done.4.refs_2_, ...), custom_call_target="tpu_custom_call" | custom-call | tf_op jit(solution)/shard_map/pallas_call | solution.py:324
  40.6 8.7 %all_to_all.5 = f32[16,2,32]{2,1,0:T(2,128)S(1)} all-to-all(f32[16,2,32]{2,1,0:T(2,128)S(1)} %shard_map.86), channel_id=1, replica_groups=mesh['expert'=4,'hi'=2,'lo'=4] {'expert','lo'}, dimensions={0} | all-to-all | bytes 8192 | tf_op jit(solution)/shard_map/all_to_all | solution.py:331
  49.3 0.6 %reduce_sum.9 = f32[2,32]{1,0:T(2,128)} reduce(f32[16,2,32]{2,1,0:T(2,128)S(1)} %all_to_all.5, f32[]{:T(128)} %constant.15.clone.1), dimensions={0}, to_apply=%region_0.0 | reduce | flops 960 | bytes 4356 | tf_op jit(solution)/shard_map/reduce_sum | solution.py:332
Async XLA Ops:
  1.8 21.6 %copy-start.4 = (bf16[4,16,1024]{2,1,0:T(8,128)(2,1)S(1)}, bf16[4,16,1024]{2,1,0:T(8,128)(2,1)}, u32[]{:S(2)}) copy-start(bf16[4,16,1024]{2,1,0:T(8,128)(2,1)} %get-tuple-element.18) | copy-start | bytes 393220
  1.8 22.7 %copy-start.3 = (bf16[4,16,1024]{2,1,0:T(8,128)(2,1)S(1)}, bf16[4,16,1024]{2,1,0:T(8,128)(2,1)}, u32[]{:S(2)}) copy-start(bf16[4,16,1024]{2,1,0:T(8,128)(2,1)} %get-tuple-element.19) | copy-start | bytes 393220
  1.8 24.3 %copy-start.2 = (bf16[4,16,1024]{2,1,0:T(8,128)(2,1)S(1)}, bf16[4,16,1024]{2,1,0:T(8,128)(2,1)}, u32[]{:S(2)}) copy-start(bf16[4,16,1024]{2,1,0:T(8,128)(2,1)} %get-tuple-element.20) | copy-start | bytes 393220
  1.8 27.6 %copy-start.1 = (bf16[4,16,1024]{2,1,0:T(8,128)(2,1)S(1)}, bf16[4,16,1024]{2,1,0:T(8,128)(2,1)}, u32[]{:S(2)}) copy-start(bf16[4,16,1024]{2,1,0:T(8,128)(2,1)} %get-tuple-element.17.refs_4_) | copy-start | bytes 393220
  1.9 27.1 %collective-permute-start.10 = (bf16[4,16,1024]{2,1,0:T(8,128)(2,1)}, bf16[4,16,1024]{2,1,0:T(8,128)(2,1)S(1)}, u32[]{:S(2)}, u32[]{:S(2)}) collective-permute-start(bf16[4,16,1024]{2,1,0:T(8,128)(2,1)} %get-tuple-element.18), channel_id=1, source_target_pairs={{0,5},{1,4},{2,7},{3,6},{4,1},{5,0},{6,3},{7,2},{8,13},{9,12},{10,... | collective-permute-start | bytes 393224 | tf_op jit(solution)/shard_map/ppermute | solution.py:252
  6.9 22.6 %collective-permute-start.11 = (bf16[4,16,1024]{2,1,0:T(8,128)(2,1)}, bf16[4,16,1024]{2,1,0:T(8,128)(2,1)S(1)}, u32[]{:S(2)}, u32[]{:S(2)}) collective-permute-start(bf16[4,16,1024]{2,1,0:T(8,128)(2,1)} %get-tuple-element.19), channel_id=1, source_target_pairs={{0,6},{1,7},{2,4},{3,5},{4,2},{5,3},{6,0},{7,1},{8,14},{9,15},{10,... | collective-permute-start | bytes 393224 | tf_op jit(solution)/shard_map/ppermute | solution.py:252
  10.8 6.8 %copy-start = (f32[88,128]{1,0:T(8,128)S(1)}, f32[88,128]{1,0:T(8,128)}, u32[]{:S(2)}) copy-start(f32[88,128]{1,0:T(8,128)} %shard_map.82.refs_0_) | copy-start | bytes 135172
  10.8 6.8 %collective-permute-start = (f32[88,128]{1,0:T(8,128)}, f32[88,128]{1,0:T(8,128)S(1)}, u32[]{:S(2)}, u32[]{:S(2)}) collective-permute-start(f32[88,128]{1,0:T(8,128)} %shard_map.82.refs_0_), channel_id=1, source_target_pairs={{0,8},{8,0},{16,24},{24,16},{1,9},{9,1},{17,25},{25,17},{2,10},{10... | collective-permute-start | bytes 135176 | tf_op jit(solution)/shard_map/ppermute | solution.py:283
  10.9 6.7 %collective-permute-start.1 = (f32[88,128]{1,0:T(8,128)}, f32[88,128]{1,0:T(8,128)S(1)}, u32[]{:S(2)}, u32[]{:S(2)}) collective-permute-start(f32[88,128]{1,0:T(8,128)} %shard_map.82.refs_0_), channel_id=1, source_target_pairs={{0,16},{8,24},{16,0},{24,8},{1,17},{9,25},{17,1},{25,9},{2,18},{10... | collective-permute-start | bytes 135176 | tf_op jit(solution)/shard_map/ppermute | solution.py:283
  12.5 5.1 %collective-permute-start.2 = (f32[88,128]{1,0:T(8,128)}, f32[88,128]{1,0:T(8,128)S(1)}, u32[]{:S(2)}, u32[]{:S(2)}) collective-permute-start(f32[88,128]{1,0:T(8,128)} %shard_map.82.refs_0_), channel_id=1, source_target_pairs={{0,24},{8,16},{16,8},{24,0},{1,25},{9,17},{17,9},{25,1},{2,26},{10... | collective-permute-start | bytes 135176 | tf_op jit(solution)/shard_map/ppermute | solution.py:283
  19.0 4.4 %collective-permute-start.3 = (bf16[2,8,16,128]{3,2,1,0:T(8,128)(2,1)S(1)}, bf16[2,8,16,128]{3,2,1,0:T(8,128)(2,1)S(1)}, u32[]{:S(2)}, u32[]{:S(2)}) collective-permute-start(bf16[2,8,16,128]{3,2,1,0:T(8,128)(2,1)S(1)} %get-tuple-element.14), channel_id=1, source_target_pairs={{0,1},{1,0},{2,3},{3,2},{4,5},{5,4},{6,7},{7,6},{8,9},{9,8},{10,11... | collective-permute-start | bytes 196616 | tf_op jit(solution)/shard_map/ppermute | solution.py:321
  19.6 4.9 %collective-permute-start.4 = (bf16[2,8,16,128]{3,2,1,0:T(8,128)(2,1)S(1)}, bf16[2,8,16,128]{3,2,1,0:T(8,128)(2,1)S(1)}, u32[]{:S(2)}, u32[]{:S(2)}) collective-permute-start(bf16[2,8,16,128]{3,2,1,0:T(8,128)(2,1)S(1)} %get-tuple-element.15), channel_id=1, source_target_pairs={{0,2},{1,3},{2,0},{3,1},{4,6},{5,7},{6,4},{7,5},{8,10},{9,11},{10,... | collective-permute-start | bytes 196616 | tf_op jit(solution)/shard_map/ppermute | solution.py:321
  19.9 6.2 %collective-permute-start.5 = (bf16[2,8,16,128]{3,2,1,0:T(8,128)(2,1)S(1)}, bf16[2,8,16,128]{3,2,1,0:T(8,128)(2,1)S(1)}, u32[]{:S(2)}, u32[]{:S(2)}) collective-permute-start(bf16[2,8,16,128]{3,2,1,0:T(8,128)(2,1)S(1)} %get-tuple-element.16), channel_id=1, source_target_pairs={{0,3},{1,2},{2,1},{3,0},{4,7},{5,6},{6,5},{7,4},{8,11},{9,10},{10,... | collective-permute-start | bytes 196616 | tf_op jit(solution)/shard_map/ppermute | solution.py:321
  23.5 12.0 %collective-permute-start.6 = (bf16[4,16,1024]{2,1,0:T(8,128)(2,1)S(1)}, bf16[4,16,1024]{2,1,0:T(8,128)(2,1)S(1)}, u32[]{:S(2)}, u32[]{:S(2)}) collective-permute-start(bf16[4,16,1024]{2,1,0:T(8,128)(2,1)S(1)} %copy-done.4), channel_id=1, source_target_pairs={{0,1},{1,0},{2,3},{3,2},{4,5},{5,4},{6,7},{7,6},{8,9},{9,8},{10,11... | collective-permute-start | bytes 393224 | tf_op jit(solution)/shard_map/ppermute | solution.py:252
  24.6 10.9 %collective-permute-start.7 = (bf16[4,16,1024]{2,1,0:T(8,128)(2,1)S(1)}, bf16[4,16,1024]{2,1,0:T(8,128)(2,1)S(1)}, u32[]{:S(2)}, u32[]{:S(2)}) collective-permute-start(bf16[4,16,1024]{2,1,0:T(8,128)(2,1)S(1)} %copy-done.3), channel_id=1, source_target_pairs={{0,2},{1,3},{2,0},{3,1},{4,6},{5,7},{6,4},{7,5},{8,10},{9,11},{10,... | collective-permute-start | bytes 393224 | tf_op jit(solution)/shard_map/ppermute | solution.py:252
  26.1 9.4 %collective-permute-start.12 = (bf16[4,16,1024]{2,1,0:T(8,128)(2,1)S(1)}, bf16[4,16,1024]{2,1,0:T(8,128)(2,1)S(1)}, u32[]{:S(2)}, u32[]{:S(2)}) collective-permute-start(bf16[4,16,1024]{2,1,0:T(8,128)(2,1)S(1)} %copy-done.2), channel_id=1, source_target_pairs={{0,7},{1,6},{2,5},{3,4},{4,3},{5,2},{6,1},{7,0},{8,15},{9,14},{10,... | collective-permute-start | bytes 393224 | tf_op jit(solution)/shard_map/ppermute | solution.py:252
  29.0 9.6 %collective-permute-start.8 = (bf16[4,16,1024]{2,1,0:T(8,128)(2,1)S(1)}, bf16[4,16,1024]{2,1,0:T(8,128)(2,1)S(1)}, u32[]{:S(2)}, u32[]{:S(2)}) collective-permute-start(bf16[4,16,1024]{2,1,0:T(8,128)(2,1)S(1)} %copy-done.2), channel_id=1, source_target_pairs={{0,3},{1,2},{2,1},{3,0},{4,7},{5,6},{6,5},{7,4},{8,11},{9,10},{10,... | collective-permute-start | bytes 393224 | tf_op jit(solution)/shard_map/ppermute | solution.py:252
  29.5 10.5 %collective-permute-start.9 = (bf16[4,16,1024]{2,1,0:T(8,128)(2,1)S(1)}, bf16[4,16,1024]{2,1,0:T(8,128)(2,1)S(1)}, u32[]{:S(2)}, u32[]{:S(2)}) collective-permute-start(bf16[4,16,1024]{2,1,0:T(8,128)(2,1)S(1)} %copy-done.1), channel_id=1, source_target_pairs={{0,4},{1,5},{2,6},{3,7},{4,0},{5,1},{6,2},{7,3},{8,12},{9,13},{10,... | collective-permute-start | bytes 393224 | tf_op jit(solution)/shard_map/ppermute | solution.py:252
